TPU v7x, 32 devices: a whole 2x2x4 slice. The times are simulated.
32 devices in a mesh: fsdp: 32 (over z, y, x, core).
Axes of the slice: x: 2, y: 2, z: 4, core: 2. Of those that a mesh axis runs over, the one named last changes fastest.
Arguments:
- tokens: bfloat16 [2, 8192, 1024], P(None, 'fsdp'), may hold values from -6 to 6
- condition: bfloat16 [2, 8192], P(None, 'fsdp'), may hold values from -6 to 6
- attend: bfloat16 [3145728], P('fsdp'), may hold values from -0.1875 to 0.1875
- project: bfloat16 [1048576], P('fsdp'), may hold values from -0.25 to 0.25
- expand: bfloat16 [4194304], P('fsdp'), may hold values from -0.1875 to 0.1875
- contract: bfloat16 [4194304], P('fsdp'), may hold values from -0.1875 to 0.1875
- modulate: bfloat16 [6291456], P('fsdp'), may hold values from -0.1875 to 0.1875
- biases: bfloat16 [14336], P('fsdp'), may hold values from -2 to 2
- cotangent: bfloat16 [2, 8192, 1024], P(None, 'fsdp'), may hold values from -6 to 6
Outputs:
- output: bfloat16 [2, 8192, 1024], P(None, 'fsdp')
- grad_tokens: float32 [2, 8192, 1024], P(None, 'fsdp')
- grad_condition: float32 [2, 8192], P(None, 'fsdp')
- grad_attend: float32 [3145728], P('fsdp')
- grad_project: float32 [1048576], P('fsdp')
- expand_gradient: float32 [4194304], P('fsdp')
- grad_contract: float32 [4194304], P('fsdp')
- grad_modulate: float32 [6291456], P('fsdp')
- grad_biases: float32 [14336], P('fsdp')
All inputs are finite; a program needn't handle non-finite values.
Results may differ from a plain program's by a relative error of at most 0.011.
Values may be sent and summed in bfloat16 or wider, within the bound.
A program may use at most 384 MiB of HBM per device.

v0:
```python
import jax
import jax.numpy as jnp
from jax import lax
from jax.sharding import PartitionSpec as P

D = 1024
HEADS = 16
HEAD = 64
FF = 4096
SPLIT = 4


epsilon = 1e-06
highest = lax.Precision.HIGHEST


def swapped(value, axis, distance):
    mask = 2**distance
    pairs = [(source, source ^ mask) for source in range(lax.axis_size(axis))]
    return lax.ppermute(value, axis, pairs)


def normalize(values):
    center = values - jnp.mean(values, axis=-1, keepdims=True)
    spread = jnp.mean(center * center, axis=-1, keepdims=True)
    return center * lax.rsqrt(spread + epsilon)


def modulated(values, offsets, factors):
    return normalize(values) * (1.0 + factors[:, None, :]) + offsets[:, None, :]


def gelu_tanh(values):
    return jax.nn.gelu(values, approximate=True)


def unpack(flat_weights):
    return (
        flat_weights[0].reshape(D, 3 * D),
        flat_weights[1].reshape(D, D),
        flat_weights[2].reshape(D, FF),
        flat_weights[3].reshape(FF, D),
        flat_weights[4].reshape(D, 6 * D),
    )


def gather_group(pieces, position, sections):
    current = pieces
    for section_bit in range(sections):
        partner = swapped(current, "fsdp", section_bit)
        is_upper = position >> section_bit & 1 == 1
        current = jnp.where(
            is_upper,
            jnp.concatenate([partner, current], axis=1),
            jnp.concatenate([current, partner], axis=1),
        )
    return current


def reduce_group(partial_sums, position, sections):
    current = partial_sums
    for section_bit in reversed(range(sections)):
        half_rows = current.shape[1] // 2
        lower_half = current[:, :half_rows]
        upper_half = current[:, half_rows:]
        is_upper = position >> section_bit & 1 == 1
        kept = jnp.where(is_upper, upper_half, lower_half)
        sent = jnp.where(is_upper, lower_half, upper_half)
        current = kept + swapped(sent, "fsdp", section_bit)
    return current


def attend_block(query_part, key_part, value_part, factor):
    scores = (
        jnp.einsum("mrhe,mlhe->mhrl", query_part, key_part, preferred_element_type=jnp.float32)
        * factor
    )
    top_score = jnp.max(scores, axis=-1, keepdims=True)
    weights = jnp.exp(scores - top_score)
    totals = jnp.sum(weights, axis=-1, keepdims=True)
    chances_low = (weights / totals).astype(jnp.bfloat16)
    blended = jnp.einsum(
        "mhrl,mlhe->mrhe", chances_low, value_part, preferred_element_type=jnp.float32
    )
    return (blended, top_score + jnp.log(totals))


def attend_back(query_part, key_part, value_part, logsum, grad_part, factor):
    scores = (
        jnp.einsum("mrhe,mlhe->mhrl", query_part, key_part, preferred_element_type=jnp.float32)
        * factor
    )
    chances = jnp.exp(scores - logsum)
    grad_chances = jnp.einsum(
        "mrhe,mlhe->mhrl", grad_part, value_part, preferred_element_type=jnp.float32
    )
    row_terms = jnp.sum(chances * grad_chances, axis=-1, keepdims=True)
    grad_scores = (chances * (grad_chances - row_terms)).astype(jnp.bfloat16)
    grad_query = (
        jnp.einsum("mhrl,mlhe->mrhe", grad_scores, key_part, preferred_element_type=jnp.float32)
        * factor
    )
    grad_key = (
        jnp.einsum("mhrl,mrhe->mlhe", grad_scores, query_part, preferred_element_type=jnp.float32)
        * factor
    )
    grad_value = jnp.einsum(
        "mhrl,mrhe->mlhe",
        chances.astype(jnp.bfloat16),
        grad_part,
        preferred_element_type=jnp.float32,
    )
    return (grad_query, grad_key, grad_value)


def per_device(tokens, condition, attend, project, expand, contract, modulate, biases, cotangent):
    position = lax.axis_index("fsdp")
    micro_count, row_count, model_width = tokens.shape
    sections = SPLIT.bit_length() - 1
    gathered = (
        lax.all_gather(attend, "fsdp", axis=0, tiled=True),
        lax.all_gather(project, "fsdp", axis=0, tiled=True),
        lax.all_gather(expand, "fsdp", axis=0, tiled=True),
        lax.all_gather(contract, "fsdp", axis=0, tiled=True),
        lax.all_gather(modulate, "fsdp", axis=0, tiled=True),
        lax.all_gather(biases, "fsdp", axis=0, tiled=True),
        lax.all_gather(condition, "fsdp", axis=1, tiled=True),
    )
    attend_full, project_full, expand_weight_complete, contract_weight_complete, modulate_full = (
        unpack(gathered[:5])
    )
    bias_all = gathered[5].astype(jnp.float32)
    bias_query = bias_all[0:D]
    bias_value = bias_all[D : 2 * D]
    bias_project = bias_all[2 * D : 3 * D]
    bias_expand = bias_all[3 * D : 3 * D + FF]
    bias_contract = bias_all[3 * D + FF : 4 * D + FF]
    bias_modulate = bias_all[4 * D + FF :]
    cond_all = gathered[6].astype(jnp.float32).reshape(micro_count, -1, D)
    latent_own = position // SPLIT
    cond_own = lax.dynamic_index_in_dim(cond_all, latent_own, axis=1, keepdims=False)
    cond_act = jax.nn.silu(cond_own).astype(jnp.bfloat16)
    modulation = (
        jnp.dot(cond_act, modulate_full, preferred_element_type=jnp.float32) + bias_modulate
    )
    blocks = [modulation[:, part * D : (part + 1) * D] for part in range(6)]
    offsets_one, factors_one, gates_one, offsets_two, factors_two, gates_two = blocks
    inputs = tokens.astype(jnp.float32)
    first_low = modulated(inputs, offsets_one, factors_one).astype(jnp.bfloat16)
    bias_row = jnp.concatenate([bias_query, jnp.zeros((D,), jnp.float32), bias_value])
    projected = (
        jnp.einsum("mrd,de->mre", first_low, attend_full, preferred_element_type=jnp.float32)
        + bias_row
    ).astype(jnp.bfloat16)
    queries = projected[..., :D].reshape(micro_count, row_count, HEADS, HEAD)
    key_values = gather_group(projected[..., D:], position, sections)
    latent_rows = key_values.shape[1]
    key_rows = key_values[..., :D].reshape(micro_count, latent_rows, HEADS, HEAD)
    value_rows = key_values[..., D:].reshape(micro_count, latent_rows, HEADS, HEAD)
    factor = HEAD ** (-0.5)
    group_heads = 4
    blended_parts = []
    logsums = []
    for group_start in range(0, HEADS, group_heads):
        chosen_heads = slice(group_start, group_start + group_heads)
        blended, logsum = attend_block(
            queries[:, :, chosen_heads],
            key_rows[:, :, chosen_heads],
            value_rows[:, :, chosen_heads],
            factor,
        )
        blended_parts.append(blended)
        logsums.append(logsum)
    blended_all = (
        jnp.concatenate(blended_parts, axis=2)
        .reshape(micro_count, row_count, D)
        .astype(jnp.bfloat16)
    )
    attended = (
        jnp.einsum("mrd,de->mre", blended_all, project_full, preferred_element_type=jnp.float32)
        + bias_project
    )
    middle = inputs + gates_one[:, None, :] * attended
    second_half = modulated(middle, offsets_two, factors_two).astype(jnp.bfloat16)
    hidden = (
        jnp.einsum(
            "kqc,cn->kqn", second_half, expand_weight_complete, preferred_element_type=jnp.float32
        )
        + bias_expand
    )
    activated, gelu_pull = jax.vjp(gelu_tanh, hidden)
    activation_reduced = activated.astype(jnp.bfloat16)
    branch = (
        jnp.einsum(
            "oyg,gx->oyx",
            activation_reduced,
            contract_weight_complete,
            preferred_element_type=jnp.float32,
        )
        + bias_contract
    )
    output = (middle + gates_two[:, None, :] * branch).astype(jnp.bfloat16)
    regathered = (
        lax.all_gather(attend, "fsdp", axis=0, tiled=True),
        lax.all_gather(project, "fsdp", axis=0, tiled=True),
        lax.all_gather(expand, "fsdp", axis=0, tiled=True),
        lax.all_gather(contract, "fsdp", axis=0, tiled=True),
        lax.all_gather(modulate, "fsdp", axis=0, tiled=True),
    )
    (
        attend_back_w,
        project_back_w,
        expand_weight_backward,
        contract_weight_backward,
        modulate_back_w,
    ) = unpack(regathered)
    upstream = cotangent.astype(jnp.float32)
    branch_gradient = (gates_two[:, None, :] * upstream).astype(jnp.bfloat16)
    grad_gates_two = jnp.sum(upstream * branch, axis=1)
    grad_contract = jnp.einsum(
        "jtu,jtp->up", activation_reduced, branch_gradient, preferred_element_type=jnp.float32
    )
    grad_act = jnp.einsum(
        "bso,ao->bsa", branch_gradient, contract_weight_backward, preferred_element_type=jnp.float32
    )
    hidden_gradient = gelu_pull(grad_act)[0].astype(jnp.bfloat16)
    expand_gradient = jnp.einsum(
        "qok,qos->ks", second_half, hidden_gradient, preferred_element_type=jnp.float32
    )
    grad_second = jnp.einsum(
        "atj,xj->atx", hidden_gradient, expand_weight_backward, preferred_element_type=jnp.float32
    )
    norm_out_two, norm_pull_two = jax.vjp(modulated, middle, offsets_two, factors_two)
    grad_middle_norm, grad_offsets_two, grad_factors_two = norm_pull_two(grad_second)
    grad_middle = upstream + grad_middle_norm
    grad_attended = (gates_one[:, None, :] * grad_middle).astype(jnp.bfloat16)
    grad_gates_one = jnp.sum(grad_middle * attended, axis=1)
    grad_project = jnp.einsum(
        "mrd,mre->de", blended_all, grad_attended, preferred_element_type=jnp.float32
    )
    grad_blended = jnp.einsum(
        "mre,de->mrd", grad_attended, project_back_w, preferred_element_type=jnp.float32
    )
    grad_blended = grad_blended.astype(jnp.bfloat16).reshape(micro_count, row_count, HEADS, HEAD)
    query_grads = []
    key_grads = []
    value_grads = []
    for group_number, group_start in enumerate(range(0, HEADS, group_heads)):
        chosen_heads = slice(group_start, group_start + group_heads)
        grad_query, grad_key, grad_value = attend_back(
            queries[:, :, chosen_heads],
            key_rows[:, :, chosen_heads],
            value_rows[:, :, chosen_heads],
            logsums[group_number],
            grad_blended[:, :, chosen_heads],
            factor,
        )
        query_grads.append(grad_query)
        key_grads.append(grad_key)
        value_grads.append(grad_value)
    grad_queries = jnp.concatenate(query_grads, axis=2).reshape(micro_count, row_count, D)
    grad_keys = jnp.concatenate(key_grads, axis=2).reshape(micro_count, latent_rows, D)
    grad_values = jnp.concatenate(value_grads, axis=2).reshape(micro_count, latent_rows, D)
    grad_pairs_own = reduce_group(
        jnp.concatenate([grad_keys, grad_values], axis=-1), position, sections
    )
    grad_projected = jnp.concatenate([grad_queries, grad_pairs_own], axis=-1).astype(jnp.bfloat16)
    grad_attend = jnp.einsum(
        "mrd,mre->de", first_low, grad_projected, preferred_element_type=jnp.float32
    )
    grad_first = jnp.einsum(
        "mre,de->mrd", grad_projected, attend_back_w, preferred_element_type=jnp.float32
    )
    norm_out_one, norm_pull_one = jax.vjp(modulated, inputs, offsets_one, factors_one)
    grad_inputs_norm, grad_offsets_one, grad_factors_one = norm_pull_one(grad_first)
    grad_tokens = grad_middle + grad_inputs_norm
    grad_modulation = jnp.concatenate(
        [
            grad_offsets_one,
            grad_factors_one,
            grad_gates_one,
            grad_offsets_two,
            grad_factors_two,
            grad_gates_two,
        ],
        axis=1,
    )
    bias_terms = jnp.concatenate(
        [
            jnp.sum(grad_projected[..., :D], axis=(0, 1), dtype=jnp.float32),
            jnp.sum(grad_projected[..., 2 * D :], axis=(0, 1), dtype=jnp.float32),
            jnp.sum(grad_attended, axis=(0, 1), dtype=jnp.float32),
            jnp.sum(hidden_gradient, axis=(0, 1), dtype=jnp.float32),
            jnp.sum(branch_gradient, axis=(0, 1), dtype=jnp.float32),
            jnp.sum(grad_modulation, axis=0),
        ]
    )
    grad_modulate = jnp.einsum(
        "md,me->de", cond_act.astype(jnp.float32), grad_modulation, precision=highest
    )
    grad_silu = jnp.dot(grad_modulation, modulate_back_w.T, precision=highest)
    silu_out, silu_pull = jax.vjp(jax.nn.silu, cond_own)
    grad_cond_own = silu_pull(grad_silu)[0]
    latent_count = cond_all.shape[1]
    chosen = (jnp.arange(latent_count) == latent_own)[None, :, None]
    spread = jnp.where(chosen, grad_cond_own[:, None, :], 0.0).reshape(micro_count, -1)
    results = (
        lax.psum_scatter(grad_attend.reshape(-1), "fsdp", scatter_dimension=0, tiled=True),
        lax.psum_scatter(grad_project.reshape(-1), "fsdp", scatter_dimension=0, tiled=True),
        lax.psum_scatter(expand_gradient.reshape(-1), "fsdp", scatter_dimension=0, tiled=True),
        lax.psum_scatter(grad_contract.reshape(-1), "fsdp", scatter_dimension=0, tiled=True),
        lax.psum_scatter(grad_modulate.reshape(-1), "fsdp", scatter_dimension=0, tiled=True),
        lax.psum_scatter(bias_terms, "fsdp", scatter_dimension=0, tiled=True),
        lax.psum_scatter(spread, "fsdp", scatter_dimension=1, tiled=True),
    )
    return (
        output,
        grad_tokens,
        results[6],
        results[0],
        results[1],
        results[2],
        results[3],
        results[4],
        results[5],
    )


def solution(mesh):
    in_specs = (
        P(None, "fsdp", None),
        P(None, "fsdp"),
        P("fsdp"),
        P("fsdp"),
        P("fsdp"),
        P("fsdp"),
        P("fsdp"),
        P("fsdp"),
        P(None, "fsdp", None),
    )
    out_specs = (
        P(None, "fsdp", None),
        P(None, "fsdp", None),
        P(None, "fsdp"),
        P("fsdp"),
        P("fsdp"),
        P("fsdp"),
        P("fsdp"),
        P("fsdp"),
        P("fsdp"),
    )
    return jax.shard_map(
        per_device, mesh=mesh, in_specs=in_specs, out_specs=out_specs, check_vma=False
    )
```

profile of v0, /device:TPU:0, one launch (start us, length us, event | category | flops | bytes accessed | tf_op | source)
XLA Modules:
  0.0 2186.7 jit_solution(12810311496066575732)
XLA Ops:
  11.5 42.6 %all-reduce = bf16[14336]{0:T(1024)(128)(2,1)S(1)} all-reduce(bf16[14336]{0:T(1024)(128)(2,1)S(1)} %dynamic-update-slice), channel_id=1, replica_groups=mesh['fsdp'=32] {'fsdp'}, use_global_device_ids=true, to_apply=%add | all-reduce | flops 14336 | bytes 57344
  54.2 41.0 %all_gather.26 = bf16[2,8192]{1,0:T(2,128)(2,1)S(1)} all-gather(bf16[2,256]{1,0:T(2,128)(2,1)} %param.10), channel_id=1, replica_groups=mesh['fsdp'=32] {'fsdp'}, dimensions={1}, use_global_device_ids=true | all-gather | bytes 33792 | tf_op jit(solution)/shard_map/all_gather | solution.py:127
  98.9 10.3 reshape.239
  109.3 71.5 %all-gather.6.cloned.1.call-done = bf16[6291456]{0:T(1024)(128)(2,1)} async-done(((bf16[196608]{0:T(1024)(128)(2,1)}), bf16[6291456]{0:T(1024)(128)(2,1)}) %all-gather.6.cloned.1.call-update) | async-done | bytes 12582928 | tf_op jit(solution)/shard_map/all_gather | solution.py:125
  180.8 18.4 reshape.218
  223.2 17.8 all-gather.10.cloned.1.call-done
  245.2 99.4 %all-gather.12.cloned.1.call-done = bf16[4194304]{0:T(1024)(128)(2,1)} async-done(((bf16[131072]{0:T(1024)(128)(2,1)}), bf16[4194304]{0:T(1024)(128)(2,1)}) %all-gather.12.cloned.1.call-update) | async-done | bytes 8388624 | tf_op jit(solution)/shard_map/all_gather | solution.py:123
  344.6 13.4 reshape.241
  358.0 65.3 %all-gather.14.cloned.1.call-done = bf16[4194304]{0:T(1024)(128)(2,1)} async-done(((bf16[131072]{0:T(1024)(128)(2,1)}), bf16[4194304]{0:T(1024)(128)(2,1)}) %all-gather.14.cloned.1.call-update) | async-done | bytes 8388624 | tf_op jit(solution)/shard_map/all_gather | solution.py:124
  423.2 13.3 reshape.242
  509.0 10.5 fusion.95
  519.5 14.0 convert_reduce_fusion
  545.1 11.3 convert_reduce_fusion.2
  665.3 181.2 %collective-permute-done.2 = f32[2,512,2048]{2,1,0:T(8,128)} collective-permute-done((f32[2,512,2048]{2,1,0:T(8,128)S(1)}, f32[2,512,2048]{2,1,0:T(8,128)}, u32[]{:S(2)}, u32[]{:S(2)}) %collective-permute-start.2) | collective-permute-done | bytes 8388640 | tf_op jit(solution)/shard_map/ppermute | solution.py:20
  846.5 9.6 select_add_fusion
  892.2 10.7 convolution_bitcast_fusion.2
  902.9 14.8 copy.88
  933.6 10.5 fusion.100
  947.0 14.5 convolution_bitcast_fusion.1
  961.5 12.1 copy.86
  973.5 21.1 copy.90
  996.4 40.2 %all-reduce.6 = f32[14336]{0:T(1024)S(1)} all-reduce(f32[14336]{0:T(1024)S(1)} %constant_dynamic-update-slice_fusion.10), channel_id=8, replica_groups=mesh['fsdp'=32] {'fsdp'}, use_global_device_ids=true, to_apply=%region_38.39.clone | all-reduce | flops 14336 | bytes 114688
  1042.1 44.7 %reduce-scatter.4.cloned.1.call-done = f32[256,2]{1,0:T(8,128)} async-done(((f32[8192,2]{1,0:T(8,128)}), f32[256,2]{1,0:T(8,128)}) %reduce-scatter.4.cloned.1.call-update) | async-done | bytes 2064
  1088.4 1081.8 %all-reduce.10.cloned.1.call-done = (f32[3145728]{0:T(1024)}, f32[1048576]{0:T(1024)}, f32[4194304]{0:T(1024)}, f32[4194304]{0:T(1024)}, f32[6291456]{0:T(1024)}) async-done(((f32[3145728]{0:T(1024)}, f32[1048576]{0:T(1024)}, f32[4194304]{0:T(1024)}, f32[4194304]{0:T(1024)}, f32[6291456]{0:T(1024)}), (f32[3145728]{0:T(1024)}, f32[1048576]{0:T(1024)}, f32[4194304]{0:T(1024)}, f32[4194304]{0:T(1024)}, ...) | async-done | bytes 75497488
  (337 shorter events, 300.5 us)
Async XLA Ops:
  7.2 91.7 %all-gather.8.cloned.1.call-start = ((), (), s32[]{:S(2)}) async-start(), calls=%async_computation.2 | async-start | bytes 6488064 | tf_op jit(solution)/shard_map/all_gather | solution.py:121
  7.9 172.9 %all-gather.6.cloned.1.call-start = ((), (), s32[]{:S(2)}) async-start(), calls=%async_computation.1 | async-start | bytes 12976128 | tf_op jit(solution)/shard_map/all_gather | solution.py:125
  8.7 232.4 %all-gather.10.cloned.1.call-start = ((), (), s32[]{:S(2)}) async-start(), calls=%async_computation.3 | async-start | bytes 2162688 | tf_op jit(solution)/shard_map/all_gather | solution.py:122
  9.4 335.2 %all-gather.12.cloned.1.call-start = ((), (), s32[]{:S(2)}) async-start(), calls=%async_computation.4 | async-start | bytes 8650752 | tf_op jit(solution)/shard_map/all_gather | solution.py:123
  10.0 413.3 %all-gather.14.cloned.1.call-start = ((), (), s32[]{:S(2)}) async-start(), calls=%async_computation.5 | async-start | bytes 8650752 | tf_op jit(solution)/shard_map/all_gather | solution.py:124
  10.6 1076.3 %reduce-scatter.4.cloned.1.call-start = ((), (), s32[]{:S(2)}) async-start(), calls=%async_computation.6 | async-start | bytes 4325376
  95.2 104.0 %copy-start.36 = (bf16[2,8192]{1,0:T(2,128)(2,1)}, bf16[2,8192]{1,0:T(2,128)(2,1)S(1)}, u32[]{:S(2)}) copy-start(bf16[2,8192]{1,0:T(2,128)(2,1)S(1)} %all_gather.26) | copy-start | bytes 98308
  97.2 108.5 %copy-start.30 = (f32[2,256]{1,0:T(2,128)}, f32[2,256]{1,0:T(2,128)S(1)}, u32[]{:S(2)}) copy-start(f32[2,256]{1,0:T(2,128)S(1)} %broadcast_multiply_fusion.1) | copy-start | bytes 6148
  98.9 106.8 %copy-start.32 = (f32[2,256]{1,0:T(2,128)}, f32[2,256]{1,0:T(2,128)S(1)}, u32[]{:S(2)}) copy-start(f32[2,256]{1,0:T(2,128)S(1)} %fusion.112) | copy-start | bytes 6148
  205.7 303.3 %copy-start.50 = (f32[2,1024]{1,0:T(2,128)}, f32[2,1024]{1,0:T(2,128)S(1)}, u32[]{:S(2)}) copy-start(f32[2,1024]{1,0:T(2,128)S(1)} %get-tuple-element.35) | copy-start | bytes 24580
  205.7 336.9 %copy-start.39 = (f32[2,1024]{1,0:T(2,128)}, f32[2,1024]{1,0:T(2,128)S(1)}, u32[]{:S(2)}) copy-start(f32[2,1024]{1,0:T(2,128)S(1)} %get-tuple-element.36) | copy-start | bytes 24580
  212.1 4.4 collective-permute-start
  221.8 215.3 %collective-permute-start.1 = (bf16[2,512,2048]{2,1,0:T(8,128)(2,1)}, bf16[2,512,2048]{2,1,0:T(8,128)(2,1)}, u32[]{:S(2)}, u32[]{:S(2)}) collective-permute-start(bf16[2,512,2048]{2,1,0:T(8,128)(2,1)} %maximum_select_fusion.1), channel_id=1, source_target_pairs={{0,2},{1,3},{2,0},{3,1},{4,6},{5,7},{6,4},{7,5},{8,10},{9,11},{10,... | collective-permute-start | bytes 12582920 | tf_op jit(solution)/shard_map/ppermute | solution.py:20
  357.9 78.6 %slice-start.29 = ((bf16[2,256,3072]{2,1,0:T(8,128)(2,1)}), bf16[2,256,1024]{2,1,0:T(8,128)(2,1)S(1)}, s32[]{:S(2)}) async-start(bf16[2,256,3072]{2,1,0:T(8,128)(2,1)} %copy-done.12), calls=%async_computation.37 | async-start | bytes 2097152 | tf_op jit(solution)/shard_map/slice | solution.py:155
  437.1 34.5 %copy-start.25 = (bf16[2,256,1024]{1,2,0:T(8,128)(2,1)}, bf16[2,256,1024]{1,2,0:T(8,128)(2,1)S(1)}, u32[]{:S(2)}) copy-start(bf16[2,256,1024]{1,2,0:T(8,128)(2,1)S(1)} %copy.68) | copy-start | bytes 3145732
  508.6 34.0 %copy-start.43 = (f32[2,256]{1,0:T(2,128)}, f32[2,256]{1,0:T(2,128)S(1)}, u32[]{:S(2)}) copy-start(f32[2,256]{1,0:T(2,128)S(1)} %broadcast_multiply_fusion) | copy-start | bytes 6148
  509.0 33.7 %copy-start.48 = (f32[2,256]{1,0:T(2,128)}, f32[2,256]{1,0:T(2,128)S(1)}, u32[]{:S(2)}) copy-start(f32[2,256]{1,0:T(2,128)S(1)} %fusion.113) | copy-start | bytes 6148
  509.0 24.6 %slice-start.25 = ((s8[8388608]{0:T(1024)(128)(4,1)}), s8[4194304]{0:T(1024)(128)(4,1)S(1)}, s32[]{:S(2)}) async-start(s8[8388608]{0:T(1024)(128)(4,1)} %bitcast.210), calls=%async_computation.33 | async-start | bytes 8388608
  663.7 182.8 %collective-permute-start.2 = (f32[2,512,2048]{2,1,0:T(8,128)S(1)}, f32[2,512,2048]{2,1,0:T(8,128)}, u32[]{:S(2)}, u32[]{:S(2)}) collective-permute-start(f32[2,512,2048]{2,1,0:T(8,128)S(1)} %broadcast_select_fusion), channel_id=1, source_target_pairs={{0,2},{1,3},{2,0},{3,1},{4,6},{5,7},{6,4},{7,5},{8,10},{9,11},{10,... | collective-permute-start | bytes 25165832 | tf_op jit(solution)/shard_map/ppermute | solution.py:20
  860.8 57.0 %collective-permute-start.3 = (f32[2,256,2048]{2,1,0:T(8,128)}, f32[2,256,2048]{2,1,0:T(8,128)}, u32[]{:S(2)}, u32[]{:S(2)}) collective-permute-start(f32[2,256,2048]{2,1,0:T(8,128)} %slice_select_fusion), channel_id=1, source_target_pairs={{0,1},{1,0},{2,3},{3,2},{4,5},{5,4},{6,7},{7,6},{8,9},{9,8},{10,11... | collective-permute-start | bytes 12582920 | tf_op jit(solution)/shard_map/ppermute | solution.py:20
  892.2 25.6 %slice-start.19 = ((s8[8388608]{0:T(1024)(128)(4,1)}), s8[4194304]{0:T(1024)(128)(4,1)S(1)}, s32[]{:S(2)}) async-start(s8[8388608]{0:T(1024)(128)(4,1)} %bitcast.180), calls=%async_computation.27 | async-start | bytes 8388608
  892.2 29.1 %slice-start.27 = ((s8[6291456]{0:T(1024)(128)(4,1)}), s8[4194304]{0:T(1024)(128)(4,1)S(1)}, s32[]{:S(2)}) async-start(s8[6291456]{0:T(1024)(128)(4,1)} %bitcast.212), calls=%async_computation.35 | async-start | bytes 8388608
  946.9 1223.3 %all-reduce.10.cloned.1.call-start = ((), (), s32[]{:S(2)}) async-start(), calls=%async_computation.7 | async-start | bytes 150994944
  994.6 42.7 %copy-start.47 = (f32[2,256]{1,0:T(2,128)S(1)}, f32[2,256]{1,0:T(2,128)}, u32[]{:S(2)}) copy-start(f32[2,256]{1,0:T(2,128)} %copy-done.46) | copy-start | bytes 6148
  (79 other events, 528.0 us)
Sparse Core Ops, SparseCore 0:
  10.9 72.4 all-gather.7
  86.3 94.4 all-gather.5
  183.6 57.3 all-gather.9
  243.8 100.7 all-gather.11
  347.3 75.9 all-gather.13
  947.0 139.7 reduce-scatter.3
  1093.3 1076.9 all-reduce.9
where the time goes:
time: 2200 us; the launch traced here: 2190 us
  waiting for transfers between devices  1570 us (71%)
  matrix products  198 us (9%)
  local copies, waits for them, and re-layouts  187 us (8%)
  blocking collectives  124 us (6%)
  other arithmetic  90 us (4%)
    unnamed x9, waiting for transfers between devices  1130 us
    ppermute x4, waiting for transfers between devices, swapped(): return lax.ppermute(value, axis, pairs)  185 us
    all_gather x1, waiting for transfers between devices, per_device(): lax.all_gather(expand, 'fsdp', axis=0, tiled=True)  99.4 us
    unnamed x211, local copies, waits for them, and re-layouts  89 us
    unnamed x2, blocking collectives  82.9 us
    all_gather x1, waiting for transfers between devices, per_device(): lax.all_gather(modulate, 'fsdp', axis=0, tiled=True)  71.5 us
    all_gather x1, waiting for transfers between devices, per_device(): lax.all_gather(contract, 'fsdp', axis=0, tiled=True)  65.3 us
  transfers between devices with their start and end apart: 11, of which 8 were waited for; matrix products, arithmetic and copies ran while one was open for 9% of the time, Pallas kernels for 0%

commit v1 on v0

v1 whole, which is shorter than its diff:
```python
import functools

import jax
import jax.numpy as jnp
from jax import lax
from jax.experimental import pallas as pl
from jax.experimental.pallas import tpu as pltpu
from jax.sharding import PartitionSpec as P

D = 1024
HEADS = 16
HEAD = 64
FF = 4096
GROUP = 4
OWN = D // GROUP
SCALE = HEAD**-0.5
LANES = 128
MICROS = 2

epsilon = 1e-06
highest = lax.Precision.HIGHEST
MESH = pl.DeviceIdType.MESH
MIB = 1 << 20


def silu(values):
    return values / (1.0 + jnp.exp(-values))


class Links:
    def __init__(self, planes, send_sem, recv_sem, local_sem=None):
        me = lax.axis_index("fsdp")
        self.planes = planes
        self.c = me % 2
        self.x = (me // 2) % 2
        self.y = (me // 4) % 2
        self.z = me // 8
        self.core = me + 1 - 2 * self.c
        self.beside = me + 2 - 4 * self.x
        self.across = me + 4 - 8 * self.y
        self.place = me % 8
        self.send_sem, self.recv_sem, self.local_sem = send_sem, recv_sem, local_sem
        self.used = 0
        self.local_used = 0
        self.pending = []

    def plane(self, step):
        return (self.z + step) % self.planes

    def plane_device(self, step):
        return self.plane(step) * 8 + self.place

    def partners(self):
        return [self.core, self.beside, self.across] + [
            self.plane_device(step) for step in range(1, self.planes)
        ]

    def greet(self, partners):
        barrier = pltpu.get_barrier_semaphore()
        for partner in partners:
            pl.semaphore_signal(barrier, inc=1, device_id=(partner,), device_id_type=MESH)
        pl.semaphore_wait(barrier, len(partners))

    def send(self, source, target, device):
        copy = pltpu.make_async_remote_copy(
            src_ref=source,
            dst_ref=target,
            send_sem=self.send_sem.at[self.used],
            recv_sem=self.recv_sem.at[self.used],
            device_id=(device,),
            device_id_type=MESH,
        )
        self.used += 1
        copy.start()
        self.pending.append(copy)
        return copy

    def local(self, source, target):
        copy = pltpu.make_async_copy(source, target, self.local_sem.at[self.local_used])
        self.local_used += 1
        copy.start()
        return copy

    def finish_sends(self):
        for copy in self.pending:
            copy.wait_send()
        self.pending = []


def arrived(copies):
    for copy in copies:
        copy.wait_recv()


ANY = pl.BlockSpec(memory_space=pl.ANY)
VMEM = pl.BlockSpec(memory_space=pltpu.VMEM)


def remote_call(body, name, collective_id, outs, in_specs, out_specs, scratch, sems, local_sems, vmem):
    return pl.pallas_call(
        body,
        out_shape=outs,
        in_specs=in_specs,
        out_specs=out_specs,
        scratch_shapes=[
            pltpu.SemaphoreType.DMA((sems,)),
            pltpu.SemaphoreType.DMA((sems,)),
            pltpu.SemaphoreType.DMA((max(local_sems, 1),)),
            *scratch,
        ],
        compiler_params=pltpu.CompilerParams(
            collective_id=collective_id, has_side_effects=True, vmem_limit_bytes=vmem
        ),
        name=name,
    )


def small_gather_body(planes, own_ref, out_ref, send_sem, recv_sem, local_sem):
    links = Links(planes, send_sem, recv_sem)
    links.greet(links.partners())
    z, y, x, c = links.z, links.y, links.x, links.c
    out_ref[z, y, x, c] = own_ref[...]
    spread(links, out_ref)
    links.finish_sends()


def spread(links, out_ref):
    z, y, x, c = links.z, links.y, links.x, links.c
    block = out_ref.at[z, y, x, c]
    arrived([links.send(block, block, links.plane_device(s)) for s in range(1, links.planes)])
    block = out_ref.at[:, y, x, c]
    arrived([links.send(block, block, links.across)])
    block = out_ref.at[:, :, x, c]
    arrived([links.send(block, block, links.beside)])
    block = out_ref.at[:, :, :, c]
    arrived([links.send(block, block, links.core)])


def small_gather(own, planes, collective_id):
    return remote_call(
        functools.partial(small_gather_body, planes),
        "small_gather",
        collective_id,
        jax.ShapeDtypeStruct((planes, 2, 2, 2, *own.shape), own.dtype),
        [VMEM],
        VMEM,
        [],
        planes + 2,
        0,
        40 * MIB,
    )(own)


class WeightGather:
    def __init__(self, links, shard, full, parts):
        self.links, self.shard, self.full = links, shard, full
        width = shard.shape[-1] // parts
        self.columns = [pl.ds(part * width, width) for part in range(parts)]
        z, y, x, c = links.z, links.y, links.x, links.c
        self.own = links.local(shard, full.at[z, y, x, c])
        self.own_there = False


def gather_first(weight, part):
    links, columns = weight.links, weight.columns[part]
    source = weight.shard.at[:, columns]
    target = weight.full.at[links.z, links.y, links.x, links.c, :, columns]
    return [links.send(source, target, links.plane_device(s)) for s in range(1, links.planes)]


def gather_second(weight, part, late):
    links, columns = weight.links, weight.columns[part]
    if not weight.own_there:
        weight.own.wait()
        weight.own_there = True
    block = weight.full.at[:, links.y, links.x, links.c, :, columns]
    late.append(links.send(block, block, links.core))
    return [links.send(block, block, links.beside if part % 2 == 0 else links.across)]


def gather_third(weight, part, late):
    links, columns = weight.links, weight.columns[part]
    y, x, c = links.y, links.x, links.c
    if part % 2 == 0:
        fresh = weight.full.at[:, y, 1 - x, c, :, columns]
        block, device = weight.full.at[:, y, :, c, :, columns], links.across
    else:
        fresh = weight.full.at[:, 1 - y, x, c, :, columns]
        block, device = weight.full.at[:, :, x, c, :, columns], links.beside
    late.append(links.send(fresh, fresh, links.core))
    return [links.send(block, block, device)]


def gather_fourth(weight, part, late):
    links, columns = weight.links, weight.columns[part]
    y, x, c = links.y, links.x, links.c
    if part % 2 == 0:
        fresh = weight.full.at[:, 1 - y, :, c, :, columns]
    else:
        fresh = weight.full.at[:, :, 1 - x, c, :, columns]
    late.append(links.send(fresh, fresh, links.core))


def gather_steps(pieces):
    count = len(pieces)
    late = []
    first, second, third = {}, {}, {}
    for k in range(min(2, count)):
        first[k] = gather_first(*pieces[k])
    yield
    for k in range(count + 4):
        if k < count:
            if k + 2 < count:
                first[k + 2] = gather_first(*pieces[k + 2])
            arrived(first.pop(k))
            second[k] = gather_second(*pieces[k], late)
        if 0 <= k - 2 < count:
            arrived(second.pop(k - 2))
            third[k - 2] = gather_third(*pieces[k - 2], late)
        if 0 <= k - 4 < count:
            arrived(third.pop(k - 4))
            gather_fourth(*pieces[k - 4], late)
        yield
    arrived(late)


def gather_body(
    planes,
    tokens,
    attend,
    project,
    expand,
    contract,
    partial,
    tokens_out,
    attend_out,
    project_out,
    expand_out,
    contract_out,
    modulation_out,
    send_sem,
    recv_sem,
    local_sem,
    attend_held,
    sum_core,
    sum_beside,
    sum_across,
    sum_planes,
    total,
):
    links = Links(planes, send_sem, recv_sem, local_sem)
    links.greet(links.partners())
    z, y, x, c = links.z, links.y, links.x, links.c

    weights = [
        WeightGather(links, project, project_out, 2),
        WeightGather(links, expand, expand_out, 4),
        WeightGather(links, contract, contract_out, 4),
    ]
    pieces = [(w, part) for w in weights for part in range(len(w.columns))]

    own_slice = links.local(attend.at[x, c], attend_out.at[z, y, x, c])
    to_core = links.send(attend.at[x, 1 - c], attend_out.at[z, y, x, c], links.core)
    held = links.send(attend.at[1 - x, 1 - c], attend_held, links.core)
    to_beside = links.send(attend.at[1 - x, c], attend_out.at[z, y, x, c], links.beside)
    own_tokens = links.local(tokens, tokens_out.at[:, x, c])
    tokens_core = links.send(tokens, tokens_out.at[:, x, c], links.core)
    tokens_beside = links.send(tokens, tokens_out.at[:, x, c], links.beside)
    step = links.send(partial.at[:, :, :, 1 - c], sum_core, links.core)

    arrived([held])
    held_beside = links.send(attend_held, attend_out.at[z, y, x, 1 - c], links.beside)
    steps = gather_steps(pieces)
    next(steps)

    arrived([step])
    sum_core[...] = sum_core[...] + partial[:, :, :, c]
    step = links.send(sum_core.at[:, :, 1 - x], sum_beside, links.beside)

    own_slice.wait()
    arrived([to_core, to_beside, held_beside])
    half = attend_out.shape[-1] // 2
    over_planes = []
    for part in range(2):
        block = attend_out.at[z, y, :, :, :, pl.ds(part * half, half)]
        over_planes.append(
            [links.send(block, block, links.plane_device(s)) for s in range(1, planes)]
        )

    arrived([step])
    sum_beside[...] = sum_beside[...] + sum_core[:, :, x]
    step = links.send(sum_beside.at[:, 1 - y], sum_across, links.across)

    over_y = []
    for part in range(2):
        arrived(over_planes[part])
        block = attend_out.at[:, y, :, :, :, pl.ds(part * half, half)]
        over_y.append(links.send(block, block, links.across))

    arrived([step])
    sum_across[...] = sum_across[...] + sum_beside[:, y]
    step = [
        links.send(sum_across.at[links.plane(s)], sum_planes.at[s - 1], links.plane_device(s))
        for s in range(1, planes)
    ]
    next(steps)

    arrived(step)
    result = sum_across[z]
    for s in range(1, planes):
        result = result + sum_planes[s - 1]
    total[...] = result
    modulation_out[x, c] = result
    step = [
        links.send(total, modulation_out.at[x, c], links.core),
        links.send(total, modulation_out.at[x, c], links.beside),
    ]
    next(steps)
    arrived(step)
    step = links.send(modulation_out.at[1 - x, c], modulation_out.at[1 - x, c], links.core)

    arrived([tokens_beside])
    fresh = tokens_out.at[:, 1 - x, c]
    tokens_late = links.send(fresh, fresh, links.core)

    for _ in steps:
        pass
    arrived([step, tokens_core, tokens_late, *over_y])
    own_tokens.wait()
    links.finish_sends()


def gather_all(tokens, attend, project, expand, contract, partial, planes):
    grid = (planes, 2, 2, 2)
    rows = partial.shape[-2]

    def full(shard):
        return jax.ShapeDtypeStruct((*grid, *shard.shape[-2:]), shard.dtype)

    return remote_call(
        functools.partial(gather_body, planes),
        "gather_all",
        1,
        (
            jax.ShapeDtypeStruct((tokens.shape[0], 2, 2, *tokens.shape[1:]), tokens.dtype),
            full(attend),
            full(project),
            full(expand),
            full(contract),
            jax.ShapeDtypeStruct((2, 2, rows, LANES), jnp.float32),
        ),
        [ANY] * 5 + [VMEM],
        (ANY,) * 5 + (VMEM,),
        [
            pltpu.VMEM((attend.shape[-2], attend.shape[-1]), attend.dtype),
            pltpu.VMEM((planes, 2, 2, rows, LANES), jnp.float32),
            pltpu.VMEM((planes, 2, rows, LANES), jnp.float32),
            pltpu.VMEM((planes, rows, LANES), jnp.float32),
            pltpu.VMEM((planes - 1, rows, LANES), jnp.float32),
            pltpu.VMEM((rows, LANES), jnp.float32),
        ],
        20 + 13 * (planes - 1) + 10 * 5,
        8,
        40 * MIB,
    )(tokens, attend, project, expand, contract, partial)


def attention_body(qkv_ref, out_ref, log_ref):
    rows = 256
    for head in range(OWN // HEAD):
        at = head * HEAD
        keys = qkv_ref[0, :, OWN + at : OWN + at + HEAD]
        values_t = qkv_ref[0, :, 2 * OWN + at : 2 * OWN + at + HEAD].T

        @pl.loop(0, qkv_ref.shape[1] // rows)
        def _(block):
            here = pl.ds(pl.multiple_of(block * rows, rows), rows)
            queries = qkv_ref[0, here, at : at + HEAD] * SCALE
            scores = lax.dot_general(
                keys, queries, (((1,), (1,)), ((), ())), preferred_element_type=jnp.float32
            )
            top = jnp.max(scores, axis=0, keepdims=True)
            weights = jnp.exp(scores - top)
            totals = jnp.sum(weights, axis=0, keepdims=True)
            blended = jnp.dot(
                values_t, weights.astype(jnp.bfloat16), preferred_element_type=jnp.float32
            )
            out_ref[0, here, at : at + HEAD] = (blended / totals).T.astype(jnp.bfloat16)
            log_ref[0, head, block] = top + jnp.log(totals)


def attention(qkv):
    micros, rows, _ = qkv.shape
    heads = OWN // HEAD
    blocks = rows // 256
    return pl.pallas_call(
        attention_body,
        grid=(micros,),
        out_shape=(
            jax.ShapeDtypeStruct((micros, rows, OWN), jnp.bfloat16),
            jax.ShapeDtypeStruct((micros, heads, blocks, 1, 256), jnp.float32),
        ),
        in_specs=[pl.BlockSpec((1, rows, 3 * OWN), lambda m: (m, 0, 0))],
        out_specs=(
            pl.BlockSpec((1, rows, OWN), lambda m: (m, 0, 0)),
            pl.BlockSpec((1, heads, blocks, 1, 256), lambda m: (m, 0, 0, 0, 0)),
        ),
        compiler_params=pltpu.CompilerParams(vmem_limit_bytes=48 * MIB),
        name="attention",
    )(qkv)


def attention_back_body(qkv_ref, blended_ref, grad_ref, log_ref, out_ref, key_sum, value_sum):
    rows = 256
    for head in range(OWN // HEAD):
        at = head * HEAD
        keys = qkv_ref[0, :, OWN + at : OWN + at + HEAD]
        keys_t = keys.T
        values = qkv_ref[0, :, 2 * OWN + at : 2 * OWN + at + HEAD]
        key_sum[...] = jnp.zeros_like(key_sum)
        value_sum[...] = jnp.zeros_like(value_sum)

        @pl.loop(0, qkv_ref.shape[1] // rows)
        def _(block):
            here = pl.ds(pl.multiple_of(block * rows, rows), rows)
            queries = qkv_ref[0, here, at : at + HEAD] * SCALE
            grads = grad_ref[0, here, at : at + HEAD]
            blended = blended_ref[0, here, at : at + HEAD]
            row_terms = jnp.sum(
                (grads.astype(jnp.float32) * blended.astype(jnp.float32)).T, axis=0, keepdims=True
            )
            scores = lax.dot_general(
                keys, queries, (((1,), (1,)), ((), ())), preferred_element_type=jnp.float32
            )
            chances = jnp.exp(scores - log_ref[0, head, block])
            grad_chances = lax.dot_general(
                values, grads, (((1,), (1,)), ((), ())), preferred_element_type=jnp.float32
            )
            grad_scores = (chances * (grad_chances - row_terms)).astype(jnp.bfloat16)
            value_sum[...] += jnp.dot(
                chances.astype(jnp.bfloat16), grads, preferred_element_type=jnp.float32
            )
            key_sum[...] += jnp.dot(grad_scores, queries, preferred_element_type=jnp.float32)
            grad_queries = jnp.dot(keys_t, grad_scores, preferred_element_type=jnp.float32)
            out_ref[0, here, at : at + HEAD] = (grad_queries.T * SCALE).astype(jnp.bfloat16)

        out_ref[0, :, OWN + at : OWN + at + HEAD] = key_sum[...].astype(jnp.bfloat16)
        out_ref[0, :, 2 * OWN + at : 2 * OWN + at + HEAD] = value_sum[...].astype(jnp.bfloat16)


def attention_back(qkv, blended, grads, logs):
    micros, rows, _ = qkv.shape
    heads = OWN // HEAD
    blocks = rows // 256
    wide = pl.BlockSpec((1, rows, 3 * OWN), lambda m: (m, 0, 0))
    narrow = pl.BlockSpec((1, rows, OWN), lambda m: (m, 0, 0))
    return pl.pallas_call(
        attention_back_body,
        grid=(micros,),
        out_shape=jax.ShapeDtypeStruct((micros, rows, 3 * OWN), jnp.bfloat16),
        in_specs=[
            wide,
            narrow,
            narrow,
            pl.BlockSpec((1, heads, blocks, 1, 256), lambda m: (m, 0, 0, 0, 0)),
        ],
        out_specs=wide,
        scratch_shapes=[pltpu.VMEM((rows, HEAD), jnp.float32)] * 2,
        compiler_params=pltpu.CompilerParams(vmem_limit_bytes=48 * MIB),
        name="attention_back",
    )(qkv, blended, grads, logs)


def heads_to_tokens_body(blended, out, send_sem, recv_sem, local_sem):
    links = Links(1, send_sem, recv_sem, local_sem)
    x, c = links.x, links.c
    corner = links.beside + 1 - 2 * c
    links.greet([links.core, links.beside, corner])
    target = out.at[:, :, pl.ds(pl.multiple_of((2 * x + c) * OWN, OWN), OWN)]
    own = links.local(blended.at[:, x, c], target)
    copies = [
        links.send(blended.at[:, 1 - x, 1 - c], target, corner),
        links.send(blended.at[:, 1 - x, c], target, links.beside),
        links.send(blended.at[:, x, 1 - c], target, links.core),
    ]
    arrived(copies)
    own.wait()
    links.finish_sends()


def heads_to_tokens(blended):
    micros, rows, _ = blended.shape
    own_rows = rows // GROUP
    return remote_call(
        heads_to_tokens_body,
        "heads_to_tokens",
        2,
        jax.ShapeDtypeStruct((micros, own_rows, D), blended.dtype),
        [ANY],
        ANY,
        [],
        3,
        1,
        40 * MIB,
    )(blended.reshape(micros, 2, 2, own_rows, OWN))


def tokens_to_heads_body(grads, out, send_sem, recv_sem, local_sem):
    links = Links(1, send_sem, recv_sem, local_sem)
    x, c = links.x, links.c
    corner = links.beside + 1 - 2 * c
    links.greet([links.core, links.beside, corner])

    def columns(to_x, to_c):
        return grads.at[:, :, pl.ds(pl.multiple_of((2 * to_x + to_c) * OWN, OWN), OWN)]

    target = out.at[:, x, c]
    own = links.local(columns(x, c), target)
    copies = [
        links.send(columns(1 - x, 1 - c), target, corner),
        links.send(columns(1 - x, c), target, links.beside),
        links.send(columns(x, 1 - c), target, links.core),
    ]
    arrived(copies)
    own.wait()
    links.finish_sends()


def tokens_to_heads(grads):
    micros, own_rows, _ = grads.shape
    return remote_call(
        tokens_to_heads_body,
        "tokens_to_heads",
        3,
        jax.ShapeDtypeStruct((micros, 2, 2, own_rows, OWN), grads.dtype),
        [ANY],
        ANY,
        [],
        3,
        1,
        40 * MIB,
    )(grads).reshape(micros, GROUP * own_rows, OWN)


def token_sums_body(partial, out, send_sem, recv_sem, local_sem, from_core, own, from_beside):
    links = Links(1, send_sem, recv_sem, local_sem)
    x, c = links.x, links.c
    links.greet([links.core, links.beside])
    far = links.send(partial.at[:, 1 - x, 1 - c], from_core.at[0], links.core)
    near = links.send(partial.at[:, x, 1 - c], from_core.at[1], links.core)
    loads = [
        links.local(partial.at[:, 1 - x, c], own.at[0]),
        links.local(partial.at[:, x, c], own.at[1]),
    ]
    micros = out.shape[0]
    loads[0].wait()
    arrived([far])
    passed = []
    for m in range(micros):
        own[0, m] = (
            own[0, m].astype(jnp.float32) + from_core[0, m].astype(jnp.float32)
        ).astype(jnp.bfloat16)
        passed.append(links.send(own.at[0, m], from_beside.at[m], links.beside))
    loads[1].wait()
    arrived([near])
    for m in range(micros):
        out[m] = own[1, m].astype(jnp.float32) + from_core[1, m].astype(jnp.float32)
    for m in range(micros):
        arrived([passed[m]])
        out[m] += from_beside[m].astype(jnp.float32)
    links.finish_sends()


def token_sums(partial):
    micros, rows, width = partial.shape
    own_rows = rows // GROUP
    held = pltpu.VMEM((2, micros, own_rows, width), partial.dtype)
    return remote_call(
        token_sums_body,
        "token_sums",
        4,
        jax.ShapeDtypeStruct((micros, own_rows, width), jnp.float32),
        [ANY],
        VMEM,
        [held, held, pltpu.VMEM((micros, own_rows, width), partial.dtype)],
        4,
        2,
        40 * MIB,
    )(partial.reshape(micros, 2, 2, own_rows, width))


def small_sums_body(planes, partial, out, send_sem, recv_sem, local_sem, from_core, from_beside):
    links = Links(planes, send_sem, recv_sem)
    links.greet(links.partners())
    z, y, x, c = links.z, links.y, links.x, links.c
    arrived([links.send(partial.at[:, 1 - c], from_core, links.core)])
    from_core[...] = from_core[...] + partial[:, c]
    arrived([links.send(from_core.at[1 - x], from_beside, links.beside)])
    out[z, y, x, c] = from_core[x] + from_beside[...]
    spread(links, out)
    links.finish_sends()


def small_sums(partial, planes):
    block = partial.shape[2:]
    return remote_call(
        functools.partial(small_sums_body, planes),
        "small_sums",
        5,
        jax.ShapeDtypeStruct((planes, 2, 2, 2, *block), jnp.float32),
        [VMEM],
        VMEM,
        [pltpu.VMEM((2, *block), jnp.float32), pltpu.VMEM(block, jnp.float32)],
        planes + 4,
        0,
        40 * MIB,
    )(partial)


class SumPiece:
    def __init__(self, links, grads, out, columns, part, scratch):
        self.links, self.grads, self.out = links, grads, out
        self.columns, self.part = columns, part
        self.own, self.first, self.second, self.third, self.fourth = scratch


def add_blocks(target, left, right, count):
    @pl.loop(0, count)
    def _(i):
        target(i)[...] = (
            left(i)[...].astype(jnp.float32) + right(i)[...].astype(jnp.float32)
        ).astype(jnp.bfloat16)


def sum_first(piece):
    links = piece.links
    c = links.c
    source = piece.grads.at[:, :, :, 1 - c, :, piece.columns]
    sent = links.send(source, piece.first, links.core)
    loaded = links.local(piece.grads.at[:, :, :, c, :, piece.columns], piece.own)
    return sent, loaded


def sum_second(piece, before):
    links = piece.links
    x, y, planes = links.x, links.y, links.planes
    sent, loaded = before
    loaded.wait()
    arrived([sent])
    own, first = piece.own, piece.first
    turn = piece.part % 2 == 0
    for order in range(2):

        def at(ref):
            def block(i):
                z, other = i // 2, i % 2
                if turn:
                    return ref.at[z, other, (1 - x) if order == 0 else x]
                return ref.at[z, (1 - y) if order == 0 else y, other]

            return block

        add_blocks(at(own), at(own), at(first), planes * 2)
        if order == 0:
            source = own.at[:, :, 1 - x] if turn else own.at[:, 1 - y]
            copy = links.send(source, piece.second, links.beside if turn else links.across)
    return copy


def sum_third(piece, before):
    links = piece.links
    x, y, planes = links.x, links.y, links.planes
    arrived([before])
    own, second = piece.own, piece.second
    turn = piece.part % 2 == 0
    for order in range(2):
        if turn:
            away = (1 - y) if order == 0 else y

            def kept(i):
                return own.at[i, away, x]

        else:
            away = (1 - x) if order == 0 else x

            def kept(i):
                return own.at[i, y, away]

        def came(i):
            return second.at[i, away]

        add_blocks(came, kept, came, planes)
        if order == 0:
            copy = links.send(
                second.at[:, away], piece.third, links.across if turn else links.beside
            )
    return copy


def sum_fourth(piece, before):
    links = piece.links
    x, y, z, planes = links.x, links.y, links.z, links.planes
    arrived([before])
    second, third = piece.second, piece.third
    stay = y if piece.part % 2 == 0 else x

    def kept(i):
        return second.at[i, stay]

    def came(i):
        return third.at[i]

    add_blocks(came, kept, came, planes)
    return [
        links.send(third.at[links.plane(s)], piece.fourth.at[s - 1], links.plane_device(s))
        for s in range(1, planes)
    ]


def sum_last(piece, before):
    links = piece.links
    arrived(before)
    result = piece.third[links.z].astype(jnp.float32)
    for s in range(1, links.planes):
        result = result + piece.fourth[s - 1].astype(jnp.float32)
    piece.out[:, piece.columns] = result


def sum_steps(pieces):
    count = len(pieces)
    stages = (sum_second, sum_third, sum_fourth, sum_last)
    state = {}
    for k in range(count + 5):
        if k < count:
            state[k] = sum_first(pieces[k])
        yield
        for stage, run in enumerate(stages):
            j = k - 1 - stage
            if 0 <= j < count:
                state[j] = run(pieces[j], state[j])
        yield


def sums_body(planes, plan, attend, *refs):
    links_sems, scratch = refs[2 * len(plan) + 1 :][:3], refs[2 * len(plan) + 4 :]
    grads, attend_out, outs = refs[: len(plan)], refs[len(plan)], refs[len(plan) + 1 :][: len(plan)]
    links = Links(planes, *links_sems)
    links.greet(links.partners())
    z, y, x, c = links.z, links.y, links.x, links.c
    attend_own, attend_across, attend_planes, attend_sum, attend_held = scratch[:5]
    scratch = scratch[5:]
    pieces = []
    used = 0
    for parts, grad, out in zip(plan, grads, outs):
        width = grad.shape[-1] // parts
        for part in range(parts):
            pieces.append(
                SumPiece(links, grad, out, pl.ds(part * width, width), part, scratch[used : used + 5])
            )
            used += 5

    step = links.send(attend.at[:, 1 - y], attend_across, links.across)
    loaded = links.local(attend.at[:, y], attend_own)
    steps = sum_steps(pieces)
    next(steps)
    next(steps)
    loaded.wait()
    arrived([step])
    for i in range(2):

        def block(ref):
            return lambda k: ref.at[k // 2, i, k % 2]

        add_blocks(block(attend_own), block(attend_own), block(attend_across), planes * 2)
    over = [
        links.send(attend_own.at[links.plane(s)], attend_planes.at[s - 1], links.plane_device(s))
        for s in range(1, planes)
    ]
    next(steps)
    next(steps)
    arrived(over)
    for i in range(2):
        for j in range(2):
            result = attend_own[z, i, j].astype(jnp.float32)
            for s in range(1, planes):
                result = result + attend_planes[s - 1, i, j].astype(jnp.float32)
            attend_sum[i, j] = result
    beside = links.send(attend_sum.at[1 - x], attend_held, links.beside)
    near = links.send(attend_sum.at[x, 1 - c], attend_out.at[x, c], links.core)
    attend_out[x, c] = attend_sum[x, c]
    next(steps)
    next(steps)
    arrived([beside])
    attend_out[1 - x, c] = attend_held[c]
    far = links.send(attend_held.at[1 - c], attend_out.at[1 - x, c], links.core)
    for _ in steps:
        pass
    arrived([near, far])
    links.finish_sends()


def weight_sums(attend, weights, plan, planes):
    def piece_scratch(grad, parts):
        rows, width = grad.shape[-2], grad.shape[-1] // parts
        return [
            pltpu.VMEM((planes, 2, 2, rows, width), jnp.bfloat16),
            pltpu.VMEM((planes, 2, 2, rows, width), jnp.bfloat16),
            pltpu.VMEM((planes, 2, rows, width), jnp.bfloat16),
            pltpu.VMEM((planes, rows, width), jnp.bfloat16),
            pltpu.VMEM((planes - 1, rows, width), jnp.bfloat16),
        ]

    rows, width = attend.shape[-2:]
    scratch = [
        pltpu.VMEM((planes, 2, 2, rows, width), jnp.bfloat16),
        pltpu.VMEM((planes, 2, 2, rows, width), jnp.bfloat16),
        pltpu.VMEM((planes - 1, 2, 2, rows, width), jnp.bfloat16),
        pltpu.VMEM((2, 2, rows, width), jnp.float32),
        pltpu.VMEM((2, rows, width), jnp.float32),
    ]
    for grad, parts in zip(weights, plan):
        for _ in range(parts):
            scratch += piece_scratch(grad, parts)
    return remote_call(
        functools.partial(sums_body, planes, plan),
        "weight_sums",
        6,
        (
            jax.ShapeDtypeStruct((2, 2, rows, width), jnp.float32),
            *(jax.ShapeDtypeStruct(grad.shape[-2:], jnp.float32) for grad in weights),
        ),
        [ANY] * (1 + len(weights)),
        (VMEM,) * (1 + len(weights)),
        scratch,
        8 + planes + sum(plan) * (2 + planes),
        2 + sum(plan),
        60 * MIB,
    )(attend, *weights)


def normalize(values):
    center = values - jnp.mean(values, axis=-1, keepdims=True)
    spread_of = jnp.mean(center * center, axis=-1, keepdims=True)
    scale = lax.rsqrt(spread_of + epsilon)
    return center * scale, scale


def norm_back(grads, normed, scale, factors):
    inner = grads * (1.0 + factors)
    return scale * (
        inner
        - jnp.mean(inner, axis=-1, keepdims=True)
        - normed * jnp.mean(inner * normed, axis=-1, keepdims=True)
    )


def einsum(spec, left, right):
    return jnp.einsum(spec, left, right, preferred_element_type=jnp.float32)


def per_device(tokens, condition, attend, project, expand, contract, modulate, biases, cotangent):
    devices = lax.axis_size("fsdp")
    planes = devices // 8
    latents = devices // GROUP
    me = lax.axis_index("fsdp")
    quarter, latent = me % GROUP, me // GROUP
    micros, own_rows, _ = tokens.shape
    latent_rows = own_rows * GROUP
    rows = D // devices
    grid = (planes, 2, 2, 2)

    held = jnp.concatenate([condition.reshape(-1), biases]).astype(jnp.float32)
    held = jnp.pad(held, (0, -held.size % (8 * LANES)))
    small = small_gather(held.reshape(-1, LANES), planes, 0).reshape(devices, -1)
    conditions = small[:, : condition.size].reshape(latents, GROUP, micros, -1)
    conditions = conditions.transpose(2, 0, 1, 3).reshape(micros * latents, D)
    cond_act = silu(conditions).astype(jnp.bfloat16)
    bias_all = small[:, condition.size : condition.size + biases.size].reshape(-1)
    bias_query = bias_all[0:D]
    bias_value = bias_all[D : 2 * D]
    bias_project = bias_all[2 * D : 3 * D]
    bias_expand = bias_all[3 * D : 3 * D + FF]
    bias_contract = bias_all[3 * D + FF : 4 * D + FF]
    bias_modulate = bias_all[4 * D + FF :]

    modulate_rows = modulate.reshape(rows, 6 * D)
    cond_own = lax.dynamic_slice_in_dim(cond_act, me * rows, rows, axis=1)
    partial = jnp.dot(cond_own, modulate_rows, preferred_element_type=jnp.float32)
    partial = partial.reshape(micros, latents, GROUP, -1).transpose(1, 2, 0, 3)
    partial = partial.reshape(planes, 2, 2, 2, -1, LANES)

    attend_shard = attend.reshape(rows, 3, 2, 2, OWN).transpose(2, 3, 0, 1, 4)
    gathered = gather_all(
        tokens,
        attend_shard.reshape(2, 2, rows, 3 * OWN),
        project.reshape(rows, D),
        expand.reshape(rows, FF),
        contract.reshape(FF // devices, D),
        partial,
        planes,
    )
    tokens_latent = gathered[0].reshape(micros, latent_rows, D)
    attend_own = gathered[1].reshape(D, 3 * OWN)
    project_full = gathered[2].reshape(D, D)
    expand_full = gathered[3].reshape(D, FF)
    contract_full = gathered[4].reshape(FF, D)
    modulation = gathered[5].reshape(GROUP, micros, -1).transpose(1, 0, 2)
    modulation = modulation.reshape(micros, 6 * D) + bias_modulate
    offsets_one, factors_one, gates_one, offsets_two, factors_two, gates_two = (
        modulation[:, None, part * D : (part + 1) * D] for part in range(6)
    )

    normed_latent, _ = normalize(tokens_latent.astype(jnp.float32))
    first = (normed_latent * (1.0 + factors_one) + offsets_one).astype(jnp.bfloat16)
    bias_row = jnp.concatenate(
        [
            lax.dynamic_slice_in_dim(bias_query, quarter * OWN, OWN),
            jnp.zeros((OWN,), jnp.float32),
            lax.dynamic_slice_in_dim(bias_value, quarter * OWN, OWN),
        ]
    )
    projected = (einsum("mrd,de->mre", first, attend_own) + bias_row).astype(jnp.bfloat16)
    blended_heads, logs = attention(projected)
    blended = heads_to_tokens(blended_heads)

    inputs = tokens.astype(jnp.float32)
    attended = einsum("mrd,de->mre", blended, project_full) + bias_project
    middle = inputs + gates_one * attended
    normed_two, scale_two = normalize(middle)
    second = (normed_two * (1.0 + factors_two) + offsets_two).astype(jnp.bfloat16)
    hidden = einsum("mrd,de->mre", second, expand_full) + bias_expand
    activated, gelu_pull = jax.vjp(lambda v: jax.nn.gelu(v, approximate=True), hidden)
    act_low = activated.astype(jnp.bfloat16)
    branch = einsum("mrd,de->mre", act_low, contract_full) + bias_contract
    output = (middle + gates_two * branch).astype(jnp.bfloat16)

    upstream = cotangent.astype(jnp.float32)
    grad_branch = (gates_two * upstream).astype(jnp.bfloat16)
    grad_gates_two = jnp.sum(upstream * branch, axis=1)
    grad_contract = einsum("mrd,mre->de", act_low, grad_branch)
    grad_act = einsum("mre,de->mrd", grad_branch, contract_full)
    grad_hidden = gelu_pull(grad_act)[0].astype(jnp.bfloat16)
    grad_expand = einsum("mrd,mre->de", second, grad_hidden)
    grad_second = einsum("mre,de->mrd", grad_hidden, expand_full)
    grad_middle = upstream + norm_back(grad_second, normed_two, scale_two, factors_two)
    grad_attended = (gates_one * grad_middle).astype(jnp.bfloat16)
    grad_gates_one = jnp.sum(grad_middle * attended, axis=1)
    grad_project = einsum("mrd,mre->de", blended, grad_attended)
    grad_blended = einsum("mre,de->mrd", grad_attended, project_full).astype(jnp.bfloat16)
    grad_heads = tokens_to_heads(grad_blended)
    grad_projected = attention_back(projected, blended_heads, grad_heads, logs)
    grad_attend = einsum("mrd,mre->de", first, grad_projected)
    grad_first = token_sums(
        einsum("mre,de->mrd", grad_projected, attend_own).astype(jnp.bfloat16)
    )
    normed_one, scale_one = normalize(inputs)
    grad_tokens = grad_middle + norm_back(grad_first, normed_one, scale_one, factors_one)

    grad_modulation = jnp.concatenate(
        [
            jnp.sum(grad_first, axis=1),
            jnp.sum(grad_first * normed_one, axis=1),
            grad_gates_one,
            jnp.sum(grad_second, axis=1),
            jnp.sum(grad_second * normed_two, axis=1),
            grad_gates_two,
        ],
        axis=1,
    )

    def token_sum(values):
        return jnp.sum(values, axis=(0, 1), dtype=jnp.float32)

    heads_sum = token_sum(grad_projected)
    bias_terms = jnp.concatenate(
        [
            lax.dynamic_update_slice(
                jnp.zeros((D,), jnp.float32), heads_sum[:OWN], (quarter * OWN,)
            ),
            lax.dynamic_update_slice(
                jnp.zeros((D,), jnp.float32), heads_sum[2 * OWN :], (quarter * OWN,)
            ),
            token_sum(grad_attended),
            token_sum(grad_hidden),
            token_sum(grad_branch),
        ]
    )
    to_sum = jnp.concatenate(
        [
            grad_modulation.reshape(micros, GROUP, -1).transpose(1, 0, 2).reshape(GROUP, -1),
            bias_terms.reshape(GROUP, -1),
        ],
        axis=1,
    )
    sums = small_sums(to_sum.reshape(2, 2, -1, LANES), planes).reshape(latents, GROUP, -1)
    split = micros * 6 * D // GROUP
    grad_modulations = sums[:, :, :split].reshape(latents, GROUP, micros, -1)
    grad_modulations = grad_modulations.transpose(2, 0, 1, 3).reshape(micros * latents, 6 * D)
    bias_sums = jnp.concatenate(
        [jnp.sum(sums[:, :, split:], axis=0).reshape(-1), jnp.sum(grad_modulations, axis=0)]
    )
    grad_biases = lax.dynamic_slice_in_dim(bias_sums, me * biases.size, biases.size)
    grad_modulate = lax.dot_general(
        cond_own.astype(jnp.float32),
        grad_modulations,
        (((0,), (0,)), ((), ())),
        precision=highest,
    )
    grad_cond_cols = lax.dot_general(
        grad_modulations,
        modulate_rows.astype(jnp.float32),
        (((1,), (1,)), ((), ())),
        precision=highest,
    )
    cols = grad_cond_cols.reshape(-1)
    cols = jnp.pad(cols, (0, -cols.size % (8 * LANES)))
    cols_all = small_gather(cols.reshape(-1, LANES), planes, 7).reshape(devices, -1)
    cols_all = cols_all[:, : micros * latents * rows].reshape(devices, micros, latents, rows)
    cols_own = lax.dynamic_index_in_dim(cols_all, latent, axis=2, keepdims=False)
    width = D // GROUP
    cols_own = lax.dynamic_slice_in_dim(
        cols_own, quarter * (devices // GROUP), devices // GROUP, axis=0
    )
    grad_silu = cols_own.transpose(1, 0, 2).reshape(micros, width)
    values = condition.astype(jnp.float32)
    gate = 1.0 / (1.0 + jnp.exp(-values))
    grad_condition = gate * (1.0 + values * (1.0 - gate)) * grad_silu

    weights = (
        grad_contract.astype(jnp.bfloat16).reshape(*grid, FF // devices, D),
        grad_expand.astype(jnp.bfloat16).reshape(*grid, rows, FF),
        grad_project.astype(jnp.bfloat16).reshape(*grid, rows, D),
    )
    attend_sum, contract_sum, expand_sum, project_sum = weight_sums(
        grad_attend.astype(jnp.bfloat16).reshape(*grid, rows, 3 * OWN), weights, (4, 4, 2), planes
    )
    attend_sum = attend_sum.reshape(2, 2, rows, 3, OWN).transpose(2, 3, 0, 1, 4)
    return (
        output,
        grad_tokens,
        grad_condition,
        attend_sum.reshape(-1),
        project_sum.reshape(-1),
        expand_sum.reshape(-1),
        contract_sum.reshape(-1),
        grad_modulate.reshape(-1),
        grad_biases,
    )


def solution(mesh):
    in_specs = (
        P(None, "fsdp", None),
        P(None, "fsdp"),
        P("fsdp"),
        P("fsdp"),
        P("fsdp"),
        P("fsdp"),
        P("fsdp"),
        P("fsdp"),
        P(None, "fsdp", None),
    )
    out_specs = (
        P(None, "fsdp", None),
        P(None, "fsdp", None),
        P(None, "fsdp"),
        P("fsdp"),
        P("fsdp"),
        P("fsdp"),
        P("fsdp"),
        P("fsdp"),
        P("fsdp"),
    )
    return jax.shard_map(
        per_device, mesh=mesh, in_specs=in_specs, out_specs=out_specs, check_vma=False
    )
```

time: 2200 us -> 587 us (0.27)
  waiting for transfers between devices: 1570 us -> 0 us
  Pallas kernels: 0 us -> 441 us
  local copies, waits for them, and re-layouts: 187 us -> 30.9 us
  blocking collectives: 124 us -> 0 us
  matrix products: 198 us -> 89.6 us
  other arithmetic: 90 us -> 13.6 us
    unnamed x9 -> x0, waiting for transfers between devices: 1130 us -> none
    pallas_call x0 -> x10, Pallas kernels: none -> 441 us  [the longest x1 136 us: gather_all(): remote_call(functools.partial(gather_body, planes), 'gather_all', 1, (jax...]
    all_gather x5 -> x0, waiting for transfers between devices: 254 us -> none  [the longest x1 99.4 us: per_device(): lax.all_gather(expand, 'fsdp', axis=0, tiled=True)]
    ppermute x4 -> x0, waiting for transfers between devices: 185 us -> none  [swapped(): return lax.ppermute(value, axis, pairs)]
    dot_general x39 -> x15, matrix products: 198 us -> 89.6 us  [the longest x12 87.7 us: einsum(): return jnp.einsum(spec, left, right, preferred_element_type=jnp.float32)]
    unnamed x2 -> x0, blocking collectives: 82.9 us -> none
    unnamed x211 -> x111, local copies, waits for them, and re-layouts: 89 us -> 12.7 us
    reshape x8 -> x18, local copies, waits for them, and re-layouts: 78.3 us -> 7.16 us  [the longest x1 1.3 us: per_device(): attend_sum = attend_sum.reshape(2, 2, rows, 3, OWN).transpose(2, 3, 0, 1, 4)]
  transfers between devices with their start and end apart: 11 -> 0, of which waited for: 8 -> 0; matrix products, arithmetic and copies ran while one was open for 9% -> 0% of each run, Pallas kernels for 0% -> 0%
where the time goes in v1:
time: 587 us; the launch traced here: 577 us
  Pallas kernels  441 us (75%)
  matrix products  89.6 us (15%)
  local copies, waits for them, and re-layouts  30.9 us (5%)
  other arithmetic  13.6 us (2%)
    pallas_call x1, Pallas kernels, gather_all(): remote_call(functools.partial(gather_body, planes), 'gather_all', 1, (jax...  136 us
    pallas_call x1, Pallas kernels, weight_sums(): remote_call(functools.partial(sums_body, planes, plan), 'weight_sums', 6,...  130 us
    dot_general x12, matrix products, einsum(): return jnp.einsum(spec, left, right, preferred_element_type=jnp.float32)  87.7 us
    pallas_call x1, Pallas kernels, attention_back(): pl.pallas_call(attention_back_body, grid=(micros,), out_shape=jax.ShapeDt...  34.9 us
    pallas_call x1, Pallas kernels, attention(): pl.pallas_call(attention_body, grid=(micros,), out_shape=(jax.ShapeDtypeS...  30.8 us
    pallas_call x1, Pallas kernels, token_sums(): remote_call(token_sums_body, 'token_sums', 4, jax.ShapeDtypeStruct((micro...  28.3 us
    pallas_call x2, Pallas kernels, small_gather(): remote_call(functools.partial(small_gather_body, planes), 'small_gather',...  27.4 us
    pallas_call x1, Pallas kernels, small_sums(): remote_call(functools.partial(small_sums_body, planes), 'small_sums', 5,...  24.5 us

profile of v1, /device:TPU:0, one launch (start us, length us, event | category | flops | bytes accessed | tf_op | source)
XLA Modules:
  0.0 577.0 jit_solution(13759850736493084209)
XLA Ops:
  2.1 14.9 %small_gather.2 = f32[4,2,2,2,8,128]{5,4,3,2,1,0:T(8,128)S(1)} custom-call(f32[8,128]{1,0:T(8,128)S(1)} %fusion.42.own_ref), custom_call_target="tpu_custom_call" | custom-call | tf_op jit(solution)/shard_map/small_gather/pallas_call | solution.py:140
  23.9 135.9 %gather_all.1 = (bf16[2,2,2,256,1024]{4,3,2,1,0:T(8,128)(2,1)S(1)}, bf16[4,2,2,2,32,768]{5,4,3,2,1,0:T(8,128)(2,1)S(1)}, bf16[4,2,2,2,32,1024]{5,4,3,2,1,0:T(8,1...) custom-call(bf16[2,256,1024]{2,1,0:T(8,128)(2,1)S(1)} %copy-done.2, ...), custom_call_target="tpu_custom_call" | custom-call | tf_op jit(solution)/shard_map/gather_all/pallas_call | solution.py:340
  159.8 2.0 copy-done
  164.9 3.0 convert_reduce_fusion.2
  171.3 3.6 add_convert_fusion.2.qkv_ref
  175.0 30.8 %attention.1 = (bf16[2,1024,256]{2,1,0:T(8,128)(2,1)S(1)}, f32[2,4,4,1,256]{4,3,2,1,0:T(1,128)S(1)}) custom-call(bf16[2,1024,768]{2,1,0:T(8,128)(2,1)S(1)} %add_convert_fusion.2.qkv_ref), custom_call_target="tpu_custom_call" | custom-call | tf_op jit(solution)/shard_map/attention/pallas_call | solution.py:396
  205.8 14.5 %heads_to_tokens.1 = bf16[2,256,1024]{2,1,0:T(8,128)(2,1)S(1)} custom-call(bf16[2,2,2,256,256]{4,3,2,1,0:T(8,128)(2,1)S(1)} %bitcast.138), custom_call_target="tpu_custom_call" | custom-call | tf_op jit(solution)/shard_map/heads_to_tokens/pallas_call | solution.py:494
  222.4 10.6 %fusion.29 = f32[2,256,4096]{2,1,0:T(8,128)} fusion(bf16[1024,4096,1]{1,0,2:T(8,128)(2,1)} %bitcast.183, f32[2,256,1024]{2,1,0:T(8,128)S(1)} %get-tuple-element.48, f32[2,1024]{1,0:T(2,128)S(1)} %get-tuple-element.58, f32[2,1024]{1,0:T(2,128)S(1)} %get-tuple-element.59, f32[2,256]{1,0:T(2,128)S(1)} %add_rsqrt_fusion.2, f32[2,256]{1,0:T(2,128)S(1)} %get-tuple-element.68), kind=kOutput, calls=%fused_computation.73 | convolution fusion | flops 4297588736 | bytes 18894848 | tf_op jit(solution)/shard_map/mrd,de->mre/dot_general | solution.py:858
  233.0 13.5 %convert_reduce_fusion = (f32[4096]{0:T(1024)S(1)}, bf16[2,256,4096]{2,1,0:T(8,128)(2,1)S(1)}) fusion(f32[2,256,4096]{2,1,0:T(8,128)} %fusion.29, f32[4096]{0:T(1024)S(1)} %slice.88, bf16[4096,1024,1]{1,0,2:T(8,128)(2,1)} %bitcast.181, bf16[2,256,1024]{2,1,0:T(8,128)(2,1)S(1)} %copy-done.41, f32[2,1024]{1,0:T(2,128)S(1)} %get-tuple-element.57), kind=kOutput, calls=%fused_computation.12 | convolution fusion | flops 4344770560 | bytes 22061056 | tf_op jit(solution)/shard_map/mre,de->mrd/dot_general | solution.py:858
  246.5 9.0 %multiply_reduce_fusion.1 = (f32[2,1024]{1,0:T(2,128)S(1)}, f32[2,256]{1,0:T(2,128)S(1)}, f32[2,256]{1,0:T(2,128)S(1)}, f32[2,1024]{1,0:T(2,128)S(1)}, f32[2,256,1024]{2,1,0:T(8,128)S(1)}) fusion(f32[2,256,1024]{2,1,0:T(8,128)S(1)} %get-tuple-element.48, f32[2,256]{1,0:T(2,128)S(1)} %add_rsqrt_fusion.2, f32[2,256]{1,0:T(2,128)S(1)} %get-tuple-element.68, ...), kind=kOutput, calls=%fused_computation.49 | convolution fusion | flops 4299680768 | bytes 16809984 | tf_op jit(solution)/shard_map/mre,de->mrd/dot_general | solution.py:858
  255.7 12.2 %fusion.24 = (f32[2,1024]{1,0:T(2,128)S(1)}, f32[1024]{0:T(1024)S(1)}, bf16[2,256,1024]{2,1,0:T(8,128)(2,1)}, f32[2,1024]{1,0:T(2,128)S(1)}, f32[2,256,1024]{2,1,0:T(8,128)S(1)}) fusion(bf16[2,256,1024]{2,1,0:T(8,128)(2,1)S(1)} %copy-done.41, f32[1024]{0:T(1024)S(1)} %copy-done.36, f32[2,1024]{1,0:T(2,128)S(1)} %get-tuple-element.57, ...), kind=kOutput, calls=%fused_computation.46 | convolution fusion | flops 4327468032 | bytes 27332608 | tf_op jit(solution)/shard_map/mrd,de->mre/dot_general | solution.py:858
  269.5 14.4 %tokens_to_heads.1 = bf16[2,2,2,256,256]{4,3,2,1,0:T(8,128)(2,1)S(1)} custom-call(bf16[2,256,1024]{2,1,0:T(8,128)(2,1)S(1)} %convolution_convert_fusion.1.grads), custom_call_target="tpu_custom_call" | custom-call | tf_op jit(solution)/shard_map/tokens_to_heads/pallas_call | solution.py:531
  283.9 34.9 %attention_back.1 = bf16[2,1024,768]{2,1,0:T(8,128)(2,1)S(1)} custom-call(bf16[2,1024,768]{2,1,0:T(8,128)(2,1)} %copy-done.5, bf16[2,1024,256]{2,1,0:T(8,128)(2,1)S(1)} %get-tuple-element.24.blended_ref, bf16[2,1024,256]{2,1,0:T(8,128)(2,1)S(1)} %bitcast.139, f32[2,4,4,1,256]{4,3,2,1,0:T(1,128)S(1)} %get-tuple-element.28.log_ref), custom_call_target="tpu_custom_call" | custom-call | tf_op jit(solution)/shard_map/attention_back/pallas_call | solution.py:457
  318.8 3.7 convolution_convert_fusion
  322.5 28.3 %token_sums.1 = f32[2,256,1024]{2,1,0:T(8,128)S(1)} custom-call(bf16[2,2,2,256,1024]{4,3,2,1,0:T(8,128)(2,1)S(1)} %bitcast.137), custom_call_target="tpu_custom_call" | custom-call | tf_op jit(solution)/shard_map/token_sums/pallas_call | solution.py:578
  351.9 2.0 fusion.20
  354.8 24.5 %small_sums.1 = f32[4,2,2,2,40,128]{5,4,3,2,1,0:T(8,128)S(1)} custom-call(f32[2,2,40,128]{3,2,1,0:T(8,128)S(1)} %bitcast.142), custom_call_target="tpu_custom_call" | custom-call | tf_op jit(solution)/shard_map/small_sums/pallas_call | solution.py:606
  381.5 12.5 %small_gather.3 = f32[4,2,2,2,8,128]{5,4,3,2,1,0:T(8,128)S(1)} custom-call(f32[8,128]{1,0:T(8,128)S(1)} %pad_bitcast_fusion.own_ref), custom_call_target="tpu_custom_call" | custom-call | tf_op jit(solution)/shard_map/small_gather/pallas_call | solution.py:140
  394.9 7.2 %copy.42 = f32[2,1024,1024]{1,2,0:T(8,128)} copy(bf16[2,1024,1024]{2,1,0:T(8,128)(2,1)} %bitcast.136) | data formatting | bytes 12582912 | tf_op jit(solution)/shard_map/convert_element_type | solution.py:913
  404.1 8.4 %bitcast_convert_fusion.3 = bf16[1024,768]{1,0:T(8,128)(2,1)} fusion(bf16[2,1024,768]{2,1,0:T(8,128)(2,1)S(1)} %copy-done.4, f32[2,1024,1024]{1,2,0:T(8,128)} %copy.42, f32[2,1024]{1,0:T(2,128)} %copy-done.24, f32[2,1024]{1,0:T(2,128)S(1)} %get-tuple-element.61, f32[2,1024]{1,0:T(2,128)} %rsqrt.31, f32[2,1024]{1,0:T(2,128)} %div.61), kind=kOutput, calls=%fused_computation.25 | convolution fusion | flops 3232497664 | bytes 13139968 | tf_op jit(solution)/shard_map/mrd,mre->de/dot_general | solution.py:858
  412.6 13.6 %bitcast_convert_fusion.1 = bf16[4096,1024]{1,0:T(8,128)(2,1)} fusion(bf16[2,256,1024]{2,1,0:T(8,128)(2,1)S(1)} %copy-done.42, f32[2,1024]{1,0:T(2,128)S(1)} %copy-done.32, f32[2,256,4096]{2,1,0:T(8,128)} %fusion.29, f32[4096]{0:T(1024)S(1)} %copy-done.26), kind=kOutput, calls=%fused_computation.1 | convolution fusion | flops 4321705984 | bytes 17850368 | tf_op jit(solution)/shard_map/mrd,mre->de/dot_general | solution.py:858
  426.2 7.5 %bitcast_convert_fusion = bf16[1024,4096]{1,0:T(8,128)(2,1)} fusion(bf16[2,256,4096]{2,1,0:T(8,128)(2,1)S(1)} %copy-done.44, f32[2,256,1024]{2,1,0:T(8,128)S(1)} %copy-done.16, f32[2,1024]{1,0:T(2,128)S(1)} %copy-done.28, f32[2,1024]{1,0:T(2,128)S(1)} %copy-done.30, f32[2,256]{1,0:T(2,128)S(1)} %copy-done.40, f32[2,256]{1,0:T(2,128)S(1)} %copy-done.34), kind=kOutput, calls=%fused_computation | convolution fusion | flops 4301783040 | bytes 14700544 | tf_op jit(solution)/shard_map/mrd,mre->de/dot_general | solution.py:858
  433.7 2.6 bitcast_convert_fusion.2
  436.4 130.1 %weight_sums.1 = (f32[2,2,32,768]{3,2,1,0:T(8,128)}, f32[128,1024]{1,0:T(8,128)}, f32[32,4096]{1,0:T(8,128)}, f32[32,1024]{1,0:T(8,128)}) custom-call(bf16[4,2,2,2,32,768]{5,4,3,2,1,0:T(8,128)(2,1)} %bitcast.156, bf16[4,2,2,2,128,1024]{5,4,3,2,1,0:T(8,128)(2,1)} %bitcast.147, bf16[4,2,2,2,32,4096]{5,4,3,2,1,0:T(8,128)(2,1)} %bitcast.148, ...), custom_call_target="tpu_custom_call" | custom-call | tf_op jit(solution)/shard_map/weight_sums/pallas_call | solution.py:824
  (184 shorter events, 35.2 us)
Async XLA Ops:
  0.6 21.5 %copy-start.21 = (bf16[196608]{0:T(1024)(128)(2,1)S(1)}, bf16[196608]{0:T(1024)(128)(2,1)}, u32[]{:S(2)}) copy-start(bf16[196608]{0:T(1024)(128)(2,1)} %param.15) | copy-start | bytes 1179652
  17.7 202.6 %copy-start.37 = (f32[1024]{0:T(1024)}, f32[1024]{0:T(1024)S(1)}, u32[]{:S(2)}) copy-start(f32[1024]{0:T(1024)S(1)} %get-tuple-element.54) | copy-start | bytes 12292
  164.4 10.5 %copy-start.24 = (f32[2,1024]{1,0:T(2,128)}, f32[2,1024]{1,0:T(2,128)S(1)}, u32[]{:S(2)}) copy-start(f32[2,1024]{1,0:T(2,128)S(1)} %get-tuple-element.60) | copy-start | bytes 24580
  164.5 57.9 %copy-start.27 = (f32[2,1024]{1,0:T(2,128)}, f32[2,1024]{1,0:T(2,128)S(1)}, u32[]{:S(2)}) copy-start(f32[2,1024]{1,0:T(2,128)S(1)} %get-tuple-element.58) | copy-start | bytes 24580
  164.5 91.1 %copy-start.29 = (f32[2,1024]{1,0:T(2,128)}, f32[2,1024]{1,0:T(2,128)S(1)}, u32[]{:S(2)}) copy-start(f32[2,1024]{1,0:T(2,128)S(1)} %get-tuple-element.59) | copy-start | bytes 24580
  164.5 91.1 %copy-start.31 = (f32[2,1024]{1,0:T(2,128)}, f32[2,1024]{1,0:T(2,128)S(1)}, u32[]{:S(2)}) copy-start(f32[2,1024]{1,0:T(2,128)S(1)} %get-tuple-element.57) | copy-start | bytes 24580
  175.0 47.0 %copy-start.5 = (bf16[2,1024,768]{2,1,0:T(8,128)(2,1)}, bf16[2,1024,768]{2,1,0:T(8,128)(2,1)S(1)}, u32[]{:S(2)}) copy-start(bf16[2,1024,768]{2,1,0:T(8,128)(2,1)S(1)} %add_convert_fusion.2.qkv_ref) | copy-start | bytes 9437188
  175.0 45.4 %copy-start.9 = (bf16[4,2,2,2,32,1024]{5,4,3,2,1,0:T(8,128)(2,1)S(1)}, bf16[4,2,2,2,32,1024]{5,4,3,2,1,0:T(8,128)(2,1)}, u32[]{:S(2)}) copy-start(bf16[4,2,2,2,32,1024]{5,4,3,2,1,0:T(8,128)(2,1)} %copy-done.8) | copy-start | bytes 6291460
  222.0 33.7 %copy-start.15 = (f32[2,256,1024]{2,1,0:T(8,128)}, f32[2,256,1024]{2,1,0:T(8,128)S(1)}, u32[]{:S(2)}) copy-start(f32[2,256,1024]{2,1,0:T(8,128)S(1)} %get-tuple-element.48) | copy-start | bytes 6291460
  222.0 33.6 %copy-start.33 = (f32[2,256]{1,0:T(2,128)}, f32[2,256]{1,0:T(2,128)S(1)}, u32[]{:S(2)}) copy-start(f32[2,256]{1,0:T(2,128)S(1)} %get-tuple-element.68) | copy-start | bytes 6148
  222.4 33.3 %copy-start.39 = (f32[2,256]{1,0:T(2,128)}, f32[2,256]{1,0:T(2,128)S(1)}, u32[]{:S(2)}) copy-start(f32[2,256]{1,0:T(2,128)S(1)} %add_rsqrt_fusion.2) | copy-start | bytes 6148
  222.4 10.6 %copy-start.41 = (bf16[2,256,1024]{2,1,0:T(8,128)(2,1)S(1)}, bf16[2,256,1024]{2,1,0:T(8,128)(2,1)}, u32[]{:S(2)}) copy-start(bf16[2,256,1024]{2,1,0:T(8,128)(2,1)} %param.17) | copy-start | bytes 3145732
  233.0 22.7 %copy-start.25 = (f32[4096]{0:T(1024)}, f32[4096]{0:T(1024)S(1)}, u32[]{:S(2)}) copy-start(f32[4096]{0:T(1024)S(1)} %slice.88) | copy-start | bytes 49156
  246.5 9.2 %copy-start.36 = (f32[1024]{0:T(1024)S(1)}, f32[1024]{0:T(1024)}, u32[]{:S(2)}) copy-start(f32[1024]{0:T(1024)} %get-tuple-element.53) | copy-start | bytes 12292
  246.5 9.2 %copy-start.38 = (f32[1024]{0:T(1024)S(1)}, f32[1024]{0:T(1024)}, u32[]{:S(2)}) copy-start(f32[1024]{0:T(1024)} %copy-done.37) | copy-start | bytes 12292
  318.8 35.1 %copy-start.3 = (bf16[2,1024,768]{2,1,0:T(8,128)(2,1)}, bf16[2,1024,768]{2,1,0:T(8,128)(2,1)S(1)}, u32[]{:S(2)}) copy-start(bf16[2,1024,768]{2,1,0:T(8,128)(2,1)S(1)} %attention_back.1) | copy-start | bytes 9437188
  379.3 15.1 %copy-start.35 = (bf16[2,256]{1,0:T(2,128)(2,1)S(1)}, bf16[2,256]{1,0:T(2,128)(2,1)}, u32[]{:S(2)}) copy-start(bf16[2,256]{1,0:T(2,128)(2,1)} %param.10) | copy-start | bytes 3076
  379.5 15.4 %copy-start.14 = (f32[8,4,5120]{2,1,0:T(4,128)}, f32[8,4,5120]{2,1,0:T(4,128)S(1)}, u32[]{:S(2)}) copy-start(f32[8,4,5120]{2,1,0:T(4,128)S(1)} %reshape.277) | copy-start | bytes 1966084
  412.5 13.6 %copy-start.16 = (f32[2,256,1024]{2,1,0:T(8,128)S(1)}, f32[2,256,1024]{2,1,0:T(8,128)}, u32[]{:S(2)}) copy-start(f32[2,256,1024]{2,1,0:T(8,128)} %copy-done.15) | copy-start | bytes 6291460
  412.5 13.6 %copy-start.28 = (f32[2,1024]{1,0:T(2,128)S(1)}, f32[2,1024]{1,0:T(2,128)}, u32[]{:S(2)}) copy-start(f32[2,1024]{1,0:T(2,128)} %copy-done.27) | copy-start | bytes 24580
  412.5 13.6 %copy-start.30 = (f32[2,1024]{1,0:T(2,128)S(1)}, f32[2,1024]{1,0:T(2,128)}, u32[]{:S(2)}) copy-start(f32[2,1024]{1,0:T(2,128)} %copy-done.29) | copy-start | bytes 24580
  412.6 13.6 %copy-start.34 = (f32[2,256]{1,0:T(2,128)S(1)}, f32[2,256]{1,0:T(2,128)}, u32[]{:S(2)}) copy-start(f32[2,256]{1,0:T(2,128)} %copy-done.33) | copy-start | bytes 6148
  412.6 13.6 %copy-start.40 = (f32[2,256]{1,0:T(2,128)S(1)}, f32[2,256]{1,0:T(2,128)}, u32[]{:S(2)}) copy-start(f32[2,256]{1,0:T(2,128)} %copy-done.39) | copy-start | bytes 6148
  412.6 13.6 %copy-start.44 = (bf16[2,256,4096]{2,1,0:T(8,128)(2,1)S(1)}, bf16[2,256,4096]{2,1,0:T(8,128)(2,1)}, u32[]{:S(2)}) copy-start(bf16[2,256,4096]{2,1,0:T(8,128)(2,1)} %copy-done.43) | copy-start | bytes 12582916
  (21 other events, 100.0 us)

commit v2 on v1

--- a/solution.py
+++ b/solution.py
@@ -62,6 +62,7 @@
         pl.semaphore_wait(barrier, len(partners))
 
     def send(self, source, target, device):
+        assert self.used < self.send_sem.shape[0]
         copy = pltpu.make_async_remote_copy(
             src_ref=source,
             dst_ref=target,
@@ -76,6 +77,7 @@
         return copy
 
     def local(self, source, target):
+        assert self.local_used < self.local_sem.shape[0]
         copy = pltpu.make_async_copy(source, target, self.local_sem.at[self.local_used])
         self.local_used += 1
         copy.start()
@@ -224,32 +226,27 @@
     arrived(late)
 
 
-def gather_body(
-    planes,
-    tokens,
-    attend,
-    project,
-    expand,
-    contract,
-    partial,
-    tokens_out,
-    attend_out,
-    project_out,
-    expand_out,
-    contract_out,
-    modulation_out,
-    send_sem,
-    recv_sem,
-    local_sem,
-    attend_held,
-    sum_core,
-    sum_beside,
-    sum_across,
-    sum_planes,
-    total,
-):
+def gather_body(planes, fused, *refs):
+    tokens, attend, project, expand, contract, partial = refs[:6]
+    refs = refs[6:]
+    if fused:
+        shift_ref, bias_ref = refs[:2]
+        refs = refs[2:]
+    attend_out, project_out, expand_out, contract_out, modulation_out = refs[:5]
+    refs = refs[5:]
+    if fused:
+        first_out, qkv_out, heads_out, log_out, blended_out = refs[:5]
+        refs = refs[5:]
+    else:
+        tokens_out = refs[0]
+        refs = refs[1:]
+    send_sem, recv_sem, local_sem, attend_held = refs[:4]
+    sum_core, sum_beside, sum_across, sum_planes, total = refs[4:9]
+    if fused:
+        tokens_out = refs[9]
     links = Links(planes, send_sem, recv_sem, local_sem)
-    links.greet(links.partners())
+    corner = links.beside + 1 - 2 * links.c
+    links.greet(links.partners() + ([corner] if fused else []))
     z, y, x, c = links.z, links.y, links.x, links.c
 
     weights = [
@@ -322,71 +319,161 @@
     arrived([tokens_beside])
     fresh = tokens_out.at[:, 1 - x, c]
     tokens_late = links.send(fresh, fresh, links.core)
-
-    for _ in steps:
-        pass
-    arrived([step, tokens_core, tokens_late, *over_y])
-    own_tokens.wait()
+    if fused:
+        next(steps)
+        arrived([step, tokens_core, tokens_late, *over_y])
+        own_tokens.wait()
+        exchanged = []
+        own_heads = pl.ds(pl.multiple_of((2 * x + c) * OWN, OWN), OWN)
+        own_rows = tokens.shape[1]
+        for m in range(tokens.shape[0]):
+            project_tokens(
+                m, tokens_out, attend_out, modulation_out, shift_ref, bias_ref, first_out, qkv_out
+            )
+            next(steps, None)
+            for head in range(OWN // HEAD):
+                attention_unit(qkv_out.at[m], heads_out.at[m], log_out.at[m], head)
+                next(steps, None)
+            target = blended_out.at[m, :, own_heads]
+
+            def part_of(to_x, to_c, m=m):
+                start = pl.multiple_of((2 * to_x + to_c) * own_rows, own_rows)
+                return heads_out.at[m, pl.ds(start, own_rows)]
+
+            exchanged += [
+                links.send(part_of(1 - x, 1 - c), target, corner),
+                links.send(part_of(1 - x, c), target, links.beside),
+                links.send(part_of(x, 1 - c), target, links.core),
+            ]
+            own_part = links.local(part_of(x, c), target)
+            own_part.wait()
+        for _ in steps:
+            pass
+        arrived(exchanged)
+    else:
+        for _ in steps:
+            pass
+        arrived([step, tokens_core, tokens_late, *over_y])
+        own_tokens.wait()
     links.finish_sends()
 
 
-def gather_all(tokens, attend, project, expand, contract, partial, planes):
+def modulation_row(modulation, m, block):
+    per_quarter = modulation.shape[2] // MICROS
+    pieces = []
+    for k in range(block * D // LANES, (block + 1) * D // LANES):
+        quarter, row = k // per_quarter, m * per_quarter + k % per_quarter
+        pieces.append(modulation[quarter // 2, quarter % 2, row : row + 1, :])
+    return jnp.concatenate(pieces, axis=1)
+
+
+def project_tokens(m, tokens, attend, modulation, shift, bias, first_out, qkv_out):
+    offsets = modulation_row(modulation, m, 0) + shift[0:1, :]
+    factors = 1.0 + modulation_row(modulation, m, 1) + shift[1:2, :]
+    rows = tokens.shape[3]
+
+    @pl.loop(0, GROUP)
+    def _(block):
+        values = tokens[m, block // 2, block % 2].astype(jnp.float32)
+        normed, _ = normalize(values)
+        first = (normed * factors + offsets).astype(jnp.bfloat16)
+        here = pl.ds(pl.multiple_of(block * rows, rows), rows)
+        first_out[m, here, :] = first
+        weights = attend[...].reshape(D, 3 * OWN)
+        product = jnp.dot(first, weights, preferred_element_type=jnp.float32)
+        qkv_out[m, here, :] = (product + bias[...]).astype(jnp.bfloat16)
+
+
+def gather_all(tokens, attend, project, expand, contract, partial, planes, shift=None, bias=None):
     grid = (planes, 2, 2, 2)
     rows = partial.shape[-2]
+    micros, own_rows, _ = tokens.shape
+    latent_rows = own_rows * GROUP
+    fused = shift is not None
 
     def full(shard):
         return jax.ShapeDtypeStruct((*grid, *shard.shape[-2:]), shard.dtype)
 
+    def low(*shape):
+        return jax.ShapeDtypeStruct(shape, jnp.bfloat16)
+
+    outs = [
+        full(attend),
+        full(project),
+        full(expand),
+        full(contract),
+        jax.ShapeDtypeStruct((2, 2, rows, LANES), jnp.float32),
+    ]
+    tokens_shape = (micros, 2, 2, own_rows, D)
+    scratch = [
+        pltpu.VMEM((attend.shape[-2], attend.shape[-1]), attend.dtype),
+        pltpu.VMEM((planes, 2, 2, rows, LANES), jnp.float32),
+        pltpu.VMEM((planes, 2, rows, LANES), jnp.float32),
+        pltpu.VMEM((planes, rows, LANES), jnp.float32),
+        pltpu.VMEM((planes - 1, rows, LANES), jnp.float32),
+        pltpu.VMEM((rows, LANES), jnp.float32),
+    ]
+    in_specs = [ANY] * 5 + [VMEM]
+    sems = 32 + 13 * (planes - 1) + 10 * 5
+    args = (tokens, attend, project, expand, contract, partial)
+    if fused:
+        blocks = latent_rows // QUERY_ROWS
+        outs += [
+            low(micros, latent_rows, D),
+            low(micros, latent_rows, 3 * OWN),
+            low(micros, latent_rows, OWN),
+            jax.ShapeDtypeStruct((micros, OWN // HEAD, blocks, 1, QUERY_ROWS), jnp.float32),
+            low(micros, own_rows, D),
+        ]
+        in_specs += [VMEM] * 2
+        out_specs = [VMEM] + [ANY] * 3 + [VMEM] * 6
+        scratch.append(pltpu.VMEM(tokens_shape, tokens.dtype))
+        args += (shift, bias)
+    else:
+        outs.append(low(*tokens_shape))
+        out_specs = [ANY] * 4 + [VMEM, ANY]
     return remote_call(
-        functools.partial(gather_body, planes),
+        functools.partial(gather_body, planes, fused),
         "gather_all",
         1,
-        (
-            jax.ShapeDtypeStruct((tokens.shape[0], 2, 2, *tokens.shape[1:]), tokens.dtype),
-            full(attend),
-            full(project),
-            full(expand),
-            full(contract),
-            jax.ShapeDtypeStruct((2, 2, rows, LANES), jnp.float32),
-        ),
-        [ANY] * 5 + [VMEM],
-        (ANY,) * 5 + (VMEM,),
-        [
-            pltpu.VMEM((attend.shape[-2], attend.shape[-1]), attend.dtype),
-            pltpu.VMEM((planes, 2, 2, rows, LANES), jnp.float32),
-            pltpu.VMEM((planes, 2, rows, LANES), jnp.float32),
-            pltpu.VMEM((planes, rows, LANES), jnp.float32),
-            pltpu.VMEM((planes - 1, rows, LANES), jnp.float32),
-            pltpu.VMEM((rows, LANES), jnp.float32),
-        ],
-        20 + 13 * (planes - 1) + 10 * 5,
+        tuple(outs),
+        in_specs,
+        tuple(out_specs),
+        scratch,
+        sems,
         8,
-        40 * MIB,
-    )(tokens, attend, project, expand, contract, partial)
+        56 * MIB,
+    )(*args)
+
+
+QUERY_ROWS = 256
+
+
+def attention_unit(qkv, out, log, head):
+    at = head * HEAD
+    keys = qkv[:, OWN + at : OWN + at + HEAD]
+    values_t = qkv[:, 2 * OWN + at : 2 * OWN + at + HEAD].T
+
+    @pl.loop(0, qkv.shape[0] // QUERY_ROWS)
+    def _(block):
+        here = pl.ds(pl.multiple_of(block * QUERY_ROWS, QUERY_ROWS), QUERY_ROWS)
+        queries = qkv[here, at : at + HEAD] * SCALE
+        scores = lax.dot_general(
+            keys, queries, (((1,), (1,)), ((), ())), preferred_element_type=jnp.float32
+        )
+        top = jnp.max(scores, axis=0, keepdims=True)
+        weights = jnp.exp(scores - top)
+        totals = jnp.sum(weights, axis=0, keepdims=True)
+        blended = jnp.dot(
+            values_t, weights.astype(jnp.bfloat16), preferred_element_type=jnp.float32
+        )
+        out[here, at : at + HEAD] = (blended / totals).T.astype(jnp.bfloat16)
+        log[head, block] = top + jnp.log(totals)
 
 
 def attention_body(qkv_ref, out_ref, log_ref):
-    rows = 256
     for head in range(OWN // HEAD):
-        at = head * HEAD
-        keys = qkv_ref[0, :, OWN + at : OWN + at + HEAD]
-        values_t = qkv_ref[0, :, 2 * OWN + at : 2 * OWN + at + HEAD].T
-
-        @pl.loop(0, qkv_ref.shape[1] // rows)
-        def _(block):
-            here = pl.ds(pl.multiple_of(block * rows, rows), rows)
-            queries = qkv_ref[0, here, at : at + HEAD] * SCALE
-            scores = lax.dot_general(
-                keys, queries, (((1,), (1,)), ((), ())), preferred_element_type=jnp.float32
-            )
-            top = jnp.max(scores, axis=0, keepdims=True)
-            weights = jnp.exp(scores - top)
-            totals = jnp.sum(weights, axis=0, keepdims=True)
-            blended = jnp.dot(
-                values_t, weights.astype(jnp.bfloat16), preferred_element_type=jnp.float32
-            )
-            out_ref[0, here, at : at + HEAD] = (blended / totals).T.astype(jnp.bfloat16)
-            log_ref[0, head, block] = top + jnp.log(totals)
+        attention_unit(qkv_ref.at[0], out_ref.at[0], log_ref.at[0], head)
 
 
 def attention(qkv):
@@ -410,42 +497,54 @@
     )(qkv)
 
 
+def attention_back_unit(qkv, blended_all, grad_all, log, out, key_sum, value_sum, head):
+    at = head * HEAD
+    keys = qkv[:, OWN + at : OWN + at + HEAD]
+    keys_t = keys.T
+    values = qkv[:, 2 * OWN + at : 2 * OWN + at + HEAD]
+    key_sum[...] = jnp.zeros_like(key_sum)
+    value_sum[...] = jnp.zeros_like(value_sum)
+
+    @pl.loop(0, qkv.shape[0] // QUERY_ROWS)
+    def _(block):
+        here = pl.ds(pl.multiple_of(block * QUERY_ROWS, QUERY_ROWS), QUERY_ROWS)
+        queries = qkv[here, at : at + HEAD] * SCALE
+        grads = grad_all[here, at : at + HEAD]
+        blended = blended_all[here, at : at + HEAD]
+        row_terms = jnp.sum(
+            (grads.astype(jnp.float32) * blended.astype(jnp.float32)).T, axis=0, keepdims=True
+        )
+        scores = lax.dot_general(
+            keys, queries, (((1,), (1,)), ((), ())), preferred_element_type=jnp.float32
+        )
+        chances = jnp.exp(scores - log[head, block])
+        grad_chances = lax.dot_general(
+            values, grads, (((1,), (1,)), ((), ())), preferred_element_type=jnp.float32
+        )
+        grad_scores = (chances * (grad_chances - row_terms)).astype(jnp.bfloat16)
+        value_sum[...] += jnp.dot(
+            chances.astype(jnp.bfloat16), grads, preferred_element_type=jnp.float32
+        )
+        key_sum[...] += jnp.dot(grad_scores, queries, preferred_element_type=jnp.float32)
+        grad_queries = jnp.dot(keys_t, grad_scores, preferred_element_type=jnp.float32)
+        out[here, at : at + HEAD] = (grad_queries.T * SCALE).astype(jnp.bfloat16)
+
+    out[:, OWN + at : OWN + at + HEAD] = key_sum[...].astype(jnp.bfloat16)
+    out[:, 2 * OWN + at : 2 * OWN + at + HEAD] = value_sum[...].astype(jnp.bfloat16)
+
+
 def attention_back_body(qkv_ref, blended_ref, grad_ref, log_ref, out_ref, key_sum, value_sum):
-    rows = 256
     for head in range(OWN // HEAD):
-        at = head * HEAD
-        keys = qkv_ref[0, :, OWN + at : OWN + at + HEAD]
-        keys_t = keys.T
-        values = qkv_ref[0, :, 2 * OWN + at : 2 * OWN + at + HEAD]
-        key_sum[...] = jnp.zeros_like(key_sum)
-        value_sum[...] = jnp.zeros_like(value_sum)
-
-        @pl.loop(0, qkv_ref.shape[1] // rows)
-        def _(block):
-            here = pl.ds(pl.multiple_of(block * rows, rows), rows)
-            queries = qkv_ref[0, here, at : at + HEAD] * SCALE
-            grads = grad_ref[0, here, at : at + HEAD]
-            blended = blended_ref[0, here, at : at + HEAD]
-            row_terms = jnp.sum(
-                (grads.astype(jnp.float32) * blended.astype(jnp.float32)).T, axis=0, keepdims=True
-            )
-            scores = lax.dot_general(
-                keys, queries, (((1,), (1,)), ((), ())), preferred_element_type=jnp.float32
-            )
-            chances = jnp.exp(scores - log_ref[0, head, block])
-            grad_chances = lax.dot_general(
-                values, grads, (((1,), (1,)), ((), ())), preferred_element_type=jnp.float32
-            )
-            grad_scores = (chances * (grad_chances - row_terms)).astype(jnp.bfloat16)
-            value_sum[...] += jnp.dot(
-                chances.astype(jnp.bfloat16), grads, preferred_element_type=jnp.float32
-            )
-            key_sum[...] += jnp.dot(grad_scores, queries, preferred_element_type=jnp.float32)
-            grad_queries = jnp.dot(keys_t, grad_scores, preferred_element_type=jnp.float32)
-            out_ref[0, here, at : at + HEAD] = (grad_queries.T * SCALE).astype(jnp.bfloat16)
-
-        out_ref[0, :, OWN + at : OWN + at + HEAD] = key_sum[...].astype(jnp.bfloat16)
-        out_ref[0, :, 2 * OWN + at : 2 * OWN + at + HEAD] = value_sum[...].astype(jnp.bfloat16)
+        attention_back_unit(
+            qkv_ref.at[0],
+            blended_ref.at[0],
+            grad_ref.at[0],
+            log_ref.at[0],
+            out_ref.at[0],
+            key_sum,
+            value_sum,
+            head,
+        )
 
 
 def attention_back(qkv, blended, grads, logs):
@@ -741,76 +840,241 @@
         yield
 
 
-def sums_body(planes, plan, attend, *refs):
-    links_sems, scratch = refs[2 * len(plan) + 1 :][:3], refs[2 * len(plan) + 4 :]
+class AttendSums:
+    def __init__(self, links, grads, out, scratch):
+        self.links, self.grads, self.out = links, grads, out
+        self.own, self.over_y, self.over_planes, self.sum, self.held = scratch
+
+    def start(self):
+        links = self.links
+        self.step = links.send(self.grads.at[:, 1 - links.y], self.over_y, links.across)
+        self.loaded = links.local(self.grads.at[:, links.y], self.own)
+
+    def planes(self):
+        links, own, over_y = self.links, self.own, self.over_y
+        self.loaded.wait()
+        arrived([self.step])
+        for i in range(2):
+
+            def block(ref, i=i):
+                return lambda k: ref.at[k // 2, i, k % 2]
+
+            add_blocks(block(own), block(own), block(over_y), links.planes * 2)
+        self.step = [
+            links.send(own.at[links.plane(s)], self.over_planes.at[s - 1], links.plane_device(s))
+            for s in range(1, links.planes)
+        ]
+
+    def owners(self):
+        links = self.links
+        x, c = links.x, links.c
+        arrived(self.step)
+        for i in range(2):
+            for j in range(2):
+                result = self.own[links.z, i, j].astype(jnp.float32)
+                for s in range(1, links.planes):
+                    result = result + self.over_planes[s - 1, i, j].astype(jnp.float32)
+                self.sum[i, j] = result
+        self.beside = links.send(self.sum.at[1 - x], self.held, links.beside)
+        self.near = links.send(self.sum.at[x, 1 - c], self.out.at[x, c], links.core)
+        self.out[x, c] = self.sum[x, c]
+
+    def last(self):
+        links = self.links
+        x, c = links.x, links.c
+        arrived([self.beside])
+        self.out[1 - x, c] = self.held[c]
+        self.far = links.send(self.held.at[1 - c], self.out.at[1 - x, c], links.core)
+
+    def finish(self):
+        arrived([self.near, self.far])
+
+
+class TokenSums:
+    def __init__(self, links, partial, out, scratch):
+        self.links, self.partial, self.out = links, partial, out
+        self.from_core, self.from_beside = scratch
+        self.state = {}
+
+    def start(self, m):
+        links, partial = self.links, self.partial
+        x, c = links.x, links.c
+        self.state[m] = [
+            links.send(partial.at[m, 1 - x, 1 - c], self.from_core.at[0, m], links.core),
+            links.send(partial.at[m, x, 1 - c], self.from_core.at[1, m], links.core),
+        ]
+
+    def middle(self, m):
+        links, partial = self.links, self.partial
+        x, c = links.x, links.c
+        arrived(self.state[m])
+        away = partial.at[m, 1 - x, c]
+        away[...] = (
+            away[...].astype(jnp.float32) + self.from_core[0, m].astype(jnp.float32)
+        ).astype(jnp.bfloat16)
+        self.state[m] = [links.send(away, self.from_beside.at[m], links.beside)]
+
+    def finish(self, m):
+        links = self.links
+        arrived(self.state[m])
+        self.out[m] = (
+            self.partial[m, links.x, links.c].astype(jnp.float32)
+            + self.from_core[1, m].astype(jnp.float32)
+            + self.from_beside[m].astype(jnp.float32)
+        )
+
+
+def sums_body(planes, plan, *refs):
+    attend, refs = refs[0], refs[1:]
     grads, attend_out, outs = refs[: len(plan)], refs[len(plan)], refs[len(plan) + 1 :][: len(plan)]
-    links = Links(planes, *links_sems)
+    refs = refs[2 * len(plan) + 1 :]
+    links = Links(planes, *refs[:3])
     links.greet(links.partners())
-    z, y, x, c = links.z, links.y, links.x, links.c
-    attend_own, attend_across, attend_planes, attend_sum, attend_held = scratch[:5]
-    scratch = scratch[5:]
+    attend_sums = AttendSums(links, attend, attend_out, refs[3:8])
+    attend_sums.start()
+    steps = sum_steps(sum_pieces(links, plan, grads, outs, refs[8:]))
+    next(steps)
+    next(steps)
+    attend_sums.planes()
+    next(steps)
+    next(steps)
+    attend_sums.owners()
+    next(steps)
+    next(steps)
+    attend_sums.last()
+    for _ in steps:
+        pass
+    attend_sums.finish()
+    links.finish_sends()
+
+
+def sum_pieces(links, plan, grads, outs, scratch):
     pieces = []
-    used = 0
     for parts, grad, out in zip(plan, grads, outs):
         width = grad.shape[-1] // parts
         for part in range(parts):
-            pieces.append(
-                SumPiece(links, grad, out, pl.ds(part * width, width), part, scratch[used : used + 5])
+            columns = pl.ds(part * width, width)
+            used = 5 * len(pieces)
+            pieces.append(SumPiece(links, grad, out, columns, part, scratch[used : used + 5]))
+    return pieces
+
+
+def advance(steps, count):
+    for _ in range(count):
+        next(steps, None)
+
+
+def back_body(planes, plan, *refs):
+    kinds = len(plan)
+    grads, refs = refs[:kinds], refs[kinds:]
+    grad_blended, qkv, heads, logs, first, attend, refs = *refs[:6], refs[6:]
+    attend_out, outs, refs = refs[0], refs[1 : 1 + kinds], refs[1 + kinds :]
+    first_out, bias_out, refs = refs[0], refs[1], refs[2:]
+    links = Links(planes, *refs[:3])
+    refs = refs[3:]
+    attend_scratch, refs = refs[:5], refs[5:]
+    piece_scratch, refs = refs[: 5 * sum(plan)], refs[5 * sum(plan) :]
+    grad_heads, grad_qkv, key_sum, value_sum, attend_grads, partial, *token_scratch = refs
+    x, c = links.x, links.c
+    corner = links.beside + 1 - 2 * c
+    links.greet([*links.partners(), corner])
+    micros, latent_rows, _ = qkv.shape
+    own_rows = latent_rows // GROUP
+
+    here = pl.ds(pl.multiple_of((2 * x + c) * own_rows, own_rows), own_rows)
+    exchanged = []
+    for m in range(micros):
+
+        def columns(to_x, to_c, m=m):
+            return grad_blended.at[m, :, pl.ds(pl.multiple_of((2 * to_x + to_c) * OWN, OWN), OWN)]
+
+        target = grad_heads.at[m, here]
+        copies = [
+            links.send(columns(1 - x, 1 - c), target, corner),
+            links.send(columns(1 - x, c), target, links.beside),
+            links.send(columns(x, 1 - c), target, links.core),
+        ]
+        exchanged.append((copies, links.local(columns(x, c), target)))
+
+    steps = sum_steps(sum_pieces(links, plan, grads, outs, piece_scratch))
+    attend_sums = AttendSums(links, attend_grads, attend_out, attend_scratch)
+    token_sum = TokenSums(links, partial, first_out, token_scratch)
+    advance(steps, 3)
+    for m in range(micros):
+        copies, own = exchanged[m]
+        arrived(copies)
+        own.wait()
+        for head in range(OWN // HEAD):
+            attention_back_unit(
+                qkv.at[m],
+                heads.at[m],
+                grad_heads.at[m],
+                logs.at[m],
+                grad_qkv.at[m],
+                key_sum,
+                value_sum,
+                head,
             )
-            used += 5
-
-    step = links.send(attend.at[:, 1 - y], attend_across, links.across)
-    loaded = links.local(attend.at[:, y], attend_own)
-    steps = sum_steps(pieces)
-    next(steps)
-    next(steps)
-    loaded.wait()
-    arrived([step])
-    for i in range(2):
-
-        def block(ref):
-            return lambda k: ref.at[k // 2, i, k % 2]
-
-        add_blocks(block(attend_own), block(attend_own), block(attend_across), planes * 2)
-    over = [
-        links.send(attend_own.at[links.plane(s)], attend_planes.at[s - 1], links.plane_device(s))
-        for s in range(1, planes)
-    ]
-    next(steps)
-    next(steps)
-    arrived(over)
-    for i in range(2):
-        for j in range(2):
-            result = attend_own[z, i, j].astype(jnp.float32)
-            for s in range(1, planes):
-                result = result + attend_planes[s - 1, i, j].astype(jnp.float32)
-            attend_sum[i, j] = result
-    beside = links.send(attend_sum.at[1 - x], attend_held, links.beside)
-    near = links.send(attend_sum.at[x, 1 - c], attend_out.at[x, c], links.core)
-    attend_out[x, c] = attend_sum[x, c]
-    next(steps)
-    next(steps)
-    arrived([beside])
-    attend_out[1 - x, c] = attend_held[c]
-    far = links.send(attend_held.at[1 - c], attend_out.at[1 - x, c], links.core)
+            advance(steps, 2)
+        if m == micros - 1:
+            attend_product(first, grad_qkv, attend_grads, planes)
+            attend_sums.start()
+            advance(steps, 1)
+        first_product(m, grad_qkv, attend, partial)
+        token_sum.start(m)
+        advance(steps, 1)
+        token_sum.middle(m)
+    attend_sums.planes()
+    total = jnp.zeros((1, grad_qkv.shape[-1]), jnp.float32)
+    for m in range(micros):
+        total = total + jnp.sum(grad_qkv[m].astype(jnp.float32), axis=0, keepdims=True)
+    bias_out[...] = total
+    advance(steps, 2)
+    for m in range(micros):
+        token_sum.finish(m)
+    attend_sums.owners()
+    advance(steps, 2)
+    attend_sums.last()
     for _ in steps:
         pass
-    arrived([near, far])
+    attend_sums.finish()
     links.finish_sends()
 
 
-def weight_sums(attend, weights, plan, planes):
-    def piece_scratch(grad, parts):
-        rows, width = grad.shape[-2], grad.shape[-1] // parts
-        return [
-            pltpu.VMEM((planes, 2, 2, rows, width), jnp.bfloat16),
-            pltpu.VMEM((planes, 2, 2, rows, width), jnp.bfloat16),
-            pltpu.VMEM((planes, 2, rows, width), jnp.bfloat16),
-            pltpu.VMEM((planes, rows, width), jnp.bfloat16),
-            pltpu.VMEM((planes - 1, rows, width), jnp.bfloat16),
-        ]
-
-    rows, width = attend.shape[-2:]
+def attend_product(first, grad_qkv, out, planes):
+    width = D // planes
+
+    @pl.loop(0, planes)
+    def _(plane):
+        columns = pl.ds(pl.multiple_of(plane * width, width), width)
+        total = None
+        for m in range(first.shape[0]):
+            product = lax.dot_general(
+                first[m, :, columns],
+                grad_qkv[m],
+                (((0,), (0,)), ((), ())),
+                preferred_element_type=jnp.float32,
+            )
+            total = product if total is None else total + product
+        out[plane] = total.astype(jnp.bfloat16).reshape(out.shape[1:])
+
+
+def first_product(m, grad_qkv, attend, partial):
+    rows = partial.shape[3]
+
+    @pl.loop(0, GROUP)
+    def _(block):
+        here = pl.ds(pl.multiple_of(block * rows, rows), rows)
+        product = lax.dot_general(
+            grad_qkv[m, here, :],
+            attend[...].reshape(D, 3 * OWN),
+            (((1,), (1,)), ((), ())),
+            preferred_element_type=jnp.float32,
+        )
+        partial[m, block // 2, block % 2] = product.astype(jnp.bfloat16)
+
+
+def sums_scratch(rows, width, weights, plan, planes):
     scratch = [
         pltpu.VMEM((planes, 2, 2, rows, width), jnp.bfloat16),
         pltpu.VMEM((planes, 2, 2, rows, width), jnp.bfloat16),
@@ -819,23 +1083,75 @@
         pltpu.VMEM((2, rows, width), jnp.float32),
     ]
     for grad, parts in zip(weights, plan):
+        rows, width = grad.shape[-2], grad.shape[-1] // parts
         for _ in range(parts):
-            scratch += piece_scratch(grad, parts)
+            scratch += [
+                pltpu.VMEM((planes, 2, 2, rows, width), jnp.bfloat16),
+                pltpu.VMEM((planes, 2, 2, rows, width), jnp.bfloat16),
+                pltpu.VMEM((planes, 2, rows, width), jnp.bfloat16),
+                pltpu.VMEM((planes, rows, width), jnp.bfloat16),
+                pltpu.VMEM((planes - 1, rows, width), jnp.bfloat16),
+            ]
+    return scratch
+
+
+def sums_outs(rows, width, weights):
+    return (
+        jax.ShapeDtypeStruct((2, 2, rows, width), jnp.float32),
+        *(jax.ShapeDtypeStruct(grad.shape[-2:], jnp.float32) for grad in weights),
+    )
+
+
+def weight_sums(attend, weights, plan, planes):
+    rows, width = attend.shape[-2:]
     return remote_call(
         functools.partial(sums_body, planes, plan),
         "weight_sums",
         6,
-        (
-            jax.ShapeDtypeStruct((2, 2, rows, width), jnp.float32),
-            *(jax.ShapeDtypeStruct(grad.shape[-2:], jnp.float32) for grad in weights),
-        ),
+        sums_outs(rows, width, weights),
         [ANY] * (1 + len(weights)),
         (VMEM,) * (1 + len(weights)),
-        scratch,
+        sums_scratch(rows, width, weights, plan, planes),
         8 + planes + sum(plan) * (2 + planes),
         2 + sum(plan),
         60 * MIB,
     )(attend, *weights)
+
+
+def back_and_sums(weights, grad_blended, qkv, heads, logs, first, attend, plan, planes):
+    rows, width = attend.shape[-2:]
+    micros, own_rows, _ = grad_blended.shape
+    latent_rows = own_rows * GROUP
+
+    def low(*shape):
+        return pltpu.VMEM(shape, jnp.bfloat16)
+
+    return remote_call(
+        functools.partial(back_body, planes, plan),
+        "back_and_sums",
+        6,
+        (
+            *sums_outs(rows, width, weights),
+            jax.ShapeDtypeStruct((micros, own_rows, D), jnp.float32),
+            jax.ShapeDtypeStruct((1, width), jnp.float32),
+        ),
+        [ANY] * len(weights) + [VMEM] * 6,
+        (VMEM,) * (3 + len(weights)),
+        [
+            *sums_scratch(rows, width, weights, plan, planes),
+            low(micros, latent_rows, OWN),
+            low(micros, latent_rows, width),
+            pltpu.VMEM((latent_rows, HEAD), jnp.float32),
+            pltpu.VMEM((latent_rows, HEAD), jnp.float32),
+            low(*attend.shape),
+            low(micros, 2, 2, own_rows, D),
+            low(2, micros, own_rows, D),
+            low(micros, own_rows, D),
+        ],
+        24 + planes + sum(plan) * (2 + planes),
+        4 + sum(plan),
+        63 * MIB,
+    )(*weights, grad_blended, qkv, heads, logs, first, attend)
 
 
 def normalize(values):
@@ -890,7 +1206,16 @@
     partial = partial.reshape(planes, 2, 2, 2, -1, LANES)
 
     attend_shard = attend.reshape(rows, 3, 2, 2, OWN).transpose(2, 3, 0, 1, 4)
-    gathered = gather_all(
+    bias_row = jnp.concatenate(
+        [
+            lax.dynamic_slice_in_dim(bias_query, quarter * OWN, OWN),
+            jnp.zeros((OWN,), jnp.float32),
+            lax.dynamic_slice_in_dim(bias_value, quarter * OWN, OWN),
+        ]
+    )
+    fused = rows % 16 == 0 and own_rows % QUERY_ROWS == 0
+    extras = (bias_modulate.reshape(6, D)[:2], bias_row[None]) if fused else ()
+    attend_all, project_all, expand_all, contract_all, modulation_all, *rest = gather_all(
         tokens,
         attend_shard.reshape(2, 2, rows, 3 * OWN),
         project.reshape(rows, D),
@@ -898,30 +1223,27 @@
         contract.reshape(FF // devices, D),
         partial,
         planes,
-    )
-    tokens_latent = gathered[0].reshape(micros, latent_rows, D)
-    attend_own = gathered[1].reshape(D, 3 * OWN)
-    project_full = gathered[2].reshape(D, D)
-    expand_full = gathered[3].reshape(D, FF)
-    contract_full = gathered[4].reshape(FF, D)
-    modulation = gathered[5].reshape(GROUP, micros, -1).transpose(1, 0, 2)
+        *extras,
+    )
+    attend_own = attend_all.reshape(D, 3 * OWN)
+    project_full = project_all.reshape(D, D)
+    expand_full = expand_all.reshape(D, FF)
+    contract_full = contract_all.reshape(FF, D)
+    modulation = modulation_all.reshape(GROUP, micros, -1).transpose(1, 0, 2)
     modulation = modulation.reshape(micros, 6 * D) + bias_modulate
     offsets_one, factors_one, gates_one, offsets_two, factors_two, gates_two = (
         modulation[:, None, part * D : (part + 1) * D] for part in range(6)
     )
 
-    normed_latent, _ = normalize(tokens_latent.astype(jnp.float32))
-    first = (normed_latent * (1.0 + factors_one) + offsets_one).astype(jnp.bfloat16)
-    bias_row = jnp.concatenate(
-        [
-            lax.dynamic_slice_in_dim(bias_query, quarter * OWN, OWN),
-            jnp.zeros((OWN,), jnp.float32),
-            lax.dynamic_slice_in_dim(bias_value, quarter * OWN, OWN),
-        ]
-    )
-    projected = (einsum("mrd,de->mre", first, attend_own) + bias_row).astype(jnp.bfloat16)
-    blended_heads, logs = attention(projected)
-    blended = heads_to_tokens(blended_heads)
+    if fused:
+        first, projected, blended_heads, logs, blended = rest
+    else:
+        tokens_latent = rest[0].reshape(micros, latent_rows, D)
+        normed_latent, _ = normalize(tokens_latent.astype(jnp.float32))
+        first = (normed_latent * (1.0 + factors_one) + offsets_one).astype(jnp.bfloat16)
+        projected = (einsum("mrd,de->mre", first, attend_own) + bias_row).astype(jnp.bfloat16)
+        blended_heads, logs = attention(projected)
+        blended = heads_to_tokens(blended_heads)
 
     inputs = tokens.astype(jnp.float32)
     attended = einsum("mrd,de->mre", blended, project_full) + bias_project
@@ -947,12 +1269,28 @@
     grad_gates_one = jnp.sum(grad_middle * attended, axis=1)
     grad_project = einsum("mrd,mre->de", blended, grad_attended)
     grad_blended = einsum("mre,de->mrd", grad_attended, project_full).astype(jnp.bfloat16)
-    grad_heads = tokens_to_heads(grad_blended)
-    grad_projected = attention_back(projected, blended_heads, grad_heads, logs)
-    grad_attend = einsum("mrd,mre->de", first, grad_projected)
-    grad_first = token_sums(
-        einsum("mre,de->mrd", grad_projected, attend_own).astype(jnp.bfloat16)
-    )
+    weights = (
+        grad_contract.astype(jnp.bfloat16).reshape(*grid, FF // devices, D),
+        grad_expand.astype(jnp.bfloat16).reshape(*grid, rows, FF),
+        grad_project.astype(jnp.bfloat16).reshape(*grid, rows, D),
+    )
+    plan = (4, 4, 2)
+    if fused:
+        attend_sum, contract_sum, expand_sum, project_sum, grad_first, heads_sum = back_and_sums(
+            weights, grad_blended, projected, blended_heads, logs, first, attend_all, plan, planes
+        )
+        heads_sum = heads_sum[0]
+    else:
+        grad_heads = tokens_to_heads(grad_blended)
+        grad_projected = attention_back(projected, blended_heads, grad_heads, logs)
+        grad_attend = einsum("mrd,mre->de", first, grad_projected)
+        grad_first = token_sums(
+            einsum("mre,de->mrd", grad_projected, attend_own).astype(jnp.bfloat16)
+        )
+        heads_sum = jnp.sum(grad_projected, axis=(0, 1), dtype=jnp.float32)
+        attend_sum, contract_sum, expand_sum, project_sum = weight_sums(
+            grad_attend.astype(jnp.bfloat16).reshape(*grid, rows, 3 * OWN), weights, plan, planes
+        )
     normed_one, scale_one = normalize(inputs)
     grad_tokens = grad_middle + norm_back(grad_first, normed_one, scale_one, factors_one)
 
@@ -971,7 +1309,6 @@
     def token_sum(values):
         return jnp.sum(values, axis=(0, 1), dtype=jnp.float32)
 
-    heads_sum = token_sum(grad_projected)
     bias_terms = jnp.concatenate(
         [
             lax.dynamic_update_slice(
@@ -1026,14 +1363,6 @@
     gate = 1.0 / (1.0 + jnp.exp(-values))
     grad_condition = gate * (1.0 + values * (1.0 - gate)) * grad_silu
 
-    weights = (
-        grad_contract.astype(jnp.bfloat16).reshape(*grid, FF // devices, D),
-        grad_expand.astype(jnp.bfloat16).reshape(*grid, rows, FF),
-        grad_project.astype(jnp.bfloat16).reshape(*grid, rows, D),
-    )
-    attend_sum, contract_sum, expand_sum, project_sum = weight_sums(
-        grad_attend.astype(jnp.bfloat16).reshape(*grid, rows, 3 * OWN), weights, (4, 4, 2), planes
-    )
     attend_sum = attend_sum.reshape(2, 2, rows, 3, OWN).transpose(2, 3, 0, 1, 4)
     return (
         output,

time: 587 us -> 463 us (0.79); the launches traced: 577 us -> 460 us
  Pallas kernels: 441 us -> 357 us
  matrix products: 89.6 us -> 73.8 us
  local copies, waits for them, and re-layouts: 30.9 us -> 17.9 us
    pallas_call x7 -> x2, Pallas kernels: 389 us -> 304 us  [the longest x1 155 us: back_and_sums(): remote_call(functools.partial(back_body, planes, plan), 'back_and_sums',...]
    dot_general x12 -> x9, matrix products: 87.7 us -> 71.8 us  [einsum(): return jnp.einsum(spec, left, right, preferred_element_type=jnp.float32)]
    convert_element_type x1 -> x0, local copies, waits for them, and re-layouts: 7.23 us -> none  [per_device(): normed_latent, _ = normalize(tokens_latent.astype(jnp.float32))]
    unnamed x111 -> x65, local copies, waits for them, and re-layouts: 12.7 us -> 6.66 us
where the time goes in v2:
time: 463 us; the launch traced here: 460 us
  Pallas kernels  357 us (77%)
  matrix products  73.8 us (16%)
  local copies, waits for them, and re-layouts  17.9 us (4%)
  other arithmetic  9.74 us (2%)
    pallas_call x1, Pallas kernels, back_and_sums(): remote_call(functools.partial(back_body, planes, plan), 'back_and_sums',...  155 us
    pallas_call x1, Pallas kernels, gather_all(): remote_call(functools.partial(gather_body, planes, fused), 'gather_all',...  150 us
    dot_general x9, matrix products, einsum(): return jnp.einsum(spec, left, right, preferred_element_type=jnp.float32)  71.8 us
    pallas_call x2, Pallas kernels, small_gather(): remote_call(functools.partial(small_gather_body, planes), 'small_gather',...  27.4 us
    pallas_call x1, Pallas kernels, small_sums(): remote_call(functools.partial(small_sums_body, planes), 'small_sums', 5,...  25 us

profile of v2, /device:TPU:0, one launch (start us, length us, event | category | flops | bytes accessed | tf_op | source)
XLA Modules:
  0.0 460.0 jit_solution(4538731549683037999)
XLA Ops:
  2.1 14.9 %small_gather.2 = f32[4,2,2,2,8,128]{5,4,3,2,1,0:T(8,128)S(1)} custom-call(f32[8,128]{1,0:T(8,128)S(1)} %fusion.37.own_ref), custom_call_target="tpu_custom_call" | custom-call | tf_op jit(solution)/shard_map/small_gather/pallas_call | solution.py:142
  17.2 1.1 reshape.203
  18.3 0.9 reshape.204.refs_1_
  19.2 1.5 reshape.205.refs_2_
  23.3 1.1 reshape.215.refs_5_
  25.8 149.8 %gather_all.1 = (bf16[4,2,2,2,32,768]{5,4,3,2,1,0:T(8,128)(2,1)}, bf16[4,2,2,2,32,1024]{5,4,3,2,1,0:T(8,128)(2,1)}, bf16[4,2,2,2,32,4096]{5,4,3,2,1,0:T(8,128)(2...) custom-call(bf16[2,256,1024]{2,1,0:T(8,128)(2,1)} %refs_0_.1, ...), custom_call_target="tpu_custom_call" | custom-call | tf_op jit(solution)/shard_map/gather_all/pallas_call | solution.py:435
  176.7 3.7 fusion.39
  181.0 7.7 %fusion.24 = f32[2,256,4096]{2,1,0:T(8,128)} fusion(bf16[1024,4096,1]{1,0,2:T(8,128)(2,1)S(1)} %bitcast.163, f32[2,256,1024]{2,1,0:T(8,128)S(1)} %get-tuple-element.56, f32[2,1024]{1,0:T(2,128)S(1)} %get-tuple-element.66, f32[2,1024]{1,0:T(2,128)S(1)} %get-tuple-element.67, f32[2,256]{1,0:T(2,128)S(1)} %add_rsqrt_fusion.1, f32[2,256]{1,0:T(2,128)S(1)} %get-tuple-element.77), kind=kOutput, calls=%fused_computation.60 | convolution fusion | flops 4297588736 | bytes 18894848 | tf_op jit(solution)/shard_map/mrd,de->mre/dot_general | solution.py:1174
  188.7 12.3 %convert_reduce_fusion = (f32[4096]{0:T(1024)S(1)}, bf16[2,256,4096]{2,1,0:T(8,128)(2,1)S(1)}) fusion(f32[2,256,4096]{2,1,0:T(8,128)} %fusion.24, f32[4096]{0:T(1024)S(1)} %slice.102, bf16[4096,1024,1]{1,0,2:T(8,128)(2,1)S(1)} %bitcast.160, bf16[2,256,1024]{2,1,0:T(8,128)(2,1)S(1)} %copy-done.16, f32[2,1024]{1,0:T(2,128)S(1)} %get-tuple-element.68), kind=kOutput, calls=%fused_computation.11 | convolution fusion | flops 4344770560 | bytes 22061056 | tf_op jit(solution)/shard_map/mre,de->mrd/dot_general | solution.py:1174
  201.0 11.2 %multiply_reduce_fusion = (f32[2,1024]{1,0:T(2,128)S(1)}, f32[2,256]{1,0:T(2,128)S(1)}, f32[2,256]{1,0:T(2,128)S(1)}, f32[2,1024]{1,0:T(2,128)S(1)}, f32[2,256,1024]{2,1,0:T(8,128)}) fusion(f32[2,256,1024]{2,1,0:T(8,128)S(1)} %get-tuple-element.56, f32[2,256]{1,0:T(2,128)S(1)} %add_rsqrt_fusion.1, f32[2,256]{1,0:T(2,128)S(1)} %get-tuple-element.77, ...), kind=kOutput, calls=%fused_computation.36 | convolution fusion | flops 4299680768 | bytes 16809984 | tf_op jit(solution)/shard_map/mre,de->mrd/dot_general | solution.py:1174
  212.2 10.4 %fusion.19 = (f32[2,1024]{1,0:T(2,128)S(1)}, f32[1024]{0:T(1024)S(1)}, bf16[2,256,1024]{2,1,0:T(8,128)(2,1)}, f32[2,1024]{1,0:T(2,128)S(1)}, f32[2,256,1024]{2,1,0:T(8,128)S(1)}) fusion(bf16[2,256,1024]{2,1,0:T(8,128)(2,1)S(1)} %copy-done.16, f32[1024]{0:T(1024)S(1)} %get-tuple-element.61, f32[2,1024]{1,0:T(2,128)S(1)} %get-tuple-element.68, ...), kind=kOutput, calls=%fused_computation.33 | convolution fusion | flops 4327468032 | bytes 27332608 | tf_op jit(solution)/shard_map/mrd,de->mre/dot_general | solution.py:1174
  222.7 14.2 %bitcast_convert_fusion.1 = bf16[4096,1024]{1,0:T(8,128)(2,1)} fusion(bf16[2,256,1024]{2,1,0:T(8,128)(2,1)S(1)} %copy-done.16, f32[2,1024]{1,0:T(2,128)S(1)} %get-tuple-element.68, f32[2,256,4096]{2,1,0:T(8,128)} %fusion.24, f32[4096]{0:T(1024)S(1)} %slice.102), kind=kOutput, calls=%fused_computation.1 | convolution fusion | flops 4321705984 | bytes 17850368 | tf_op jit(solution)/shard_map/mrd,mre->de/dot_general | solution.py:1174
  236.9 7.4 %bitcast_convert_fusion = bf16[1024,4096]{1,0:T(8,128)(2,1)} fusion(bf16[2,256,4096]{2,1,0:T(8,128)(2,1)S(1)} %copy-done.19, f32[2,256,1024]{2,1,0:T(8,128)S(1)} %get-tuple-element.56, f32[2,1024]{1,0:T(2,128)S(1)} %get-tuple-element.66, f32[2,1024]{1,0:T(2,128)S(1)} %get-tuple-element.67, f32[2,256]{1,0:T(2,128)S(1)} %add_rsqrt_fusion.1, ...), kind=kOutput, calls=%fused_computation | convolution fusion | flops 4301783040 | bytes 14700544 | tf_op jit(solution)/shard_map/mrd,mre->de/dot_general | solution.py:1174
  245.5 2.7 bitcast_convert_fusion.2
  248.2 2.3 convolution_convert_fusion.refs_3_
  250.5 154.7 %back_and_sums.1 = (f32[2,2,32,768]{3,2,1,0:T(8,128)}, f32[128,1024]{1,0:T(8,128)}, f32[32,4096]{1,0:T(8,128)}, f32[32,1024]{1,0:T(8,128)}, f32[2,256,1024]{2,1,0:T(8,128)}, /*index=5*/f32[1,768]{1,0:T(1,128)}) custom-call(bf16[4,2,2,2,128,1024]{5,4,3,2,1,0:T(8,128)(2,1)} %bitcast.124, bf16[4,2,2,2,32,4096]{5,4,3,2,1,0:T(8,128)(2,1)} %bitcast.125, ...), custom_call_target="tpu_custom_call" | custom-call | tf_op jit(solution)/shard_map/back_and_sums/pallas_call | solution.py:1129
  405.2 3.0 fusion.16
  408.2 3.7 fusion.15
  412.5 25.0 %small_sums.1 = f32[4,2,2,2,40,128]{5,4,3,2,1,0:T(8,128)S(1)} custom-call(f32[2,2,40,128]{3,2,1,0:T(8,128)S(1)} %bitcast.123), custom_call_target="tpu_custom_call" | custom-call | tf_op jit(solution)/shard_map/small_sums/pallas_call | solution.py:705
  439.0 12.5 %small_gather.3 = f32[4,2,2,2,8,128]{5,4,3,2,1,0:T(8,128)S(1)} custom-call(f32[8,128]{1,0:T(8,128)S(1)} %pad_bitcast_fusion.own_ref), custom_call_target="tpu_custom_call" | custom-call | tf_op jit(solution)/shard_map/small_gather/pallas_call | solution.py:142
  453.0 0.9 copy.58
  455.5 0.9 copy.61
  456.4 1.3 convolution_bitcast_fusion.1
  457.7 1.0 copy.62
  (126 shorter events, 14.3 us)
Async XLA Ops:
  0.6 20.1 %copy-start.8 = (bf16[131072]{0:T(1024)(128)(2,1)S(1)}, bf16[131072]{0:T(1024)(128)(2,1)}, u32[]{:S(2)}) copy-start(bf16[131072]{0:T(1024)(128)(2,1)} %param.13) | copy-start | bytes 786436
  0.7 20.9 %copy-start.9 = (bf16[131072]{0:T(1024)(128)(2,1)S(1)}, bf16[131072]{0:T(1024)(128)(2,1)}, u32[]{:S(2)}) copy-start(bf16[131072]{0:T(1024)(128)(2,1)} %param.14) | copy-start | bytes 786436
  0.7 21.7 %copy-start.7 = (bf16[196608]{0:T(1024)(128)(2,1)S(1)}, bf16[196608]{0:T(1024)(128)(2,1)}, u32[]{:S(2)}) copy-start(bf16[196608]{0:T(1024)(128)(2,1)} %param.15) | copy-start | bytes 1179652
  22.6 152.9 %copy-start.11 = (f32[2,8,4,256]{3,1,2,0:T(8,128)}, f32[2,8,4,256]{3,1,2,0:T(8,128)S(1)}, u32[]{:S(2)}) copy-start(f32[2,8,4,256]{3,1,2,0:T(8,128)S(1)} %copy.34) | copy-start | bytes 196612
  22.9 153.5 %copy-start = (bf16[2,256,1024]{2,1,0:T(8,128)(2,1)S(1)}, bf16[2,256,1024]{2,1,0:T(8,128)(2,1)}, u32[]{:S(2)}) copy-start(bf16[2,256,1024]{2,1,0:T(8,128)(2,1)} %refs_0_.1) | copy-start | bytes 3145732
  176.7 4.3 copy-start.14
  180.4 8.3 %slice-start = ((s8[8388608]{0:T(1024)(128)(4,1)}), s8[4194304]{0:T(1024)(128)(4,1)S(1)}, s32[]{:S(2)}) async-start(s8[8388608]{0:T(1024)(128)(4,1)} %bitcast.158), calls=%async_computation | async-start | bytes 8388608
  181.0 7.7 %slice-start.1 = ((s8[8388608]{0:T(1024)(128)(4,1)}), s8[4194304]{0:T(1024)(128)(4,1)S(1)}, s32[]{:S(2)}) async-start(s8[8388608]{0:T(1024)(128)(4,1)} %bitcast.158), calls=%async_computation.1 | async-start | bytes 8388608
  181.0 7.7 %copy-start.16 = (bf16[2,256,1024]{2,1,0:T(8,128)(2,1)S(1)}, bf16[2,256,1024]{2,1,0:T(8,128)(2,1)}, u32[]{:S(2)}) copy-start(bf16[2,256,1024]{2,1,0:T(8,128)(2,1)} %param.17) | copy-start | bytes 3145732
  201.0 11.2 %copy-start.18 = (bf16[2,256,4096]{2,1,0:T(8,128)(2,1)}, bf16[2,256,4096]{2,1,0:T(8,128)(2,1)S(1)}, u32[]{:S(2)}) copy-start(bf16[2,256,4096]{2,1,0:T(8,128)(2,1)S(1)} %get-tuple-element.75) | copy-start | bytes 12582916
  222.6 21.7 %copy-start.2 = (f32[2,256,1024]{2,1,0:T(8,128)}, f32[2,256,1024]{2,1,0:T(8,128)S(1)}, u32[]{:S(2)}) copy-start(f32[2,256,1024]{2,1,0:T(8,128)S(1)} %get-tuple-element.59) | copy-start | bytes 6291460
  222.6 14.2 %copy-start.19 = (bf16[2,256,4096]{2,1,0:T(8,128)(2,1)S(1)}, bf16[2,256,4096]{2,1,0:T(8,128)(2,1)}, u32[]{:S(2)}) copy-start(bf16[2,256,4096]{2,1,0:T(8,128)(2,1)} %copy-done.18) | copy-start | bytes 12582916
  244.3 1.2 copy-start.17
  245.5 2.7 copy-start.15
  405.2 3.0 copy-start.1
  405.2 3.0 copy-start.3
  408.2 3.7 copy-start.13
  437.8 14.0 %copy-start.12 = (bf16[2,256]{1,0:T(2,128)(2,1)S(1)}, bf16[2,256]{1,0:T(2,128)(2,1)}, u32[]{:S(2)}) copy-start(bf16[2,256]{1,0:T(2,128)(2,1)} %param.10) | copy-start | bytes 3076
  437.8 14.6 %copy-start.6 = (f32[2,2,32,768]{3,2,1,0:T(8,128)S(1)}, f32[2,2,32,768]{3,2,1,0:T(8,128)}, u32[]{:S(2)}) copy-start(f32[2,2,32,768]{3,2,1,0:T(8,128)} %get-tuple-element.37) | copy-start | bytes 1179652
  438.5 15.5 %copy-start.10 = (f32[32,1024]{1,0:T(8,128)S(1)}, f32[32,1024]{1,0:T(8,128)}, u32[]{:S(2)}) copy-start(f32[32,1024]{1,0:T(8,128)} %get-tuple-element.38) | copy-start | bytes 393220
  438.9 15.7 %copy-start.5 = (f32[32,4096]{1,0:T(8,128)S(1)}, f32[32,4096]{1,0:T(8,128)}, u32[]{:S(2)}) copy-start(f32[32,4096]{1,0:T(8,128)} %get-tuple-element.39) | copy-start | bytes 1572868
  451.7 3.8 copy-start.4

commit v3 on v2

v3 whole, which is shorter than its diff:
```python
import functools

import jax
import jax.numpy as jnp
from jax import lax
from jax.experimental import pallas as pl
from jax.experimental.pallas import tpu as pltpu
from jax.sharding import PartitionSpec as P

D = 1024
HEADS = 16
HEAD = 64
FF = 4096
GROUP = 4
OWN = D // GROUP
SCALE = HEAD**-0.5
LANES = 128
MICROS = 2

epsilon = 1e-06
highest = lax.Precision.HIGHEST
MESH = pl.DeviceIdType.MESH
MIB = 1 << 20


def silu(values):
    return values / (1.0 + jnp.exp(-values))


class Links:
    def __init__(self, planes, send_sem, recv_sem, local_sem=None):
        me = lax.axis_index("fsdp")
        self.planes = planes
        self.c = me % 2
        self.x = (me // 2) % 2
        self.y = (me // 4) % 2
        self.z = me // 8
        self.core = me + 1 - 2 * self.c
        self.beside = me + 2 - 4 * self.x
        self.across = me + 4 - 8 * self.y
        self.place = me % 8
        self.send_sem, self.recv_sem, self.local_sem = send_sem, recv_sem, local_sem
        self.used = 0
        self.local_used = 0
        self.pending = []

    def plane(self, step):
        return (self.z + step) % self.planes

    def plane_device(self, step):
        return self.plane(step) * 8 + self.place

    def partners(self):
        return [self.core, self.beside, self.across] + [
            self.plane_device(step) for step in range(1, self.planes)
        ]

    def greet(self, partners):
        barrier = pltpu.get_barrier_semaphore()
        for partner in partners:
            pl.semaphore_signal(barrier, inc=1, device_id=(partner,), device_id_type=MESH)
        pl.semaphore_wait(barrier, len(partners))

    def send(self, source, target, device):
        assert self.used < self.send_sem.shape[0]
        copy = pltpu.make_async_remote_copy(
            src_ref=source,
            dst_ref=target,
            send_sem=self.send_sem.at[self.used],
            recv_sem=self.recv_sem.at[self.used],
            device_id=(device,),
            device_id_type=MESH,
        )
        self.used += 1
        copy.start()
        self.pending.append(copy)
        return copy

    def local(self, source, target):
        assert self.local_used < self.local_sem.shape[0]
        copy = pltpu.make_async_copy(source, target, self.local_sem.at[self.local_used])
        self.local_used += 1
        copy.start()
        return copy

    def finish_sends(self):
        for copy in self.pending:
            copy.wait_send()
        self.pending = []


def arrived(copies):
    for copy in copies:
        copy.wait_recv()


ANY = pl.BlockSpec(memory_space=pl.ANY)
VMEM = pl.BlockSpec(memory_space=pltpu.VMEM)


def remote_call(body, name, collective_id, outs, in_specs, out_specs, scratch, sems, local_sems, vmem):
    return pl.pallas_call(
        body,
        out_shape=outs,
        in_specs=in_specs,
        out_specs=out_specs,
        scratch_shapes=[
            pltpu.SemaphoreType.DMA((sems,)),
            pltpu.SemaphoreType.DMA((sems,)),
            pltpu.SemaphoreType.DMA((max(local_sems, 1),)),
            *scratch,
        ],
        compiler_params=pltpu.CompilerParams(
            collective_id=collective_id, has_side_effects=True, vmem_limit_bytes=vmem
        ),
        name=name,
    )


def small_gather_body(planes, own_ref, out_ref, send_sem, recv_sem, local_sem):
    links = Links(planes, send_sem, recv_sem)
    links.greet(links.partners())
    z, y, x, c = links.z, links.y, links.x, links.c
    out_ref[z, y, x, c] = own_ref[...]
    spread(links, out_ref)
    links.finish_sends()


def spread(links, out_ref):
    z, y, x, c = links.z, links.y, links.x, links.c
    block = out_ref.at[z, y, x, c]
    arrived([links.send(block, block, links.plane_device(s)) for s in range(1, links.planes)])
    block = out_ref.at[:, y, x, c]
    arrived([links.send(block, block, links.across)])
    block = out_ref.at[:, :, x, c]
    arrived([links.send(block, block, links.beside)])
    block = out_ref.at[:, :, :, c]
    arrived([links.send(block, block, links.core)])


def small_gather(own, planes, collective_id):
    return remote_call(
        functools.partial(small_gather_body, planes),
        "small_gather",
        collective_id,
        jax.ShapeDtypeStruct((planes, 2, 2, 2, *own.shape), own.dtype),
        [VMEM],
        VMEM,
        [],
        planes + 2,
        0,
        40 * MIB,
    )(own)


WIDTH = 1024
OVER_X = 640


class Pieces:
    def __init__(self, links, shards, fulls):
        self.links = links
        self.pieces, self.owns = [], []
        for shard, full in zip(shards, fulls):
            z, y, x, c = links.z, links.y, links.x, links.c
            self.owns.append([links.local(shard, full.at[z, y, x, c]), False])
            for rows, columns in cuts(shard.shape):
                self.pieces.append((len(self.owns) - 1, shard, full, rows, columns))
        count = len(self.pieces)
        self.first = [None] * count
        self.second = [None] * count
        self.third = [None] * count
        self.late = [[] for _ in range(count)]

    def block(self, k, part, *place):
        _, _, full, rows, start = self.pieces[k]
        columns = {
            "all": pl.ds(start, WIDTH),
            "T": pl.ds(start, OVER_X),
            "F": pl.ds(start + OVER_X, WIDTH - OVER_X),
        }[part]
        return full.at[(*place, rows, columns)]

    def across_planes(self, k):
        links = self.links
        _, shard, _, rows, start = self.pieces[k]
        source = shard.at[rows, pl.ds(start, WIDTH)]
        target = self.block(k, "all", links.z, links.y, links.x, links.c)
        self.first[k] = [
            links.send(source, target, links.plane_device(s)) for s in range(1, links.planes)
        ]

    def pass_to_core(self, k, part, *place):
        block = self.block(k, part, *place)
        self.late[k].append(self.links.send(block, block, self.links.core))

    def B(self, k):
        links = self.links
        own = self.owns[self.pieces[k][0]]
        if not own[1]:
            own[0].wait()
            own[1] = True
        arrived(self.first[k])
        place = (slice(None), links.y, links.x, links.c)
        over_x, over_y = self.block(k, "T", *place), self.block(k, "F", *place)
        self.second[k] = {
            "T": links.send(over_x, over_x, links.beside),
            "F": links.send(over_y, over_y, links.across),
        }
        self.pass_to_core(k, "all", *place)

    def CT(self, k):
        links = self.links
        y, x, c = links.y, links.x, links.c
        arrived([self.second[k]["T"]])
        block = self.block(k, "T", slice(None), y, slice(None), c)
        self.third[k] = {**(self.third[k] or {}), "T": links.send(block, block, links.across)}
        self.pass_to_core(k, "T", slice(None), y, 1 - x, c)

    def CF(self, k):
        links = self.links
        y, x, c = links.y, links.x, links.c
        arrived([self.second[k]["F"]])
        block = self.block(k, "F", slice(None), slice(None), x, c)
        self.third[k] = {**(self.third[k] or {}), "F": links.send(block, block, links.beside)}
        self.pass_to_core(k, "F", slice(None), 1 - y, x, c)

    def DT(self, k):
        links = self.links
        arrived([self.third[k]["T"]])
        self.pass_to_core(k, "T", slice(None), 1 - links.y, slice(None), links.c)

    def DF(self, k):
        links = self.links
        arrived([self.third[k]["F"]])
        self.pass_to_core(k, "F", slice(None), slice(None), 1 - links.x, links.c)

    def there(self, k):
        arrived(self.late[k])
        self.late[k] = []


def cuts(shape):
    rows, width = shape
    if width > WIDTH:
        return [(slice(None), start) for start in range(0, width, WIDTH)]
    count = 4 if rows % 128 == 0 else 1
    return [(pl.ds(part * (rows // count), rows // count), 0) for part in range(count)]


def gather_order(count):
    order = []
    for k in range(count + 2):
        for task, behind in (("B", 0), ("CT", 1), ("CF", 1), ("DT", 2), ("DF", 2)):
            if 0 <= k - behind < count:
                order.append((task, k - behind))
    return order


AHEAD = 2


class Opening:
    CUTS = 3

    def __init__(self, links, tokens, attend, partial, tokens_out, attend_out, modulation_out, scratch):
        self.links, self.partial = links, partial
        self.tokens_out, self.attend_out, self.modulation_out = tokens_out, attend_out, modulation_out
        held, self.from_core, self.from_beside, self.from_across, self.from_planes, self.total = scratch
        z, y, x, c = links.z, links.y, links.x, links.c
        own_slice = links.local(attend.at[x, c], attend_out.at[z, y, x, c])
        far = links.send(attend.at[1 - x, 1 - c], held, links.core)
        to_core = links.send(attend.at[x, 1 - c], attend_out.at[z, y, x, c], links.core)
        to_beside = links.send(attend.at[1 - x, c], attend_out.at[z, y, x, c], links.beside)
        step = links.send(partial.at[:, :, :, 1 - c], self.from_core, links.core)
        arrived([step])
        self.from_core[...] = self.from_core[...] + partial[:, :, :, c]
        step = links.send(self.from_core.at[:, :, 1 - x], self.from_beside, links.beside)
        arrived([far])
        far_beside = links.send(held, attend_out.at[z, y, x, 1 - c], links.beside)
        self.own_tokens = links.local(tokens, tokens_out.at[:, x, c])
        self.tokens_beside = [
            links.send(tokens.at[m], tokens_out.at[m, x, c], links.beside)
            for m in range(tokens.shape[0])
        ]
        self.rest = [links.send(tokens, tokens_out.at[:, x, c], links.core)]
        own_slice.wait()
        arrived([to_core, to_beside, far_beside])
        width = attend_out.shape[-1] // self.CUTS
        self.columns = [pl.ds(part * width, width) for part in range(self.CUTS)]
        self.over_planes = []
        for columns in self.columns:
            block = attend_out.at[z, y, :, :, :, columns]
            self.over_planes.append(
                [links.send(block, block, links.plane_device(s)) for s in range(1, links.planes)]
            )
        arrived([step])
        self.from_beside[...] = self.from_beside[...] + self.from_core[:, :, x]
        step = links.send(self.from_beside.at[:, 1 - y], self.from_across, links.across)
        self.attend_over_y(0)
        arrived([step])
        self.from_across[...] = self.from_across[...] + self.from_beside[:, y]
        self.step = [
            links.send(
                self.from_across.at[links.plane(s)],
                self.from_planes.at[s - 1],
                links.plane_device(s),
            )
            for s in range(1, links.planes)
        ]

    def attend_over_y(self, part):
        links = self.links
        arrived(self.over_planes[part])
        block = self.attend_out.at[:, links.y, :, :, :, self.columns[part]]
        self.rest.append(links.send(block, block, links.across))

    def modulation_quarter(self):
        links = self.links
        arrived(self.step)
        result = self.from_across[links.z]
        for s in range(1, links.planes):
            result = result + self.from_planes[s - 1]
        self.total[...] = result
        self.modulation_out[links.x, links.c] = result
        target = self.modulation_out.at[links.x, links.c]
        self.step = [
            links.send(self.total, target, links.core),
            links.send(self.total, target, links.beside),
        ]

    def tokens_to_core(self, m):
        links = self.links
        arrived([self.tokens_beside[m]])
        fresh = self.tokens_out.at[m, 1 - links.x, links.c]
        self.rest.append(links.send(fresh, fresh, links.core))

    def modulation_to_core(self):
        links = self.links
        arrived(self.step)
        fresh = self.modulation_out.at[1 - links.x, links.c]
        self.rest.append(links.send(fresh, fresh, links.core))

    def finish(self):
        arrived(self.rest)
        self.own_tokens.wait()


def gather_body(
    planes,
    tokens,
    attend,
    project,
    expand,
    contract,
    partial,
    attend_out,
    project_out,
    expand_out,
    contract_out,
    modulation_out,
    tokens_out,
    send_sem,
    recv_sem,
    local_sem,
    *scratch,
):
    links = Links(planes, send_sem, recv_sem, local_sem)
    links.greet(links.partners())
    opening = Opening(
        links, tokens, attend, partial, tokens_out, attend_out, modulation_out, scratch
    )
    pieces = Pieces(links, (project, expand, contract), (project_out, expand_out, contract_out))
    count = len(pieces.pieces)
    for part in range(1, Opening.CUTS):
        opening.attend_over_y(part)
    opening.modulation_quarter()
    for m in range(tokens.shape[0]):
        opening.tokens_to_core(m)
    opening.modulation_to_core()
    for k in range(min(AHEAD, count)):
        pieces.across_planes(k)
    for task, k in gather_order(count):
        getattr(pieces, task)(k)
        if task == "B" and k + AHEAD < count:
            pieces.across_planes(k + AHEAD)
    for k in range(count):
        pieces.there(k)
    opening.finish()
    links.finish_sends()


FRONT_ORDER = (
    ("az", 1), ("az", 2), ("m3", 0), ("tk", 0), ("tk", 1), ("m4", 0), ("B", 0), ("att", 0), ("unit", 0),
    ("CF", 0), ("CT", 0), ("B", 1), ("unit", 1), ("unit", 2), ("unit", 3), ("DF", 0), ("B", 2),
    ("unit", 4), ("DT", 0), ("CT", 1), ("unit", 5), ("CF", 1), ("B", 3), ("CT", 2), ("CF", 2), ("unit", 6),
    ("B", 4), ("unit", 7), ("DT", 1), ("unit", 8), ("CF", 3), ("DF", 1), ("unit", 9), ("unit", 10),
    ("CT", 3), ("unit", 11), ("DT", 2), ("unit", 12), ("DF", 2), ("B", 5), ("unit", 13), ("CT", 4),
    ("CF", 4), ("unit", 14), ("unit", 15), ("DF", 3), ("DT", 3), ("B", 6), ("unit", 16), ("unit", 17),
    ("B", 7), ("load", 0), ("own", 0), ("CF", 5), ("CT", 5), ("DT", 4), ("there", 1), ("mlp", 0), ("B", 8),
    ("DF", 4), ("CF", 6), ("CT", 6), ("there", 2), ("mlp", 1), ("CF", 7), ("CT", 7), ("DT", 5),
    ("there", 3), ("mlp", 2), ("CF", 8), ("DF", 5), ("CT", 8), ("there", 4), ("mlp", 3), ("DT", 6),
    ("DF", 6), ("DF", 7), ("DT", 7), ("DF", 8), ("DT", 8),
)


def front_body(planes, *refs):
    tokens, attend, project, expand, contract, partial, refs = *refs[:6], refs[6:]
    shift, bias_qkv, bias_project, bias_expand, cotangent, refs = *refs[:5], refs[5:]
    attend_out, project_out, expand_out, contract_out, modulation_out, refs = *refs[:5], refs[5:]
    first_out, qkv_out, heads_out, log_out, blended_out, refs = *refs[:5], refs[5:]
    middle_out, attended_out, second_out, act_out, slope_out, branch_out, grad_out = refs[:7]
    send_sem, recv_sem, local_sem = refs[7:10]
    opening_scratch, refs = refs[10:16], refs[16:]
    tokens_all, attend_all, first, qkv, heads, blended, project_all, expand_all = refs[:8]
    middle, attended, second, act, slope, grad_branch, grads, upstream = refs[8:]
    links = Links(planes, send_sem, recv_sem, local_sem)
    x, c = links.x, links.c
    corner = links.beside + 1 - 2 * c
    links.greet([*links.partners(), corner])
    opening = Opening(
        links, tokens, attend, partial, tokens_all, attend_all, modulation_out, opening_scratch
    )
    pieces = Pieces(links, (project, expand, contract), (project_out, expand_out, contract_out))
    count = len(pieces.pieces)
    for k in range(min(AHEAD, count)):
        pieces.across_planes(k)
    loaded_upstream = links.local(cotangent, upstream)
    micros, own_rows, _ = tokens.shape
    stored, stored_grads, exchanged, loading = [], [], [], []
    own_heads = pl.ds(pl.multiple_of((2 * x + c) * OWN, OWN), OWN)

    def part_of(m, to_x, to_c):
        start = pl.multiple_of((2 * to_x + to_c) * own_rows, own_rows)
        return heads.at[m, pl.ds(start, own_rows)]

    def project_micro(m):
        project_tokens(m, tokens_all, attend_all, modulation_out, shift, bias_qkv, first, qkv)
        stored.append(links.local(first.at[m], first_out.at[m]))
        stored.append(links.local(qkv.at[m], qkv_out.at[m]))

    def far_heads(m, head):
        attention_unit(qkv.at[m], heads.at[m], log_out.at[m], head, 1 - x)
        if head == OWN // HEAD - 1:
            target = blended.at[m, :, own_heads]
            exchanged.append(links.send(part_of(m, 1 - x, 1 - c), target, corner))
            exchanged.append(links.send(part_of(m, 1 - x, c), target, links.beside))

    def near_heads(m, head):
        attention_unit(qkv.at[m], heads.at[m], log_out.at[m], head, x)
        if head == OWN // HEAD - 1:
            target = blended.at[m, :, own_heads]
            exchanged.append(links.send(part_of(m, x, 1 - c), target, links.core))
            stored.append(links.local(heads.at[m], heads_out.at[m]))
            links.local(part_of(m, x, c), target).wait()

    units = []
    for m in range(micros):
        units.append(functools.partial(project_micro, m))
        units += [functools.partial(far_heads, m, head) for head in range(OWN // HEAD)]
    for m in range(micros):
        units += [functools.partial(near_heads, m, head) for head in range(OWN // HEAD)]

    def load_project():
        pieces.there(0)
        loading.append(links.local(project_out, project_all))
        loaded_upstream.wait()
        for m in range(micros):
            gate = modulation_row(modulation_out, m, 5) + shift[5:6, :]
            grad_branch[m] = (gate * upstream[m].astype(jnp.float32)).astype(jnp.bfloat16)
        stored.append(links.local(grad_branch, branch_out))

    def own_tokens():
        loading.pop().wait()
        for m in range(micros):
            stored.append(links.local(blended.at[m], blended_out.at[m]))
            product = jnp.dot(
                blended[m],
                project_all[...].reshape(D, D),
                preferred_element_type=jnp.float32,
            )
            attended[m] = product + bias_project[...]
            gate = modulation_row(modulation_out, m, 2) + shift[2:3, :]
            middle[m] = tokens_all[m, x, c].astype(jnp.float32) + gate * attended[m]
            normed, _ = normalize(middle[m])
            factors = 1.0 + modulation_row(modulation_out, m, 4) + shift[4:5, :]
            offsets = modulation_row(modulation_out, m, 3) + shift[3:4, :]
            second[m] = (normed * factors + offsets).astype(jnp.bfloat16)
        stored.append(links.local(middle, middle_out))
        stored.append(links.local(attended, attended_out))
        stored.append(links.local(second, second_out))

    parts = FF // WIDTH
    blocks = grads.shape[1]

    def expand_unit(part):
        columns = pl.ds(part * WIDTH, WIDTH)
        loaded = links.local(expand_out.at[:, :, :, :, :, columns], expand_all)
        if part >= 2:
            stored_grads[part - 2].wait()
        loaded.wait()
        expand_part(part, WIDTH, second, expand_all, bias_expand, act, slope, grad_branch, grads)
        stored.append(links.local(act.at[:, :, columns], act_out.at[:, :, columns]))
        stored.append(links.local(slope.at[:, :, columns], slope_out.at[:, :, columns]))
        stored_grads.append(
            links.local(grads.at[part % 2], grad_out.at[pl.ds(part * blocks, blocks)])
        )

    for task, k in FRONT_ORDER:
        if task == "az":
            opening.attend_over_y(k)
        elif task == "m3":
            opening.modulation_quarter()
        elif task == "tk":
            opening.tokens_to_core(k)
        elif task == "m4":
            opening.modulation_to_core()
        elif task == "att":
            opening.finish()
            stored.append(links.local(attend_all, attend_out))
        elif task == "unit":
            units[k]()
        elif task == "load":
            load_project()
        elif task == "own":
            arrived(exchanged)
            own_tokens()
        elif task == "there":
            pieces.there(k)
        elif task == "mlp":
            expand_unit(k)
        else:
            getattr(pieces, task)(k)
            if task == "B" and k + AHEAD < count:
                pieces.across_planes(k + AHEAD)
    for k in range(count):
        pieces.there(k)
    for copy in stored + stored_grads[-2:]:
        copy.wait()
    links.finish_sends()


ROOT = 0.7978845608028654
CUBE = 0.044715
CHUNK = 512


def expand_part(part, width, second, expand, bias, act, slope, grad_branch, grads):
    micros = second.shape[0]
    rows = grads.shape[2]

    @pl.loop(0, width // CHUNK)
    def _(chunk):
        inside = pl.ds(pl.multiple_of(chunk * CHUNK, CHUNK), CHUNK)
        columns = pl.ds(pl.multiple_of(part * width + chunk * CHUNK, CHUNK), CHUNK)
        weights = expand[:, :, :, :, :, inside].reshape(D, CHUNK)
        total = None
        for m in range(micros):
            hidden = jnp.dot(second[m], weights, preferred_element_type=jnp.float32)
            hidden = hidden + bias[:, columns]
            square = hidden * hidden
            bend = jnp.tanh(hidden * (ROOT + (ROOT * CUBE) * square))
            half = 0.5 + 0.5 * bend
            low = (hidden * half).astype(jnp.bfloat16)
            act[m, :, columns] = low
            steep = hidden * (0.5 * ROOT + (1.5 * ROOT * CUBE) * square)
            slope[m, :, columns] = (half + steep * (1.0 - bend * bend)).astype(jnp.bfloat16)
            product = lax.dot_general(
                low, grad_branch[m], (((0,), (0,)), ((), ())), preferred_element_type=jnp.float32
            )
            total = product if total is None else total + product
        count = CHUNK // rows
        here = pl.ds(chunk * count, count)
        grads[part % 2, here] = total.astype(jnp.bfloat16).reshape(count, rows, D)


def modulation_row(modulation, m, block):
    per_quarter = modulation.shape[2] // MICROS
    pieces = []
    for k in range(block * D // LANES, (block + 1) * D // LANES):
        quarter, row = k // per_quarter, m * per_quarter + k % per_quarter
        pieces.append(modulation[quarter // 2, quarter % 2, row : row + 1, :])
    return jnp.concatenate(pieces, axis=1)


def project_tokens(m, tokens, attend, modulation, shift, bias, first_out, qkv_out):
    offsets = modulation_row(modulation, m, 0) + shift[0:1, :]
    factors = 1.0 + modulation_row(modulation, m, 1) + shift[1:2, :]
    rows = tokens.shape[3]

    @pl.loop(0, GROUP)
    def _(block):
        values = tokens[m, block // 2, block % 2].astype(jnp.float32)
        normed, _ = normalize(values)
        first = (normed * factors + offsets).astype(jnp.bfloat16)
        here = pl.ds(pl.multiple_of(block * rows, rows), rows)
        first_out[m, here, :] = first
        weights = attend[...].reshape(D, 3 * OWN)
        product = jnp.dot(first, weights, preferred_element_type=jnp.float32)
        qkv_out[m, here, :] = (product + bias[...]).astype(jnp.bfloat16)


def gather_scratch(attend, partial, planes):
    rows = partial.shape[-2]
    return [
        pltpu.VMEM((attend.shape[-2], attend.shape[-1]), attend.dtype),
        pltpu.VMEM((planes, 2, 2, rows, LANES), jnp.float32),
        pltpu.VMEM((planes, 2, rows, LANES), jnp.float32),
        pltpu.VMEM((planes, rows, LANES), jnp.float32),
        pltpu.VMEM((planes - 1, rows, LANES), jnp.float32),
        pltpu.VMEM((rows, LANES), jnp.float32),
    ]


def gather_outs(attend, project, expand, contract, partial, planes):
    return [
        *(
            jax.ShapeDtypeStruct((planes, 2, 2, 2, *shard.shape[-2:]), shard.dtype)
            for shard in (attend, project, expand, contract)
        ),
        jax.ShapeDtypeStruct((2, 2, partial.shape[-2], LANES), jnp.float32),
    ]


def gather_sems(planes):
    return 40 + 14 * (planes - 1) + 9 * 10


def gather_all(tokens, attend, project, expand, contract, partial, planes):
    micros, own_rows, _ = tokens.shape
    return remote_call(
        functools.partial(gather_body, planes),
        "gather_all",
        1,
        (
            *gather_outs(attend, project, expand, contract, partial, planes),
            jax.ShapeDtypeStruct((micros, 2, 2, own_rows, D), tokens.dtype),
        ),
        [ANY] * 5 + [VMEM],
        (ANY,) * 4 + (VMEM, ANY),
        gather_scratch(attend, partial, planes),
        gather_sems(planes),
        8,
        56 * MIB,
    )(tokens, attend, project, expand, contract, partial)


def front(tokens, attend, project, expand, contract, partial, vectors, cotangent, planes):
    micros, own_rows, _ = tokens.shape
    latent_rows = own_rows * GROUP
    blocks = latent_rows // QUERY_ROWS
    grad_rows = contract.shape[0]

    def low(*shape):
        return jax.ShapeDtypeStruct(shape, jnp.bfloat16)

    def held(*shape, dtype=jnp.bfloat16):
        return pltpu.VMEM(shape, dtype)

    log_shape = (micros, OWN // HEAD, blocks, 1, QUERY_ROWS)
    own = (micros, own_rows, D)
    parts = FF // WIDTH
    return remote_call(
        functools.partial(front_body, planes),
        "front",
        1,
        (
            *gather_outs(attend, project, expand, contract, partial, planes),
            low(micros, latent_rows, D),
            low(micros, latent_rows, 3 * OWN),
            low(micros, latent_rows, OWN),
            jax.ShapeDtypeStruct(log_shape, jnp.float32),
            low(*own),
            jax.ShapeDtypeStruct(own, jnp.float32),
            jax.ShapeDtypeStruct(own, jnp.float32),
            low(*own),
            low(micros, own_rows, FF),
            low(micros, own_rows, FF),
            low(*own),
            low(FF // grad_rows, grad_rows, D),
        ),
        [ANY] * 5 + [VMEM] * 5 + [ANY],
        (ANY,) * 4 + (VMEM,) + (ANY,) * 3 + (VMEM,) + (ANY,) * 8,
        [
            *gather_scratch(attend, partial, planes),
            held(micros, 2, 2, own_rows, D),
            held(planes, 2, 2, 2, *attend.shape[-2:]),
            held(micros, latent_rows, D),
            held(micros, latent_rows, 3 * OWN),
            held(micros, latent_rows, OWN),
            held(*own),
            held(planes, 2, 2, 2, *project.shape),
            held(planes, 2, 2, 2, expand.shape[0], FF // parts),
            held(*own, dtype=jnp.float32),
            held(*own, dtype=jnp.float32),
            held(*own),
            held(micros, own_rows, FF),
            held(micros, own_rows, FF),
            held(*own),
            held(2, FF // parts // grad_rows, grad_rows, D),
            held(*own),
        ],
        gather_sems(planes),
        40,
        60 * MIB,
    )(tokens, attend, project, expand, contract, partial, *vectors, cotangent)


QUERY_ROWS = 256


def attention_unit(qkv, out, log, head, side=None):
    count = qkv.shape[0] // QUERY_ROWS
    start = 0
    if side is not None:
        count //= 2
        start = side * count
    at = head * HEAD
    keys = qkv[:, OWN + at : OWN + at + HEAD]
    values_t = qkv[:, 2 * OWN + at : 2 * OWN + at + HEAD].T

    @pl.loop(0, count)
    def _(index):
        block = start + index
        here = pl.ds(pl.multiple_of(block * QUERY_ROWS, QUERY_ROWS), QUERY_ROWS)
        queries = qkv[here, at : at + HEAD] * SCALE
        scores = lax.dot_general(
            keys, queries, (((1,), (1,)), ((), ())), preferred_element_type=jnp.float32
        )
        top = jnp.max(scores, axis=0, keepdims=True)
        weights = jnp.exp(scores - top)
        totals = jnp.sum(weights, axis=0, keepdims=True)
        blended = jnp.dot(
            values_t, weights.astype(jnp.bfloat16), preferred_element_type=jnp.float32
        )
        out[here, at : at + HEAD] = (blended / totals).T.astype(jnp.bfloat16)
        log[head, block] = top + jnp.log(totals)


def attention_body(qkv_ref, out_ref, log_ref):
    for head in range(OWN // HEAD):
        attention_unit(qkv_ref.at[0], out_ref.at[0], log_ref.at[0], head)


def attention(qkv):
    micros, rows, _ = qkv.shape
    heads = OWN // HEAD
    blocks = rows // 256
    return pl.pallas_call(
        attention_body,
        grid=(micros,),
        out_shape=(
            jax.ShapeDtypeStruct((micros, rows, OWN), jnp.bfloat16),
            jax.ShapeDtypeStruct((micros, heads, blocks, 1, 256), jnp.float32),
        ),
        in_specs=[pl.BlockSpec((1, rows, 3 * OWN), lambda m: (m, 0, 0))],
        out_specs=(
            pl.BlockSpec((1, rows, OWN), lambda m: (m, 0, 0)),
            pl.BlockSpec((1, heads, blocks, 1, 256), lambda m: (m, 0, 0, 0, 0)),
        ),
        compiler_params=pltpu.CompilerParams(vmem_limit_bytes=48 * MIB),
        name="attention",
    )(qkv)


def attention_back_unit(qkv, blended_all, grad_all, log, out, key_sum, value_sum, head):
    at = head * HEAD
    keys = qkv[:, OWN + at : OWN + at + HEAD]
    keys_t = keys.T
    values = qkv[:, 2 * OWN + at : 2 * OWN + at + HEAD]
    key_sum[...] = jnp.zeros_like(key_sum)
    value_sum[...] = jnp.zeros_like(value_sum)

    @pl.loop(0, qkv.shape[0] // QUERY_ROWS)
    def _(block):
        here = pl.ds(pl.multiple_of(block * QUERY_ROWS, QUERY_ROWS), QUERY_ROWS)
        queries = qkv[here, at : at + HEAD] * SCALE
        grads = grad_all[here, at : at + HEAD]
        blended = blended_all[here, at : at + HEAD]
        row_terms = jnp.sum(
            (grads.astype(jnp.float32) * blended.astype(jnp.float32)).T, axis=0, keepdims=True
        )
        scores = lax.dot_general(
            keys, queries, (((1,), (1,)), ((), ())), preferred_element_type=jnp.float32
        )
        chances = jnp.exp(scores - log[head, block])
        grad_chances = lax.dot_general(
            values, grads, (((1,), (1,)), ((), ())), preferred_element_type=jnp.float32
        )
        grad_scores = (chances * (grad_chances - row_terms)).astype(jnp.bfloat16)
        value_sum[...] += jnp.dot(
            chances.astype(jnp.bfloat16), grads, preferred_element_type=jnp.float32
        )
        key_sum[...] += jnp.dot(grad_scores, queries, preferred_element_type=jnp.float32)
        grad_queries = jnp.dot(keys_t, grad_scores, preferred_element_type=jnp.float32)
        out[here, at : at + HEAD] = (grad_queries.T * SCALE).astype(jnp.bfloat16)

    out[:, OWN + at : OWN + at + HEAD] = key_sum[...].astype(jnp.bfloat16)
    out[:, 2 * OWN + at : 2 * OWN + at + HEAD] = value_sum[...].astype(jnp.bfloat16)


def attention_back_body(qkv_ref, blended_ref, grad_ref, log_ref, out_ref, key_sum, value_sum):
    for head in range(OWN // HEAD):
        attention_back_unit(
            qkv_ref.at[0],
            blended_ref.at[0],
            grad_ref.at[0],
            log_ref.at[0],
            out_ref.at[0],
            key_sum,
            value_sum,
            head,
        )


def attention_back(qkv, blended, grads, logs):
    micros, rows, _ = qkv.shape
    heads = OWN // HEAD
    blocks = rows // 256
    wide = pl.BlockSpec((1, rows, 3 * OWN), lambda m: (m, 0, 0))
    narrow = pl.BlockSpec((1, rows, OWN), lambda m: (m, 0, 0))
    return pl.pallas_call(
        attention_back_body,
        grid=(micros,),
        out_shape=jax.ShapeDtypeStruct((micros, rows, 3 * OWN), jnp.bfloat16),
        in_specs=[
            wide,
            narrow,
            narrow,
            pl.BlockSpec((1, heads, blocks, 1, 256), lambda m: (m, 0, 0, 0, 0)),
        ],
        out_specs=wide,
        scratch_shapes=[pltpu.VMEM((rows, HEAD), jnp.float32)] * 2,
        compiler_params=pltpu.CompilerParams(vmem_limit_bytes=48 * MIB),
        name="attention_back",
    )(qkv, blended, grads, logs)


def heads_to_tokens_body(blended, out, send_sem, recv_sem, local_sem):
    links = Links(1, send_sem, recv_sem, local_sem)
    x, c = links.x, links.c
    corner = links.beside + 1 - 2 * c
    links.greet([links.core, links.beside, corner])
    target = out.at[:, :, pl.ds(pl.multiple_of((2 * x + c) * OWN, OWN), OWN)]
    own = links.local(blended.at[:, x, c], target)
    copies = [
        links.send(blended.at[:, 1 - x, 1 - c], target, corner),
        links.send(blended.at[:, 1 - x, c], target, links.beside),
        links.send(blended.at[:, x, 1 - c], target, links.core),
    ]
    arrived(copies)
    own.wait()
    links.finish_sends()


def heads_to_tokens(blended):
    micros, rows, _ = blended.shape
    own_rows = rows // GROUP
    return remote_call(
        heads_to_tokens_body,
        "heads_to_tokens",
        2,
        jax.ShapeDtypeStruct((micros, own_rows, D), blended.dtype),
        [ANY],
        ANY,
        [],
        3,
        1,
        40 * MIB,
    )(blended.reshape(micros, 2, 2, own_rows, OWN))


def tokens_to_heads_body(grads, out, send_sem, recv_sem, local_sem):
    links = Links(1, send_sem, recv_sem, local_sem)
    x, c = links.x, links.c
    corner = links.beside + 1 - 2 * c
    links.greet([links.core, links.beside, corner])

    def columns(to_x, to_c):
        return grads.at[:, :, pl.ds(pl.multiple_of((2 * to_x + to_c) * OWN, OWN), OWN)]

    target = out.at[:, x, c]
    own = links.local(columns(x, c), target)
    copies = [
        links.send(columns(1 - x, 1 - c), target, corner),
        links.send(columns(1 - x, c), target, links.beside),
        links.send(columns(x, 1 - c), target, links.core),
    ]
    arrived(copies)
    own.wait()
    links.finish_sends()


def tokens_to_heads(grads):
    micros, own_rows, _ = grads.shape
    return remote_call(
        tokens_to_heads_body,
        "tokens_to_heads",
        3,
        jax.ShapeDtypeStruct((micros, 2, 2, own_rows, OWN), grads.dtype),
        [ANY],
        ANY,
        [],
        3,
        1,
        40 * MIB,
    )(grads).reshape(micros, GROUP * own_rows, OWN)


def token_sums_body(partial, out, send_sem, recv_sem, local_sem, from_core, own, from_beside):
    links = Links(1, send_sem, recv_sem, local_sem)
    x, c = links.x, links.c
    links.greet([links.core, links.beside])
    far = links.send(partial.at[:, 1 - x, 1 - c], from_core.at[0], links.core)
    near = links.send(partial.at[:, x, 1 - c], from_core.at[1], links.core)
    loads = [
        links.local(partial.at[:, 1 - x, c], own.at[0]),
        links.local(partial.at[:, x, c], own.at[1]),
    ]
    micros = out.shape[0]
    loads[0].wait()
    arrived([far])
    passed = []
    for m in range(micros):
        own[0, m] = (
            own[0, m].astype(jnp.float32) + from_core[0, m].astype(jnp.float32)
        ).astype(jnp.bfloat16)
        passed.append(links.send(own.at[0, m], from_beside.at[m], links.beside))
    loads[1].wait()
    arrived([near])
    for m in range(micros):
        out[m] = own[1, m].astype(jnp.float32) + from_core[1, m].astype(jnp.float32)
    for m in range(micros):
        arrived([passed[m]])
        out[m] += from_beside[m].astype(jnp.float32)
    links.finish_sends()


def token_sums(partial):
    micros, rows, width = partial.shape
    own_rows = rows // GROUP
    held = pltpu.VMEM((2, micros, own_rows, width), partial.dtype)
    return remote_call(
        token_sums_body,
        "token_sums",
        4,
        jax.ShapeDtypeStruct((micros, own_rows, width), jnp.float32),
        [ANY],
        VMEM,
        [held, held, pltpu.VMEM((micros, own_rows, width), partial.dtype)],
        4,
        2,
        40 * MIB,
    )(partial.reshape(micros, 2, 2, own_rows, width))


def small_sums_body(planes, partial, out, send_sem, recv_sem, local_sem, from_core, from_beside):
    links = Links(planes, send_sem, recv_sem)
    links.greet(links.partners())
    z, y, x, c = links.z, links.y, links.x, links.c
    arrived([links.send(partial.at[:, 1 - c], from_core, links.core)])
    from_core[...] = from_core[...] + partial[:, c]
    arrived([links.send(from_core.at[1 - x], from_beside, links.beside)])
    out[z, y, x, c] = from_core[x] + from_beside[...]
    spread(links, out)
    links.finish_sends()


def small_sums(partial, planes):
    block = partial.shape[2:]
    return remote_call(
        functools.partial(small_sums_body, planes),
        "small_sums",
        5,
        jax.ShapeDtypeStruct((planes, 2, 2, 2, *block), jnp.float32),
        [VMEM],
        VMEM,
        [pltpu.VMEM((2, *block), jnp.float32), pltpu.VMEM(block, jnp.float32)],
        planes + 4,
        0,
        40 * MIB,
    )(partial)


SUMS_OVER_X = 384


def add_blocks(target, left, right, count):
    @pl.loop(0, count)
    def _(i):
        target(i)[...] = (
            left(i)[...].astype(jnp.float32) + right(i)[...].astype(jnp.float32)
        ).astype(jnp.bfloat16)


class Sums:
    def __init__(self, links, grads, outs, scratch):
        self.links = links
        self.pieces = []
        used = 0
        for grad, out in zip(grads, outs):
            own = scratch[used]
            used += 1
            for rows, start in cuts(grad.shape[-2:]):
                self.pieces.append((grad, out, rows, start, own, *scratch[used : used + 5]))
                used += 5
        self.state = [dict() for _ in self.pieces]
        self.loaded = {}

    def core(self, k):
        links = self.links
        grad, _, rows, start, _, first, *_ = self.pieces[k]
        columns = pl.ds(start, WIDTH)
        source = grad.at[:, :, :, 1 - links.c, rows, columns]
        self.state[k]["core"] = links.send(source, first, links.core)

    def load(self, k):
        links = self.links
        grad, _, rows, start, own, *_ = self.pieces[k]
        source = grad.at[:, :, :, links.c, rows, pl.ds(start, WIDTH)]
        self.state[k]["own"] = links.local(source, own)

    def S1(self, k):
        links = self.links
        x, y, planes = links.x, links.y, links.planes
        *_, own, first, over_x, over_y, _, _ = self.pieces[k]
        state = self.state[k]
        state["own"].wait()
        arrived([state["core"]])
        lead, rest = pl.ds(0, SUMS_OVER_X), pl.ds(SUMS_OVER_X, WIDTH - SUMS_OVER_X)

        def at(ref, columns, place):
            return lambda i: ref.at[(*place(i // 2, i % 2), slice(None), columns)]

        def add(columns, place):
            add_blocks(at(first, columns, place), at(own, columns, place), at(first, columns, place), planes * 2)

        add(lead, lambda z, other: (z, other, 1 - x))
        state["T"] = links.send(first.at[:, :, 1 - x, :, lead], over_x, links.beside)
        add(rest, lambda z, other: (z, 1 - y, other))
        state["F"] = links.send(first.at[:, 1 - y, :, :, rest], over_y, links.across)
        add(lead, lambda z, other: (z, other, x))
        add(rest, lambda z, other: (z, y, other))

    def S2T(self, k):
        links = self.links
        x, y = links.x, links.y
        *_, first, over_x, _, third, _ = self.pieces[k]
        lead = pl.ds(0, SUMS_OVER_X)
        arrived([self.state[k]["T"]])
        for here in (1 - y, y):
            add_blocks(
                lambda i, here=here: over_x.at[i, here],
                lambda i, here=here: first.at[i, here, x, :, lead],
                lambda i, here=here: over_x.at[i, here],
                links.planes,
            )
            if here is not y:
                self.state[k]["T"] = links.send(
                    over_x.at[:, here], third.at[:, :, lead], links.across
                )

    def S2F(self, k):
        links = self.links
        x, y = links.x, links.y
        *_, first, _, over_y, third, _ = self.pieces[k]
        rest = pl.ds(SUMS_OVER_X, WIDTH - SUMS_OVER_X)
        arrived([self.state[k]["F"]])
        for here in (1 - x, x):
            add_blocks(
                lambda i, here=here: over_y.at[i, here],
                lambda i, here=here: first.at[i, y, here, :, rest],
                lambda i, here=here: over_y.at[i, here],
                links.planes,
            )
            if here is not x:
                self.state[k]["F"] = links.send(
                    over_y.at[:, here], third.at[:, :, rest], links.beside
                )

    def S3(self, k):
        links = self.links
        x, y = links.x, links.y
        *_, over_x, over_y, third, fourth = self.pieces[k]
        arrived([self.state[k]["T"], self.state[k]["F"]])
        lead, rest = pl.ds(0, SUMS_OVER_X), pl.ds(SUMS_OVER_X, WIDTH - SUMS_OVER_X)
        for kept, here, columns in ((over_x, y, lead), (over_y, x, rest)):
            add_blocks(
                lambda i, columns=columns: third.at[i, :, columns],
                lambda i, kept=kept, here=here: kept.at[i, here],
                lambda i, columns=columns: third.at[i, :, columns],
                links.planes,
            )
        self.state[k]["planes"] = [
            links.send(third.at[links.plane(s)], fourth.at[s - 1], links.plane_device(s))
            for s in range(1, links.planes)
        ]

    def S4(self, k):
        links = self.links
        _, out, rows, start, *_, third, fourth = self.pieces[k]
        arrived(self.state[k]["planes"])
        result = third[links.z].astype(jnp.float32)
        for s in range(1, links.planes):
            result = result + fourth[s - 1].astype(jnp.float32)
        out[rows, pl.ds(start, WIDTH)] = result


def sums_order(count):
    order = []
    for k in range(count + 4):
        for task, behind in (("core", 0), ("S1", 1), ("load", 0), ("S2T", 2), ("S2F", 2), ("S3", 3), ("S4", 4)):
            if 0 <= k - behind < count:
                order.append((task, k - behind))
    return order


MIDDLE_ORDER = (
    ("mlp", 0), ("S1", 0), ("load", 1), ("mlp", 1), ("S2T", 0), ("S1", 1), ("load", 2), ("S2F", 0),
    ("S1", 2), ("load", 3), ("mlp", 2), ("S3", 0), ("S2T", 1), ("S2F", 1), ("S1", 3), ("mlp", 3),
    ("S3", 1), ("S2T", 2), ("S2F", 2), ("S2T", 3), ("S4", 0), ("own", 0), ("S2F", 3), ("own", 1),
    ("S3", 2), ("S4", 1), ("project", 0), ("S3", 3), ("S4", 2), ("S4", 3),
)
BACK_ORDER = (
    ("head", 0), ("S1", 0), ("load", 1), ("head", 1), ("S1", 1), ("load", 2), ("S2T", 0), ("head", 2),
    ("S2F", 0), ("S2T", 1), ("S1", 2), ("load", 3), ("head", 3), ("S3", 0), ("S2F", 1), ("S1", 3),
    ("load", 4), ("first", 0), ("S2T", 2), ("head", 4), ("t1", 0), ("S3", 1), ("S2T", 3), ("S4", 0),
    ("head", 5), ("S2F", 2), ("head", 6), ("S2F", 3), ("S4", 1), ("S1", 4), ("t2", 0), ("head", 7),
    ("S3", 2), ("attend", 0), ("S3", 3), ("S2F", 4), ("first", 1), ("S4", 2), ("bias", 0), ("t1", 1),
    ("S4", 3), ("S2T", 4), ("a1", 0), ("t2", 1), ("S3", 4), ("a2", 0), ("a3", 0), ("S4", 4),
)


class AttendSums:
    def __init__(self, links, grads, out, scratch):
        self.links, self.grads, self.out = links, grads, out
        self.own, self.over_y, self.over_planes, self.sum, self.held = scratch

    def start(self):
        links = self.links
        self.step = links.send(self.grads.at[:, 1 - links.y], self.over_y, links.across)
        self.loaded = links.local(self.grads.at[:, links.y], self.own)

    def planes(self):
        links, own, over_y = self.links, self.own, self.over_y
        self.loaded.wait()
        arrived([self.step])
        for i in range(2):

            def block(ref, i=i):
                return lambda k: ref.at[k // 2, i, k % 2]

            add_blocks(block(own), block(own), block(over_y), links.planes * 2)
        self.step = [
            links.send(own.at[links.plane(s)], self.over_planes.at[s - 1], links.plane_device(s))
            for s in range(1, links.planes)
        ]

    def owners(self):
        links = self.links
        x, c = links.x, links.c
        arrived(self.step)
        for i in range(2):
            for j in range(2):
                result = self.own[links.z, i, j].astype(jnp.float32)
                for s in range(1, links.planes):
                    result = result + self.over_planes[s - 1, i, j].astype(jnp.float32)
                self.sum[i, j] = result
        self.beside = links.send(self.sum.at[1 - x], self.held, links.beside)
        self.near = links.send(self.sum.at[x, 1 - c], self.out.at[x, c], links.core)
        self.out[x, c] = self.sum[x, c]

    def last(self):
        links = self.links
        x, c = links.x, links.c
        arrived([self.beside])
        self.out[1 - x, c] = self.held[c]
        self.far = links.send(self.held.at[1 - c], self.out.at[1 - x, c], links.core)

    def finish(self):
        arrived([self.near, self.far])


class TokenSums:
    def __init__(self, links, partial, out, scratch):
        self.links, self.partial, self.out = links, partial, out
        self.from_core, self.from_beside = scratch
        self.state = {}

    def start(self, m):
        links, partial = self.links, self.partial
        x, c = links.x, links.c
        self.state[m] = [
            links.send(partial.at[m, 1 - x, 1 - c], self.from_core.at[0, m], links.core),
            links.send(partial.at[m, x, 1 - c], self.from_core.at[1, m], links.core),
        ]

    def middle(self, m):
        links, partial = self.links, self.partial
        x, c = links.x, links.c
        arrived(self.state[m])
        away = partial.at[m, 1 - x, c]
        away[...] = (
            away[...].astype(jnp.float32) + self.from_core[0, m].astype(jnp.float32)
        ).astype(jnp.bfloat16)
        self.state[m] = [links.send(away, self.from_beside.at[m], links.beside)]

    def finish(self, m):
        links = self.links
        arrived(self.state[m])
        self.out[m] = (
            self.partial[m, links.x, links.c].astype(jnp.float32)
            + self.from_core[1, m].astype(jnp.float32)
            + self.from_beside[m].astype(jnp.float32)
        )


def sums_body(planes, kinds, *refs):
    attend, grads, refs = refs[0], refs[1 : 1 + kinds], refs[1 + kinds :]
    attend_out, outs, refs = refs[0], refs[1 : 1 + kinds], refs[1 + kinds :]
    links = Links(planes, *refs[:3])
    links.greet(links.partners())
    attend_sums = AttendSums(links, attend, attend_out, refs[3:8])
    attend_sums.start()
    attend_sums.planes()
    attend_sums.owners()
    attend_sums.last()
    sums = Sums(links, grads, outs, refs[8:])
    for task, k in sums_order(len(sums.pieces)):
        getattr(sums, task)(k)
    attend_sums.finish()
    links.finish_sends()


def middle_body(planes, *refs):
    grad_contract, expand, contract, project, act, slope, second, grad_branch, refs = *refs[:8], refs[8:]
    middle, attended, upstream, blended, modulation, shift, bias_contract, refs = *refs[:7], refs[7:]
    contract_out, output, middle_grad_out, rows_out, bias_out, hidden_out, refs = *refs[:6], refs[6:]
    grad_expand, grad_project, grad_heads, refs = *refs[:3], refs[3:]
    links = Links(planes, *refs[:3])
    refs = refs[3:]
    used = scratch_count([grad_contract.shape[-2:]])
    sum_scratch, refs = refs[:used], refs[used:]
    contract_held, expand_held, act_held, slope_held, second_held, second_t, refs = *refs[:6], refs[6:]
    branch_grad, grads, branch, grad_second, middle_held, attended_held, refs = *refs[:6], refs[6:]
    upstream_held, project_held, blended_held, attended_grad, project_grads, refs = *refs[:5], refs[5:]
    middle_grad, grad_blended = refs
    x, c = links.x, links.c
    corner = links.beside + 1 - 2 * c
    micros, own_rows, _ = second.shape
    parts = FF // WIDTH
    part_width = FF // parts
    contract_blocks = contract.shape[0] // parts

    def load(part):
        columns = pl.ds(part * part_width, part_width)
        slot = part % 2
        return [
            links.local(
                contract.at[pl.ds(part * contract_blocks, contract_blocks)], contract_held.at[slot]
            ),
            links.local(expand.at[:, :, :, :, :, columns], expand_held.at[slot]),
            links.local(act.at[:, :, columns], act_held.at[slot]),
            links.local(slope.at[:, :, columns], slope_held.at[slot]),
        ]

    loaded = links.local(second, second_held), links.local(grad_branch, branch_grad)
    loading = {0: load(0), 1: load(1)}
    links.greet([*links.partners(), corner])
    sums = Sums(links, (grad_contract,), (contract_out,), sum_scratch)
    for k in range(len(sums.pieces)):
        sums.core(k)
    sums.load(0)
    later = [
        links.local(middle, middle_held),
        links.local(attended, attended_held),
        links.local(upstream, upstream_held),
        links.local(project, project_held),
        links.local(blended, blended_held),
    ]
    for copy in loaded:
        copy.wait()
    for m in range(micros):
        second_t[:, m * own_rows : (m + 1) * own_rows] = second_held[m].T
    branch[...] = jnp.zeros_like(branch)
    grad_second[...] = jnp.zeros_like(grad_second)
    stored = []

    def mlp_unit(part):
        for copy in loading.pop(part):
            copy.wait()
        slot = part % 2
        if part >= 2:
            stored[part - 2].wait()
        contract_part(
            part * part_width,
            contract_held.at[slot],
            expand_held.at[slot],
            act_held.at[slot],
            slope_held.at[slot],
            second_t,
            branch_grad,
            grads.at[slot],
            branch,
            grad_second,
            hidden_out,
        )
        if part + 2 < parts:
            loading[part + 2] = load(part + 2)
        columns = pl.ds(part * part_width, part_width)
        stored.append(links.local(grads.at[slot], grad_expand.at[:, :, :, :, :, columns]))

    totals = [jnp.zeros((1, D), jnp.float32)] * 2

    def own_tokens(m):
        def vector(block):
            return modulation_row(modulation, m, block) + shift[block : block + 1, :]

        ahead = upstream_held[m].astype(jnp.float32)
        outward = branch[m] + bias_contract[...]
        output[m] = (middle_held[m] + vector(5) * outward).astype(jnp.bfloat16)
        rows_out[m, 5:6, :] = jnp.sum(ahead * outward, axis=0, keepdims=True)
        normed, scale = normalize(middle_held[m])
        values = grad_second[m]
        rows_out[m, 3:4, :] = jnp.sum(values, axis=0, keepdims=True)
        rows_out[m, 4:5, :] = jnp.sum(values * normed, axis=0, keepdims=True)
        back = ahead + norm_back(values, normed, scale, vector(4))
        middle_grad[m] = back
        rows_out[m, 2:3, :] = jnp.sum(back * attended_held[m], axis=0, keepdims=True)
        lowered = (vector(2) * back).astype(jnp.bfloat16)
        attended_grad[m] = lowered
        totals[0] += jnp.sum(lowered.astype(jnp.float32), axis=0, keepdims=True)
        totals[1] += jnp.sum(branch_grad[m].astype(jnp.float32), axis=0, keepdims=True)
        product = lax.dot_general(
            lowered,
            project_held[...].reshape(D, D),
            (((1,), (1,)), ((), ())),
            preferred_element_type=jnp.float32,
        )
        grad_blended[m] = product.astype(jnp.bfloat16)
        here = pl.ds(pl.multiple_of((2 * x + c) * own_rows, own_rows), own_rows)

        def columns_of(to_x, to_c):
            start = pl.multiple_of((2 * to_x + to_c) * OWN, OWN)
            return grad_blended.at[m, :, pl.ds(start, OWN)]

        target = grad_heads.at[m, here]
        exchanged.append(links.send(columns_of(1 - x, 1 - c), target, corner))
        exchanged.append(links.send(columns_of(1 - x, c), target, links.beside))
        exchanged.append(links.send(columns_of(x, 1 - c), target, links.core))
        stored.append(links.local(columns_of(x, c), target))

    exchanged = []

    def project_unit():
        total = None
        for m in range(micros):
            product = lax.dot_general(
                blended_held[m],
                attended_grad[m],
                (((0,), (0,)), ((), ())),
                preferred_element_type=jnp.float32,
            )
            total = product if total is None else total + product
        project_grads[...] = total.astype(jnp.bfloat16).reshape(project_grads.shape)
        stored.append(links.local(project_grads, grad_project))
        stored.append(links.local(middle_grad, middle_grad_out))

    for task, k in MIDDLE_ORDER:
        if task == "mlp":
            mlp_unit(k)
        elif task == "own":
            if k == 0:
                for copy in later:
                    copy.wait()
            own_tokens(k)
        elif task == "project":
            project_unit()
        else:
            getattr(sums, task)(k)
    bias_out[0:1, :] = totals[0]
    bias_out[1:2, :] = totals[1]
    arrived(exchanged)
    for copy in stored[parts - 2 :]:
        copy.wait()
    links.finish_sends()


def contract_part(
    start,
    contract,
    expand,
    act,
    slope,
    second_t,
    grad_branch,
    grads,
    branch,
    grad_second,
    hidden_sums,
):
    micros = grad_branch.shape[0]
    blocks = CHUNK // contract.shape[1]

    @pl.loop(0, act.shape[-1] // CHUNK)
    def _(chunk):
        inside = pl.ds(pl.multiple_of(chunk * CHUNK, CHUNK), CHUNK)
        columns = pl.ds(pl.multiple_of(start + chunk * CHUNK, CHUNK), CHUNK)
        outward = contract[pl.ds(chunk * blocks, blocks)].reshape(CHUNK, D)
        inward = expand[:, :, :, :, :, inside].reshape(D, CHUNK)
        lows = []
        for m in range(micros):
            branch[m] += jnp.dot(act[m, :, inside], outward, preferred_element_type=jnp.float32)
            grad_act = lax.dot_general(
                grad_branch[m], outward, (((1,), (1,)), ((), ())), preferred_element_type=jnp.float32
            )
            lows.append((grad_act * slope[m, :, inside].astype(jnp.float32)).astype(jnp.bfloat16))
            grad_second[m] += lax.dot_general(
                lows[m], inward, (((1,), (1,)), ((), ())), preferred_element_type=jnp.float32
            )
        grad_hidden = jnp.concatenate(lows, axis=0)
        product = jnp.dot(second_t[...], grad_hidden, preferred_element_type=jnp.float32)
        grads[:, :, :, :, :, inside] = product.astype(jnp.bfloat16).reshape(
            *grads.shape[:-1], CHUNK
        )
        hidden_sums[:, columns] = jnp.sum(
            grad_hidden.astype(jnp.float32), axis=0, keepdims=True
        )


def back_body(planes, *refs):
    grad_expand, grad_project, grad_heads, qkv, heads, logs, first, attend, refs = *refs[:8], refs[8:]
    attend_out, expand_out, project_out, first_out, bias_out, refs = *refs[:5], refs[5:]
    links = Links(planes, *refs[:3])
    attend_held_scratch, refs = refs[3:8], refs[8:]
    used = scratch_count([grad_expand.shape[-2:], grad_project.shape[-2:]])
    sum_scratch, refs = refs[:used], refs[used:]
    grads_held, qkv_held, heads_held, first_held, attend_held, grad_qkv, refs = *refs[:6], refs[6:]
    key_sum, value_sum, attend_grads, partial, *token_scratch = refs
    micros, latent_rows, _ = qkv.shape
    loads = [
        links.local(grad_heads, grads_held),
        links.local(qkv, qkv_held),
        links.local(heads, heads_held),
        links.local(attend, attend_held),
        links.local(first, first_held),
    ]
    links.greet(links.partners())
    sums = Sums(links, (grad_expand, grad_project), (expand_out, project_out), sum_scratch)
    for k in range(len(sums.pieces)):
        sums.core(k)
    sums.load(0)
    attend_sums = AttendSums(links, attend_grads, attend_out, attend_held_scratch)
    token_sum = TokenSums(links, partial, first_out, token_scratch)

    def head_unit(m, head):
        if m == 0 and head == 0:
            for copy in loads:
                copy.wait()
        attention_back_unit(
            qkv_held.at[m],
            heads_held.at[m],
            grads_held.at[m],
            logs.at[m],
            grad_qkv.at[m],
            key_sum,
            value_sum,
            head,
        )

    def first_unit(m):
        first_product(m, grad_qkv, attend_held, partial)
        token_sum.start(m)

    def attend_unit():
        attend_product(first_held, grad_qkv, attend_grads, planes)
        attend_sums.start()

    def bias_unit():
        total = jnp.zeros((1, grad_qkv.shape[-1]), jnp.float32)
        for m in range(micros):
            total = total + jnp.sum(grad_qkv[m].astype(jnp.float32), axis=0, keepdims=True)
        bias_out[...] = total

    heads_each = OWN // HEAD
    for task, k in BACK_ORDER:
        if task == "head":
            head_unit(k // heads_each, k % heads_each)
        elif task == "first":
            first_unit(k)
        elif task == "attend":
            attend_unit()
        elif task == "bias":
            bias_unit()
        elif task == "t1":
            token_sum.middle(k)
        elif task == "t2":
            token_sum.finish(k)
        elif task == "a1":
            attend_sums.planes()
        elif task == "a2":
            attend_sums.owners()
        elif task == "a3":
            attend_sums.last()
        else:
            getattr(sums, task)(k)
    attend_sums.finish()
    links.finish_sends()


def attend_product(first, grad_qkv, out, planes):
    width = D // planes

    @pl.loop(0, planes)
    def _(plane):
        columns = pl.ds(pl.multiple_of(plane * width, width), width)
        total = None
        for m in range(first.shape[0]):
            product = lax.dot_general(
                first[m, :, columns],
                grad_qkv[m],
                (((0,), (0,)), ((), ())),
                preferred_element_type=jnp.float32,
            )
            total = product if total is None else total + product
        out[plane] = total.astype(jnp.bfloat16).reshape(out.shape[1:])


def first_product(m, grad_qkv, attend, partial):
    rows = partial.shape[3]

    @pl.loop(0, GROUP)
    def _(block):
        here = pl.ds(pl.multiple_of(block * rows, rows), rows)
        product = lax.dot_general(
            grad_qkv[m, here, :],
            attend[...].reshape(D, 3 * OWN),
            (((1,), (1,)), ((), ())),
            preferred_element_type=jnp.float32,
        )
        partial[m, block // 2, block % 2] = product.astype(jnp.bfloat16)


def attend_scratch(attend, planes):
    rows, width = attend.shape[-2:]
    return [
        pltpu.VMEM((planes, 2, 2, rows, width), jnp.bfloat16),
        pltpu.VMEM((planes, 2, 2, rows, width), jnp.bfloat16),
        pltpu.VMEM((planes - 1, 2, 2, rows, width), jnp.bfloat16),
        pltpu.VMEM((2, 2, rows, width), jnp.float32),
        pltpu.VMEM((2, rows, width), jnp.float32),
    ]


def sum_scratch(shapes, planes):
    held = []
    for shape in shapes:
        pieces = cuts(shape)
        rows = shape[0] if shape[1] > WIDTH else shape[0] // len(pieces)
        held.append(low_held(planes, 2, 2, rows, WIDTH))
        for _ in pieces:
            held += [
                low_held(planes, 2, 2, rows, WIDTH),
                low_held(planes, 2, rows, SUMS_OVER_X),
                low_held(planes, 2, rows, WIDTH - SUMS_OVER_X),
                low_held(planes, rows, WIDTH),
                low_held(planes - 1, rows, WIDTH),
            ]
    return held


def count_pieces(shapes):
    return sum(len(cuts(shape)) for shape in shapes)


def scratch_count(shapes):
    return len(shapes) + 5 * count_pieces(shapes)


def full_shape(*shape):
    return jax.ShapeDtypeStruct(shape, jnp.float32)


def low_shape(*shape):
    return jax.ShapeDtypeStruct(shape, jnp.bfloat16)


def full_held(*shape):
    return pltpu.VMEM(shape, jnp.float32)


def low_held(*shape):
    return pltpu.VMEM(shape, jnp.bfloat16)


def sum_sems(shapes, planes):
    return count_pieces(shapes) * (4 + planes)


def weight_sums(attend, weights, planes):
    shapes = [grad.shape[-2:] for grad in weights]
    return remote_call(
        functools.partial(sums_body, planes, len(weights)),
        "weight_sums",
        6,
        (full_shape(2, 2, *attend.shape[-2:]), *(full_shape(*shape) for shape in shapes)),
        [ANY] * (1 + len(weights)),
        (VMEM,) * (1 + len(weights)),
        [*attend_scratch(attend, planes), *sum_scratch(shapes, planes)],
        8 + planes + sum_sems(shapes, planes),
        2 + count_pieces(shapes),
        60 * MIB,
    )(attend, *weights)


def middle_part(grad_contract, weights, held, vectors, planes):
    expand, contract, project = weights
    second = held[2]
    micros, own_rows, _ = second.shape
    own = second.shape
    shape = grad_contract.shape[-2:]
    width = WIDTH
    blocks = width // shape[0]
    return remote_call(
        functools.partial(middle_body, planes),
        "middle",
        6,
        (
            full_shape(*shape),
            low_shape(*own),
            full_shape(*own),
            full_shape(micros, 8, D),
            full_shape(8, D),
            full_shape(1, FF),
            low_shape(*expand.shape),
            low_shape(*project.shape),
            low_shape(micros, own_rows * GROUP, OWN),
        ),
        [ANY] * 12 + [VMEM] * 3,
        (VMEM, VMEM, ANY) + (VMEM,) * 3 + (ANY,) * 3,
        [
            *sum_scratch([shape], planes),
            low_held(2, blocks, *shape),
            low_held(2, *expand.shape[:-1], width),
            low_held(2, micros, own_rows, width),
            low_held(2, micros, own_rows, width),
            low_held(*own),
            low_held(D, micros * own_rows),
            low_held(*own),
            low_held(2, *expand.shape[:-1], width),
            full_held(*own),
            full_held(*own),
            full_held(*own),
            full_held(*own),
            low_held(*own),
            low_held(*project.shape),
            low_held(*own),
            low_held(*own),
            low_held(*project.shape),
            full_held(*own),
            low_held(*own),
        ],
        8 + sum_sems([shape], planes),
        48,
        63 * MIB,
    )(
        grad_contract,
        expand,
        contract.reshape(FF // shape[0], *shape),
        project,
        *held,
        *vectors,
    )


def back_part(grad_expand, grad_project, grad_heads, qkv, heads, logs, first, attend, planes):
    shapes = [grad_expand.shape[-2:], grad_project.shape[-2:]]
    micros, latent_rows, width = qkv.shape
    own_rows = latent_rows // GROUP
    return remote_call(
        functools.partial(back_body, planes),
        "back",
        7,
        (
            full_shape(2, 2, *attend.shape[-2:]),
            *(full_shape(*shape) for shape in shapes),
            full_shape(micros, own_rows, D),
            full_shape(1, width),
        ),
        [ANY] * 5 + [VMEM] + [ANY] * 2,
        (VMEM,) * 5,
        [
            *attend_scratch(attend, planes),
            *sum_scratch(shapes, planes),
            low_held(*grad_heads.shape),
            low_held(*qkv.shape),
            low_held(*heads.shape),
            low_held(*first.shape),
            low_held(*attend.shape),
            low_held(*qkv.shape),
            full_held(latent_rows, HEAD),
            full_held(latent_rows, HEAD),
            low_held(*attend.shape),
            low_held(micros, 2, 2, own_rows, D),
            low_held(2, micros, own_rows, D),
            low_held(micros, own_rows, D),
        ],
        20 + planes + sum_sems(shapes, planes),
        8 + count_pieces(shapes),
        63 * MIB,
    )(grad_expand, grad_project, grad_heads, qkv, heads, logs, first, attend)


def normalize(values):
    center = values - jnp.mean(values, axis=-1, keepdims=True)
    spread_of = jnp.mean(center * center, axis=-1, keepdims=True)
    scale = lax.rsqrt(spread_of + epsilon)
    return center * scale, scale


def norm_back(grads, normed, scale, factors):
    inner = grads * (1.0 + factors)
    return scale * (
        inner
        - jnp.mean(inner, axis=-1, keepdims=True)
        - normed * jnp.mean(inner * normed, axis=-1, keepdims=True)
    )


def einsum(spec, left, right):
    return jnp.einsum(spec, left, right, preferred_element_type=jnp.float32)


def per_device(tokens, condition, attend, project, expand, contract, modulate, biases, cotangent):
    devices = lax.axis_size("fsdp")
    planes = devices // 8
    latents = devices // GROUP
    me = lax.axis_index("fsdp")
    quarter, latent = me % GROUP, me // GROUP
    micros, own_rows, _ = tokens.shape
    latent_rows = own_rows * GROUP
    rows = D // devices
    grid = (planes, 2, 2, 2)

    held = jnp.concatenate([condition.reshape(-1), biases]).astype(jnp.float32)
    held = jnp.pad(held, (0, -held.size % (8 * LANES)))
    small = small_gather(held.reshape(-1, LANES), planes, 0).reshape(devices, -1)
    conditions = small[:, : condition.size].reshape(latents, GROUP, micros, -1)
    conditions = conditions.transpose(2, 0, 1, 3).reshape(micros * latents, D)
    cond_act = silu(conditions).astype(jnp.bfloat16)
    bias_all = small[:, condition.size : condition.size + biases.size].reshape(-1)
    bias_query = bias_all[0:D]
    bias_value = bias_all[D : 2 * D]
    bias_project = bias_all[2 * D : 3 * D]
    bias_expand = bias_all[3 * D : 3 * D + FF]
    bias_contract = bias_all[3 * D + FF : 4 * D + FF]
    bias_modulate = bias_all[4 * D + FF :]

    modulate_rows = modulate.reshape(rows, 6 * D)
    cond_own = lax.dynamic_slice_in_dim(cond_act, me * rows, rows, axis=1)
    partial = jnp.dot(cond_own, modulate_rows, preferred_element_type=jnp.float32)
    partial = partial.reshape(micros, latents, GROUP, -1).transpose(1, 2, 0, 3)
    partial = partial.reshape(planes, 2, 2, 2, -1, LANES)

    attend_shard = attend.reshape(rows, 3, 2, 2, OWN).transpose(2, 3, 0, 1, 4)
    bias_row = jnp.concatenate(
        [
            lax.dynamic_slice_in_dim(bias_query, quarter * OWN, OWN),
            jnp.zeros((OWN,), jnp.float32),
            lax.dynamic_slice_in_dim(bias_value, quarter * OWN, OWN),
        ]
    )
    shards = (
        tokens,
        attend_shard.reshape(2, 2, rows, 3 * OWN),
        project.reshape(rows, D),
        expand.reshape(rows, FF),
        contract.reshape(FF // devices, D),
        partial,
    )
    shift = bias_modulate.reshape(6, D)
    fused = rows % 16 == 0 and own_rows % QUERY_ROWS == 0 and planes * 2 <= 8
    if fused:
        vectors = (shift, bias_row[None], bias_project[None], bias_expand[None])
        attend_all, project_all, expand_all, contract_all, modulation_all, *rest = front(
            *shards, vectors, cotangent, planes
        )
    else:
        attend_all, project_all, expand_all, contract_all, modulation_all, *rest = gather_all(
            *shards, planes
        )
    modulation = modulation_all.reshape(GROUP, micros, -1).transpose(1, 0, 2)
    modulation = modulation.reshape(micros, 6 * D) + bias_modulate
    offsets_one, factors_one, gates_one, offsets_two, factors_two, gates_two = (
        modulation[:, None, part * D : (part + 1) * D] for part in range(6)
    )
    inputs = tokens.astype(jnp.float32)
    if fused:
        first, projected, heads, logs, blended, middle, attended, second, act, slope, low, grads = rest
        contract_sum, output, grad_middle, row_sums, bias_sums, hidden_sums, *onward = middle_part(
            grads.reshape(*grid, FF // devices, D),
            (expand_all, contract_all, project_all),
            (act, slope, second, low, middle, attended, cotangent, blended),
            (modulation_all, shift, bias_contract[None]),
            planes,
        )
        attend_sum, expand_sum, project_sum, grad_first, heads_sum = back_part(
            *onward, projected, heads, logs, first, attend_all, planes
        )
        heads_sum, attended_sum, branch_sum = heads_sum[0], bias_sums[0], bias_sums[1]
        hidden_sum = hidden_sums[0]
        later_sums = row_sums[:, 2:6].reshape(micros, 4 * D)
    else:
        attend_own = attend_all.reshape(D, 3 * OWN)
        project_full = project_all.reshape(D, D)
        expand_full = expand_all.reshape(D, FF)
        contract_full = contract_all.reshape(FF, D)
        tokens_latent = rest[0].reshape(micros, latent_rows, D)
        normed_latent, _ = normalize(tokens_latent.astype(jnp.float32))
        first = (normed_latent * (1.0 + factors_one) + offsets_one).astype(jnp.bfloat16)
        projected = (einsum("mrd,de->mre", first, attend_own) + bias_row).astype(jnp.bfloat16)
        blended_heads, logs = attention(projected)
        blended = heads_to_tokens(blended_heads)

        attended = einsum("mrd,de->mre", blended, project_full) + bias_project
        middle = inputs + gates_one * attended
        normed_two, scale_two = normalize(middle)
        second = (normed_two * (1.0 + factors_two) + offsets_two).astype(jnp.bfloat16)
        hidden = einsum("mrd,de->mre", second, expand_full) + bias_expand
        activated, gelu_pull = jax.vjp(lambda v: jax.nn.gelu(v, approximate=True), hidden)
        act_low = activated.astype(jnp.bfloat16)
        branch = einsum("mrd,de->mre", act_low, contract_full) + bias_contract
        output = (middle + gates_two * branch).astype(jnp.bfloat16)

        upstream = cotangent.astype(jnp.float32)
        grad_branch = (gates_two * upstream).astype(jnp.bfloat16)
        grad_contract = einsum("mrd,mre->de", act_low, grad_branch)
        grad_act = einsum("mre,de->mrd", grad_branch, contract_full)
        grad_hidden = gelu_pull(grad_act)[0].astype(jnp.bfloat16)
        grad_expand = einsum("mrd,mre->de", second, grad_hidden)
        grad_second = einsum("mre,de->mrd", grad_hidden, expand_full)
        grad_middle = upstream + norm_back(grad_second, normed_two, scale_two, factors_two)
        grad_attended = (gates_one * grad_middle).astype(jnp.bfloat16)
        grad_project = einsum("mrd,mre->de", blended, grad_attended)
        grad_blended = einsum("mre,de->mrd", grad_attended, project_full).astype(jnp.bfloat16)
        grad_heads = tokens_to_heads(grad_blended)
        grad_projected = attention_back(projected, blended_heads, grad_heads, logs)
        grad_attend = einsum("mrd,mre->de", first, grad_projected)
        grad_first = token_sums(
            einsum("mre,de->mrd", grad_projected, attend_own).astype(jnp.bfloat16)
        )
        weights = (
            grad_contract.astype(jnp.bfloat16).reshape(*grid, FF // devices, D),
            grad_expand.astype(jnp.bfloat16).reshape(*grid, rows, FF),
            grad_project.astype(jnp.bfloat16).reshape(*grid, rows, D),
        )
        attend_sum, contract_sum, expand_sum, project_sum = weight_sums(
            grad_attend.astype(jnp.bfloat16).reshape(*grid, rows, 3 * OWN), weights, planes
        )

        def token_sum(values):
            return jnp.sum(values, axis=(0, 1), dtype=jnp.float32)

        heads_sum, attended_sum = token_sum(grad_projected), token_sum(grad_attended)
        hidden_sum, branch_sum = token_sum(grad_hidden), token_sum(grad_branch)
        later_sums = jnp.concatenate(
            [
                jnp.sum(grad_middle * attended, axis=1),
                jnp.sum(grad_second, axis=1),
                jnp.sum(grad_second * normed_two, axis=1),
                jnp.sum(upstream * branch, axis=1),
            ],
            axis=1,
        )
    normed_one, scale_one = normalize(inputs)
    grad_tokens = grad_middle + norm_back(grad_first, normed_one, scale_one, factors_one)

    grad_modulation = jnp.concatenate(
        [jnp.sum(grad_first, axis=1), jnp.sum(grad_first * normed_one, axis=1), later_sums], axis=1
    )
    bias_terms = jnp.concatenate(
        [
            lax.dynamic_update_slice(
                jnp.zeros((D,), jnp.float32), heads_sum[:OWN], (quarter * OWN,)
            ),
            lax.dynamic_update_slice(
                jnp.zeros((D,), jnp.float32), heads_sum[2 * OWN :], (quarter * OWN,)
            ),
            attended_sum,
            hidden_sum,
            branch_sum,
        ]
    )
    to_sum = jnp.concatenate(
        [
            grad_modulation.reshape(micros, GROUP, -1).transpose(1, 0, 2).reshape(GROUP, -1),
            bias_terms.reshape(GROUP, -1),
        ],
        axis=1,
    )
    sums = small_sums(to_sum.reshape(2, 2, -1, LANES), planes).reshape(latents, GROUP, -1)
    split = micros * 6 * D // GROUP
    grad_modulations = sums[:, :, :split].reshape(latents, GROUP, micros, -1)
    grad_modulations = grad_modulations.transpose(2, 0, 1, 3).reshape(micros * latents, 6 * D)
    bias_sums = jnp.concatenate(
        [jnp.sum(sums[:, :, split:], axis=0).reshape(-1), jnp.sum(grad_modulations, axis=0)]
    )
    grad_biases = lax.dynamic_slice_in_dim(bias_sums, me * biases.size, biases.size)
    grad_modulate = lax.dot_general(
        cond_own.astype(jnp.float32),
        grad_modulations,
        (((0,), (0,)), ((), ())),
        precision=highest,
    )
    grad_cond_cols = lax.dot_general(
        grad_modulations,
        modulate_rows.astype(jnp.float32),
        (((1,), (1,)), ((), ())),
        precision=highest,
    )
    cols = grad_cond_cols.reshape(-1)
    cols = jnp.pad(cols, (0, -cols.size % (8 * LANES)))
    cols_all = small_gather(cols.reshape(-1, LANES), planes, 8).reshape(devices, -1)
    cols_all = cols_all[:, : micros * latents * rows].reshape(devices, micros, latents, rows)
    cols_own = lax.dynamic_index_in_dim(cols_all, latent, axis=2, keepdims=False)
    width = D // GROUP
    cols_own = lax.dynamic_slice_in_dim(
        cols_own, quarter * (devices // GROUP), devices // GROUP, axis=0
    )
    grad_silu = cols_own.transpose(1, 0, 2).reshape(micros, width)
    values = condition.astype(jnp.float32)
    gate = 1.0 / (1.0 + jnp.exp(-values))
    grad_condition = gate * (1.0 + values * (1.0 - gate)) * grad_silu

    attend_sum = attend_sum.reshape(2, 2, rows, 3, OWN).transpose(2, 3, 0, 1, 4)
    return (
        output,
        grad_tokens,
        grad_condition,
        attend_sum.reshape(-1),
        project_sum.reshape(-1),
        expand_sum.reshape(-1),
        contract_sum.reshape(-1),
        grad_modulate.reshape(-1),
        grad_biases,
    )


def solution(mesh):
    in_specs = (
        P(None, "fsdp", None),
        P(None, "fsdp"),
        P("fsdp"),
        P("fsdp"),
        P("fsdp"),
        P("fsdp"),
        P("fsdp"),
        P("fsdp"),
        P(None, "fsdp", None),
    )
    out_specs = (
        P(None, "fsdp", None),
        P(None, "fsdp", None),
        P(None, "fsdp"),
        P("fsdp"),
        P("fsdp"),
        P("fsdp"),
        P("fsdp"),
        P("fsdp"),
        P("fsdp"),
    )
    return jax.shard_map(
        per_device, mesh=mesh, in_specs=in_specs, out_specs=out_specs, check_vma=False
    )
```

time: 463 us -> 383 us (0.83)
  matrix products: 73.8 us -> 2.75 us
  Pallas kernels: 357 us -> 343 us
    dot_general x9 -> x0, matrix products: 71.8 us -> none  [einsum(): return jnp.einsum(spec, left, right, preferred_element_type=jnp.float32)]
    pallas_call x2 -> x3, Pallas kernels: 304 us -> 294 us  [the longest x1 131 us: front(): remote_call(functools.partial(front_body, planes), 'front', 1, (*gather_o...]
    pallas_call x1, Pallas kernels: 25 us -> 20.1 us  [small_sums(): remote_call(functools.partial(small_sums_body, planes), 'small_sums', 5,...]
where the time goes in v3:
time: 383 us; the launch traced here: 380 us
  Pallas kernels  343 us (90%)
  local copies, waits for them, and re-layouts  18.9 us (5%)
  other arithmetic  13.5 us (4%)
    pallas_call x1, Pallas kernels, front(): remote_call(functools.partial(front_body, planes), 'front', 1, (*gather_o...  131 us
    pallas_call x1, Pallas kernels, back_part(): remote_call(functools.partial(back_body, planes), 'back', 7, (full_shape(...  100 us
    pallas_call x1, Pallas kernels, middle_part(): remote_call(functools.partial(middle_body, planes), 'middle', 6, (full_sh...  62.9 us
    pallas_call x2, Pallas kernels, small_gather(): remote_call(functools.partial(small_gather_body, planes), 'small_gather',...  28.8 us
    pallas_call x1, Pallas kernels, small_sums(): remote_call(functools.partial(small_sums_body, planes), 'small_sums', 5,...  20.1 us

profile of v3, /device:TPU:0, one launch (start us, length us, event | category | flops | bytes accessed | tf_op | source)
XLA Modules:
  0.0 379.9 jit_solution(1342110331109795216)
XLA Ops:
  2.0 14.9 %small_gather.2 = f32[4,2,2,2,8,128]{5,4,3,2,1,0:T(8,128)S(1)} custom-call(f32[8,128]{1,0:T(8,128)S(1)} %fusion.26.own_ref), custom_call_target="tpu_custom_call" | custom-call | tf_op jit(solution)/shard_map/small_gather/pallas_call | solution.py:142
  18.5 1.2 reshape.175
  20.4 1.1 reshape.176.refs_5_
  23.0 0.9 reshape.165.refs_1_
  23.9 0.8 reshape.167.refs_3_
  24.7 0.8 reshape.168.refs_4_
  26.2 131.3 %front.1 = (bf16[4,2,2,2,32,768]{5,4,3,2,1,0:T(8,128)(2,1)}, bf16[4,2,2,2,32,1024]{5,4,3,2,1,0:T(8,128)(2,1)}, bf16[4,2,2,2,32,4096]{5,4,3,2,1,0:T(8,128)(2,1)},...) custom-call(bf16[2,256,1024]{2,1,0:T(8,128)(2,1)} %refs_0_.1, ...), custom_call_target="tpu_custom_call" | custom-call | tf_op jit(solution)/shard_map/front/pallas_call | solution.py:663
  157.5 62.9 %middle.1 = (f32[128,1024]{1,0:T(8,128)}, bf16[2,256,1024]{2,1,0:T(8,128)(2,1)}, f32[2,256,1024]{2,1,0:T(8,128)}, f32[2,8,1024]{2,1,0:T(8,128)}, f32[8,1024]{1,0...) custom-call(bf16[4,2,2,2,128,1024]{5,4,3,2,1,0:T(8,128)(2,1)} %bitca, ...), custom_call_target="tpu_custom_call" | custom-call | tf_op jit(solution)/shard_map/middle/pallas_call | solution.py:1624
  220.4 100.2 %back.1 = (f32[2,2,32,768]{3,2,1,0:T(8,128)}, f32[32,4096]{1,0:T(8,128)}, f32[32,1024]{1,0:T(8,128)}, f32[2,256,1024]{2,1,0:T(8,128)}, f32[1,768]{1,0:T(1,128)}) custom-call(bf16[4,2,2,2,32,4096]{5,4,3,2,1,0:T(8,128)(2,1)} %get-tuple-element.54.refs_0_, bf16[4,2,2,2,32,1024]{5,4,3,2,1,0:T(8,128)(2,1)} %get-tuple-element.55.refs_1_, ...), custom_call_target="tpu_custom_call" | custom-call | tf_op jit(solution)/shard_map/back/pallas_call | solution.py:1680
  320.7 1.5 convert_reduce_fusion
  322.2 1.7 fusion.10
  323.9 3.1 fusion.9
  327.7 0.8 fusion.28
  328.6 20.1 %small_sums.1 = f32[4,2,2,2,40,128]{5,4,3,2,1,0:T(8,128)S(1)} custom-call(f32[2,2,40,128]{3,2,1,0:T(8,128)S(1)} %bitcast.104), custom_call_target="tpu_custom_call" | custom-call | tf_op jit(solution)/shard_map/small_sums/pallas_call | solution.py:971
  350.6 1.4 convolution_bitcast_fusion.1
  352.0 1.0 copy.54
  353.0 1.0 fusion.30
  354.8 13.9 %small_gather.3 = f32[4,2,2,2,8,128]{5,4,3,2,1,0:T(8,128)S(1)} custom-call(f32[8,128]{1,0:T(8,128)S(1)} %pad_bitcast_fusion.own_ref), custom_call_target="tpu_custom_call" | custom-call | tf_op jit(solution)/shard_map/small_gather/pallas_call | solution.py:142
  369.0 1.3 fusion.23
  371.0 3.7 fusion.8
  375.2 0.9 copy.50
  376.2 0.9 copy.52
  377.8 0.9 copy.53
  378.7 1.0 copy.78
  (97 shorter events, 11.1 us)
Async XLA Ops:
  17.0 5.8 %copy-start.8 = (bf16[98304]{0:T(1024)(128)(2,1)S(1)}, bf16[98304]{0:T(1024)(128)(2,1)}, u32[]{:S(2)}) copy-start(bf16[98304]{0:T(1024)(128)(2,1)} %param.11) | copy-start | bytes 589828
  18.5 1.2 copy-start.11
  19.7 4.2 %copy-start.6 = (bf16[131072]{0:T(1024)(128)(2,1)S(1)}, bf16[131072]{0:T(1024)(128)(2,1)}, u32[]{:S(2)}) copy-start(bf16[131072]{0:T(1024)(128)(2,1)} %param.13) | copy-start | bytes 786436
  19.8 5.0 %copy-start.7 = (bf16[131072]{0:T(1024)(128)(2,1)S(1)}, bf16[131072]{0:T(1024)(128)(2,1)}, u32[]{:S(2)}) copy-start(bf16[131072]{0:T(1024)(128)(2,1)} %param.14) | copy-start | bytes 786436
  20.0 5.5 %copy-start.12 = (bf16[32768]{0:T(1024)(128)(2,1)S(1)}, bf16[32768]{0:T(1024)(128)(2,1)}, u32[]{:S(2)}) copy-start(bf16[32768]{0:T(1024)(128)(2,1)} %param.12) | copy-start | bytes 196612
  220.4 100.2 %copy-start.9 = (f32[2,2,24,128]{3,2,1,0:T(8,128)S(1)}, f32[2,2,24,128]{3,2,1,0:T(8,128)}, u32[]{:S(2)}) copy-start(f32[2,2,24,128]{3,2,1,0:T(8,128)} %get-tuple-element.51.refs_12_) | copy-start | bytes 147460
  320.6 3.3 copy-start
  322.2 4.8 %copy-start.13 = (f32[2,8,1024]{2,1,0:T(8,128)S(1)}, f32[2,8,1024]{2,1,0:T(8,128)}, u32[]{:S(2)}) copy-start(f32[2,8,1024]{2,1,0:T(8,128)} %get-tuple-element.63) | copy-start | bytes 196612
  322.2 4.9 %copy-start.15 = (f32[1,768]{1,0:T(1,128)S(1)}, f32[1,768]{1,0:T(1,128)}, u32[]{:S(2)}) copy-start(f32[1,768]{1,0:T(1,128)} %get-tuple-element.64) | copy-start | bytes 9220
  322.2 6.3 %copy-start.14 = (f32[1,4096]{1,0:T(1,128)S(1)}, f32[1,4096]{1,0:T(1,128)}, u32[]{:S(2)}) copy-start(f32[1,4096]{1,0:T(1,128)} %get-tuple-element.66) | copy-start | bytes 49156
  350.5 20.5 %copy-start.1 = (f32[2,256,1024]{2,1,0:T(8,128)S(1)}, f32[2,256,1024]{2,1,0:T(8,128)}, u32[]{:S(2)}) copy-start(f32[2,256,1024]{2,1,0:T(8,128)} %get-tuple-element.62) | copy-start | bytes 6291460
  371.0 3.7 copy-start.5
  374.7 1.5 copy-start.4
  374.7 2.4 copy-start.10
  374.7 3.1 copy-start.3
  374.9 3.7 copy-start.2
